TPU v7x, 32 devices: a whole 2x2x4 slice. The times are simulated.
32 devices in a mesh: row: 8 (over z, y), col: 4 (over x, core).
Axes of the slice: x: 2, y: 2, z: 4, core: 2. Of those that a mesh axis runs over, the one named last changes fastest.
Arguments:
- embeddings: bfloat16 [512, 1024], P(('row', 'col')), may hold values from -20 to 20
- group_ids: int32 [512], P(('row', 'col')), may hold values from 0 to 127, as said below
Outputs:
- loss: float32 [], replicated
- grad: bfloat16 [512, 1024], P(('row', 'col'))
Inputs may be any that keep to these rules, and one draw needn't show every extreme that they name: `group_ids`: every group id is held by exactly 4 rows, spread over the batch.
All inputs are finite; a program needn't handle non-finite values.
Results may differ from a plain program's by a relative error of at most 0.0045.
Values may be sent and summed in bfloat16 or wider, within the bound.
No kernel may reach another device: no remote copies, remote signals or barrier semaphores. Data moves between devices by JAX's collectives and lax.ppermute only.
A program may use at most 64 MiB of HBM per device.

v0:
```python
import jax
import jax.numpy as jnp
from jax import lax
from jax.sharding import PartitionSpec as P


def joined(part, axis, combine):
    gathered = jax.tree.map(lambda a: lax.all_gather(a, axis), part)

    def take(source):
        return jax.tree.map(lambda a: lax.dynamic_index_in_dim(a, source, 0, False), gathered)

    return lax.fori_loop(
        1, lax.axis_size(axis), lambda source, state: combine(state, take(source)), take(0)
    )


def combine_stats(first, second):
    peak = jnp.maximum(first[0], second[0])
    total = first[1] * jnp.exp(first[0] - peak) + second[1] * jnp.exp(second[0] - peak)
    return (peak, total, first[2] + second[2], first[3] + second[3])


def on_device(embeddings, group_ids):
    row_count = lax.axis_size("row")
    col_count = lax.axis_size("col")
    row_index = lax.axis_index("row")
    col_index = lax.axis_index("col")
    rows = embeddings.shape[0]
    width = embeddings.shape[1]
    scale = 1.0 / jnp.sqrt(jnp.float32(width))
    whole = rows * row_count * col_count
    queries, query_groups = (
        lax.all_gather(embeddings, "col", axis=0, tiled=True),
        lax.all_gather(group_ids, "col", axis=0, tiled=True),
    )
    keys, key_groups = (
        lax.all_gather(embeddings, "row", axis=0, tiled=True),
        lax.all_gather(group_ids, "row", axis=0, tiled=True),
    )
    query_len = rows * col_count
    key_len = rows * row_count
    query_pos = row_index * query_len + jnp.arange(query_len, dtype=jnp.int32)
    key_local = jnp.arange(key_len, dtype=jnp.int32)
    key_pos = (key_local // rows * col_count + col_index) * rows + key_local % rows
    scores = (
        lax.dot_general(queries, keys, (((1,), (1,)), ((), ())), preferred_element_type=jnp.float32)
        * scale
    )
    selfs = query_pos[:, None] == key_pos[None, :]
    positive = jnp.logical_and(query_groups[:, None] == key_groups[None, :], jnp.logical_not(selfs))
    masked = jnp.where(selfs, jnp.float32(-1e30), scores)
    peak = jnp.max(masked, axis=1)
    total = jnp.sum(jnp.exp(masked - peak[:, None]), axis=1)
    possum = jnp.sum(jnp.where(positive, scores, jnp.float32(0.0)), axis=1)
    count = jnp.sum(positive.astype(jnp.float32), axis=1)
    peak, total, possum, count = joined((peak, total, possum, count), "col", combine_stats)
    lse = peak + jnp.log(total)
    inverse = 1.0 / count
    row_loss = lse - possum * inverse
    own_start = col_index * rows
    own_loss = lax.dynamic_slice_in_dim(row_loss, own_start, rows, 0)
    loss = lax.psum(jnp.sum(own_loss), ("row", "col")) / whole
    weight = (
        jnp.exp(masked - lse[:, None]) - jnp.where(positive, inverse[:, None], jnp.float32(0.0))
    ) / whole
    weight = weight.astype(jnp.bfloat16)
    own_lse = lax.dynamic_slice_in_dim(lse, own_start, rows, 0)
    own_inverse = lax.dynamic_slice_in_dim(inverse, own_start, rows, 0)
    key_lse, key_inverse = (
        lax.all_gather(own_lse, "row", axis=0, tiled=True),
        lax.all_gather(own_inverse, "row", axis=0, tiled=True),
    )
    mirrored = (
        jnp.exp(masked - key_lse[None, :])
        - jnp.where(positive, key_inverse[None, :], jnp.float32(0.0))
    ) / whole
    mirrored = mirrored.astype(jnp.bfloat16)
    both_term = jnp.dot(weight, keys, preferred_element_type=jnp.float32) + jnp.dot(
        mirrored, keys, preferred_element_type=jnp.float32
    )
    grad = scale * lax.psum_scatter(both_term, "col", scatter_dimension=0, tiled=True)
    return (loss, grad.astype(jnp.bfloat16))


def solution(mesh):
    in_specs = (P(("row", "col"), None), P(("row", "col")))
    out_specs = (P(), P(("row", "col"), None))
    return jax.shard_map(
        on_device, mesh=mesh, in_specs=in_specs, out_specs=out_specs, check_vma=False
    )
```

profile of v0, /device:TPU:0, one launch (start us, length us, event | category | flops | bytes accessed | tf_op | source)
XLA Modules:
  0.0 142.1 jit_solution(13007018784665534406)
XLA Ops:
  7.2 0.0 reduce-scatter.2.cloned.1.call-start
  7.2 6.7 %all_gather.42 = bf16[64,1024]{1,0:T(8,128)(2,1)S(1)} all-gather(bf16[16,1024]{1,0:T(8,128)(2,1)} %param.4), channel_id=1, replica_groups=mesh['row'=8,'col'=4] {'col'}, dimensions={0}, use_global_device_ids=true | all-gather | bytes 163840 | tf_op jit(solution)/shard_map/all_gather | solution.py:34
  13.9 31.6 %all_gather.43 = bf16[128,1024]{1,0:T(8,128)(2,1)S(1)} all-gather(bf16[16,1024]{1,0:T(8,128)(2,1)S(1)} %copy-done), channel_id=1, replica_groups=mesh['row'=8,'col'=4] {'row'}, dimensions={0}, use_global_device_ids=true | all-gather | bytes 294912 | tf_op jit(solution)/shard_map/all_gather | solution.py:38
  45.6 0.6 copy-done.3
  46.2 0.7 dynamic-slice.3
  46.9 0.6 dynamic-slice
  49.5 0.6 copy-done.1
  50.1 0.2 dynamic-update-slice.2
  50.3 4.9 %all-reduce.2 = s32[64]{0:T(128)S(1)} all-reduce(s32[64]{0:T(128)S(1)} %dynamic-update-slice.2), channel_id=1, replica_groups=mesh['row'=8,'col'=4] {'col'}, use_global_device_ids=true, to_apply=%add.2 | all-reduce | flops 64 | bytes 512
  55.2 0.2 dynamic-update-slice.3
  55.4 10.6 %all-reduce.3 = s32[128]{0:T(128)S(1)} all-reduce(s32[128]{0:T(128)S(1)} %dynamic-update-slice.3), channel_id=1, replica_groups=mesh['row'=8,'col'=4] {'row'}, use_global_device_ids=true, to_apply=%add.3 | all-reduce | flops 128 | bytes 1024
  66.0 0.3 fusion.10
  66.3 0.2 dynamic-update-slice
  66.6 0.2 select_reduce_fusion
  66.8 0.2 dynamic-update-slice.5
  67.1 0.2 dynamic-update-slice.4
  67.3 0.2 dynamic-update-slice.1
  67.5 5.6 %all-reduce.9 = (f32[256]{0:T(256)S(1)}, f32[256]{0:T(256)S(1)}, f32[256]{0:T(256)S(1)}, f32[256]{0:T(256)S(1)}) all-reduce(f32[256]{0:T(256)S(1)} %dynamic-update-slice, f32[256]{0:T(256)S(1)} %dynamic-update-slice.1, f32[256]{0:T(256)S(1)} %dynamic-update-slice.4, f32[256]{0:T(256)S(1)} %dynamic-update-slice.5), channel_id=2, replica_groups=mesh['row'=8,'col'=4] {'col'}, use_global_device_ids=true, to_apply=%add | all-reduce | flops 1024 | bytes 8192
  73.1 0.1 reshape.42
  73.2 0.1 reshape.41
  73.3 0.1 reshape.40
  73.4 0.1 reshape.39
  73.4 0.2 while.21
  73.6 0.2 fusion.11
  73.9 0.2 dynamic-slice_dynamic-update-slice_fusion
  74.1 0.2 dynamic-slice_dynamic-update-slice_fusion.1
  74.2 19.1 %all-reduce.8 = (f32[128]{0:T(128)S(1)}, f32[128]{0:T(128)S(1)}) all-reduce(f32[128]{0:T(128)S(1)} %dynamic-slice_dynamic-update-slice_fusion, f32[128]{0:T(128)S(1)} %dynamic-slice_dynamic-update-slice_fusion.1), channel_id=1, replica_groups=mesh['row'=8,'col'=4] {'row'}, use_global_device_ids=true, to_apply=%add.7 | all-reduce | flops 256 | bytes 2048
  93.3 0.9 convolution_add_fusion
  94.3 0.7 dynamic-slice_reduce_fusion
  95.0 37.0 %psum.7 = f32[]{:T(128)} all-reduce(f32[]{:T(128)} %dynamic-slice_reduce_fusion), channel_id=1, replica_groups=mesh['row'=8,'col'=4] {'row','col'}, use_global_device_ids=true, to_apply=%region_7.8 | all-reduce | flops 1 | bytes 8 | tf_op jit(solution)/shard_map/psum | solution.py:63
  132.6 0.0 reduce-scatter.2.cloned.1.call-done
  132.7 1.5 %multiply_convert_fusion = bf16[16,1024]{1,0:T(8,128)(2,1)} fusion(f32[16,1024]{1,0:T(8,128)} %reduce-scatter.2.cloned.1.call-done), kind=kLoop, calls=%fused_computation.15 | loop fusion | flops 32768 | bytes 98304 | tf_op jit(solution)/shard_map/convert_element_type | solution.py:83
  (28 shorter events, 0.2 us)
Async XLA Ops:
  7.2 125.5 %reduce-scatter.2.cloned.1.call-start = ((), (), s32[]{:S(2)}) async-start(), calls=%async_computation.1 | async-start | bytes 327680 | tf_op jit(solution)/shard_map/reduce_scatter | solution.py:82
  7.2 6.7 %copy-start = (bf16[16,1024]{1,0:T(8,128)(2,1)S(1)}, bf16[16,1024]{1,0:T(8,128)(2,1)}, u32[]{:S(2)}) copy-start(bf16[16,1024]{1,0:T(8,128)(2,1)} %param.4) | copy-start | bytes 98308
  45.5 0.7 copy-start.3
  46.2 0.7 copy-start.2
  49.4 0.7 copy-start.1
Sparse Core Ops, SparseCore 0:
  94.4 16.7 reduce-scatter.1
where the time goes:
time: 143 us; the launch traced here: 142 us
  blocking collectives  116 us (81%)
  between operations  17.9 us (13%)
  local copies, waits for them, and re-layouts  4.48 us (3%)
  other arithmetic  2.51 us (2%)
  matrix products  1.48 us (1%)
    unnamed x4, blocking collectives  40.3 us
    psum x1, blocking collectives, on_device(): loss = lax.psum(jnp.sum(own_loss), ('row', 'col')) / whole  37 us
    all_gather x1, blocking collectives, on_device(): lax.all_gather(embeddings, 'row', axis=0, tiled=True)  31.6 us
    all_gather x1, blocking collectives, on_device(): lax.all_gather(embeddings, 'col', axis=0, tiled=True)  6.72 us
    unnamed x25, local copies, waits for them, and re-layouts  4.14 us
  transfers between devices with their start and end apart: 1, of which 0 were waited for; matrix products, arithmetic and copies ran while one was open for 0% of the time, Pallas kernels for 0%

commit v1 on v0

v1 whole, which is shorter than its diff:
```python
import jax
import jax.numpy as jnp
from jax import lax
from jax.experimental import pallas as pl
from jax.experimental.pallas import tpu as pltpu
from jax.sharding import PartitionSpec as P

AXES = ("row", "col")
LANES = 128
RADIX = 256


def stage_bits(bits, parity):
    far = [b for b in range(bits) if b >= 3]
    near = [b for b in (1, 2) if b < bits]
    return far + (near if parity == 0 else near[::-1]) + [0]


def swap_pairs(devices, stage):
    bits = devices.bit_length() - 1
    return [(i, i ^ (1 << stage_bits(bits, i & 1)[stage])) for i in range(devices)]


def loss_and_grad(width, own_ref, near_ref, far_ref, loss_ref, grad_ref, lse_ref, inv_ref):
    own = own_ref.shape[0]
    half = near_ref.shape[0]
    total = 2 * half
    block = min(half, 256)
    scale = 1.0 / jnp.sqrt(jnp.float32(width))
    refs = (near_ref, far_ref)
    nt = (((1,), (1,)), ((), ()))

    def dot_nt(a, b):
        return lax.dot_general(a, b, nt, preferred_element_type=jnp.float32)

    lane = lax.broadcasted_iota(jnp.int32, (block, LANES), 1)
    pick = jnp.where(lane == 0, 1.0, jnp.where(lane == 1, float(RADIX), 0.0)).astype(jnp.bfloat16)

    def block_stats(side, start, loss):
        cols = refs[side][pl.ds(start, block), :width]
        col_ids = dot_nt(pick[:16], refs[side][pl.ds(start, block), width:])[:1]
        col_pos = side * half + start + lax.broadcasted_iota(jnp.int32, (block, block), 1)
        parts = []
        for other in range(2):
            for first in range(0, half, block):
                rows = refs[other][first : first + block, :width]
                s = dot_nt(rows, cols) * scale
                row_ids = dot_nt(refs[other][first : first + block, width:], pick)
                row_pos = other * half + first + lax.broadcasted_iota(jnp.int32, (block, block), 0)
                selfs = row_pos == col_pos
                positive = jnp.logical_and(row_ids == col_ids, jnp.logical_not(selfs))
                masked = jnp.where(selfs, jnp.float32(-1e30), s)
                top = jnp.max(masked, axis=0, keepdims=True)
                add = jnp.sum(jnp.exp(masked - top), axis=0, keepdims=True)
                possum = jnp.sum(jnp.where(positive, s, 0.0), axis=0, keepdims=True)
                count = jnp.sum(positive.astype(jnp.float32), axis=0, keepdims=True)
                parts.append((top, add, possum, count))
        peak = parts[0][0]
        for p in parts[1:]:
            peak = jnp.maximum(peak, p[0])
        added = sum(p[1] * jnp.exp(p[0] - peak) for p in parts)
        possum = sum(p[2] for p in parts)
        inverse = 1.0 / sum(p[3] for p in parts)
        lse = peak + jnp.log(added)
        at = pl.ds(side * half + start, block)
        lse_ref[:, at] = lse
        inv_ref[:, at] = inverse
        return loss + jnp.sum(lse - possum * inverse)

    loss = jnp.float32(0.0)
    for side in range(2):
        steps = half // block
        if steps == 1:
            loss = block_stats(side, 0, loss)
        else:
            loss = lax.fori_loop(
                0, steps, lambda k, v: block_stats(side, pl.multiple_of(k * block, block), v), loss
            )
    loss_ref[0] = loss / total

    mine = own_ref[:, :width]
    own_ids = dot_nt(own_ref[:, width:], pick[:LANES])[:, :1]
    out = jnp.zeros((2 * own, width), jnp.float32)
    s, positive = [], []
    for other in range(2):
        s.append(dot_nt(mine, refs[other][:, :width]) * scale)
        ids = dot_nt(pick[:16], refs[other][:, width:])[:1]
        positive.append(own_ids == ids)
    s = jnp.concatenate(s, axis=1)
    positive = jnp.concatenate(positive, axis=1)
    selfs = lax.broadcasted_iota(jnp.int32, s.shape, 0) == lax.broadcasted_iota(jnp.int32, s.shape, 1)
    positive = jnp.logical_and(positive, jnp.logical_not(selfs))
    masked = jnp.where(selfs, jnp.float32(-1e30), s)
    peak = jnp.max(masked, axis=1, keepdims=True)
    lse = peak + jnp.log(jnp.sum(jnp.exp(masked - peak), axis=1, keepdims=True))
    inverse = 1.0 / jnp.sum(positive.astype(jnp.float32), axis=1, keepdims=True)
    weight = (jnp.exp(masked - lse) - jnp.where(positive, inverse, 0.0)) / total
    mirrored = (jnp.exp(masked - lse_ref[...]) - jnp.where(positive, inv_ref[...], 0.0)) / total
    both = jnp.concatenate([weight, mirrored], axis=0).astype(jnp.bfloat16)
    for other in range(2):
        out += jnp.dot(
            both[:, other * half : (other + 1) * half],
            refs[other][:, :width],
            preferred_element_type=jnp.float32,
        )
    grad_ref[...] = (scale * (out[:own] + out[own:])).astype(jnp.bfloat16)


def on_device(devices, embeddings, group_ids):
    rows, width = embeddings.shape
    bits = devices.bit_length() - 1
    lane = lax.broadcasted_iota(jnp.int32, (rows, LANES), 1)
    ids = group_ids[:, None]
    coded = jnp.where(lane == 0, ids % RADIX, jnp.where(lane == 1, ids // RADIX, 0))
    held = jnp.concatenate([embeddings, coded.astype(jnp.bfloat16)], axis=1)
    own = held
    for stage in range(bits):
        came = lax.ppermute(held, AXES, swap_pairs(devices, stage))
        if stage < bits - 1:
            held = jnp.concatenate([held, came], axis=0)
    total = rows * devices
    vmem = pl.BlockSpec(memory_space=pltpu.VMEM)
    loss, grad = pl.pallas_call(
        lambda *refs: loss_and_grad(width, *refs),
        out_shape=(
            jax.ShapeDtypeStruct((1,), jnp.float32),
            jax.ShapeDtypeStruct((rows, width), jnp.bfloat16),
        ),
        in_specs=[vmem, vmem, vmem],
        out_specs=(pl.BlockSpec(memory_space=pltpu.SMEM), vmem),
        scratch_shapes=[pltpu.VMEM((1, total), jnp.float32), pltpu.VMEM((1, total), jnp.float32)],
        cost_estimate=pl.CostEstimate(
            flops=2 * total * total * width, bytes_accessed=2 * total * width, transcendentals=total * total
        ),
    )(own, held, came)
    return (loss[0], grad)


def solution(mesh):
    in_specs = (P(AXES, None), P(AXES))
    out_specs = (P(), P(AXES, None))
    devices = mesh.shape["row"] * mesh.shape["col"]

    def body(embeddings, group_ids):
        return on_device(devices, embeddings, group_ids)

    return jax.shard_map(body, mesh=mesh, in_specs=in_specs, out_specs=out_specs, check_vma=False)
```

time: 143 us -> 32.3 us (0.23)
  blocking collectives: 116 us -> 0 us
  between operations: 17.9 us -> 0.7 us
  waiting for transfers between devices: 0.04 us -> 14.9 us
  starting transfers between devices: 0.04 us -> 10.3 us
  Pallas kernels: 0 us -> 3.71 us
  local copies, waits for them, and re-layouts: 4.48 us -> 1.53 us
  other arithmetic: 2.51 us -> 0.98 us
  matrix products: 1.48 us -> 0 us
    unnamed x4 -> x0, blocking collectives: 40.3 us -> none
    all_gather x2 -> x0, blocking collectives: 38.3 us -> none  [the longest x1 31.6 us: on_device(): lax.all_gather(embeddings, 'row', axis=0, tiled=True)]
    psum x1 -> x0, blocking collectives: 37 us -> none  [on_device(): loss = lax.psum(jnp.sum(own_loss), ('row', 'col')) / whole]
    ppermute x0 -> x5, waiting for transfers between devices: none -> 14.9 us  [on_device(): came = lax.ppermute(held, AXES, swap_pairs(devices, stage))]
    ppermute x0 -> x5, starting transfers between devices: none -> 10.3 us  [on_device(): came = lax.ppermute(held, AXES, swap_pairs(devices, stage))]
    pallas_call x0 -> x1, Pallas kernels: none -> 3.71 us  [on_device(): pl.pallas_call(lambda *refs: loss_and_grad(width, *refs), out_shape=(jax....]
    unnamed x25 -> x13, local copies, waits for them, and re-layouts: 4.14 us -> 1.5 us
    dot_general x3 -> x0, matrix products: 1.48 us -> none  [the longest x1 0.93 us: on_device(): jnp.dot(mirrored, keys, preferred_element_type=jnp.float32)]
  transfers between devices with their start and end apart: 1 -> 5, of which waited for: 0 -> 5; matrix products, arithmetic and copies ran while one was open for 0% -> 0% of each run, Pallas kernels for 0% -> 0%
where the time goes in v1:
time: 32.3 us; the launch traced here: 32.1 us
  waiting for transfers between devices  14.9 us (46%)
  starting transfers between devices  10.3 us (32%)
  Pallas kernels  3.71 us (11%)
  local copies, waits for them, and re-layouts  1.53 us (5%)
  other arithmetic  0.98 us (3%)
  between operations  0.7 us (2%)
    ppermute x5, waiting for transfers between devices, on_device(): came = lax.ppermute(held, AXES, swap_pairs(devices, stage))  14.9 us
    ppermute x5, starting transfers between devices, on_device(): came = lax.ppermute(held, AXES, swap_pairs(devices, stage))  10.3 us
    pallas_call x1, Pallas kernels, on_device(): pl.pallas_call(lambda *refs: loss_and_grad(width, *refs), out_shape=(jax....  3.71 us
    unnamed x13, local copies, waits for them, and re-layouts  1.5 us
    unnamed x1, other arithmetic  0.84 us
  transfers between devices with their start and end apart: 5, of which 5 were waited for; matrix products, arithmetic and copies ran while one was open for 0% of the time, Pallas kernels for 0%

profile of v1, /device:TPU:0, one launch (start us, length us, event | category | flops | bytes accessed | tf_op | source)
XLA Modules:
  0.0 32.1 jit_solution(17059555481814140671)
XLA Ops:
  0.6 0.0 copy-start.4
  0.7 0.6 %copy-done.4 = s32[16]{0:T(128)S(1)} copy-done((s32[16]{0:T(128)S(1)}, s32[16]{0:T(128)}, u32[]{:S(2)}) %copy-start.4) | copy-done | bytes 88
  1.3 0.1 select_convert_fusion
  1.4 0.0 copy-start
  1.4 0.8 %constant_dynamic-update-slice_fusion.4 = (bf16[256,1152]{1,0:T(8,128)(2,1)S(1)}, bf16[16,1152]{1,0:T(8,128)(2,1)S(1)}) fusion(bf16[16,128]{1,0:T(8,128)(2,1)S(1)} %select_convert_fusion, bf16[16,1024]{1,0:T(8,128)(2,1)} %param.2), kind=kLoop, calls=%fused_computation.8 | loop fusion | flops 73727 | bytes 110592
  2.2 0.0 copy-start.1
  2.2 3.1 %collective-permute-start = (bf16[16,1152]{1,0:T(8,128)(2,1)S(1)}, bf16[16,1152]{1,0:T(8,128)(2,1)S(1)}, u32[]{:S(2)}, u32[]{:S(2)}) collective-permute-start(bf16[16,1152]{1,0:T(8,128)(2,1)S(1)} %get-tuple-element.7.refs_0_), channel_id=1, source_target_pairs={{0,8},{1,9},{2,10},{3,11},{4,12},{5,13},{6,14},{7,15},{8,0},{9,1},... | collective-permute-start | bytes 110600 | tf_op jit(solution)/shard_map/ppermute | solution.py:118
  5.3 1.9 %collective-permute-done = bf16[16,1152]{1,0:T(8,128)(2,1)S(1)} collective-permute-done((bf16[16,1152]{1,0:T(8,128)(2,1)S(1)}, bf16[16,1152]{1,0:T(8,128)(2,1)S(1)}, u32[]{:S(2)}, u32[]{:S(2)}) %collective-permute-start) | collective-permute-done | bytes 36896 | tf_op jit(solution)/shard_map/ppermute | solution.py:118
  7.2 0.0 copy-done
  7.2 0.0 copy-done.1
  7.2 3.1 %collective-permute-start.1 = (bf16[32,1152]{1,0:T(8,128)(2,1)S(1)}, bf16[32,1152]{1,0:T(8,128)(2,1)S(1)}, u32[]{:S(2)}, u32[]{:S(2)}) collective-permute-start(bf16[32,1152]{1,0:T(8,128)(2,1)S(1)} %pad_maximum_fusion.2), channel_id=1, source_target_pairs={{0,16},{1,17},{2,18},{3,19},{4,20},{5,21},{6,22},{7,23},{8,24},{9,... | collective-permute-start | bytes 221192 | tf_op jit(solution)/shard_map/ppermute | solution.py:118
  10.3 2.3 %collective-permute-done.1 = bf16[32,1152]{1,0:T(8,128)(2,1)S(1)} collective-permute-done((bf16[32,1152]{1,0:T(8,128)(2,1)S(1)}, bf16[32,1152]{1,0:T(8,128)(2,1)S(1)}, u32[]{:S(2)}, u32[]{:S(2)}) %collective-permute-start.1) | collective-permute-done | bytes 73760 | tf_op jit(solution)/shard_map/ppermute | solution.py:118
  12.7 1.9 %collective-permute-start.2 = (bf16[64,1152]{1,0:T(8,128)(2,1)S(1)}, bf16[64,1152]{1,0:T(8,128)(2,1)S(1)}, u32[]{:S(2)}, u32[]{:S(2)}) collective-permute-start(bf16[64,1152]{1,0:T(8,128)(2,1)S(1)} %pad_maximum_fusion.1), channel_id=1, source_target_pairs={{0,2},{1,5},{2,0},{3,7},{4,6},{5,1},{6,4},{7,3},{8,10},{9,13},{10,... | collective-permute-start | bytes 442376 | tf_op jit(solution)/shard_map/ppermute | solution.py:118
  14.6 4.0 %collective-permute-done.2 = bf16[64,1152]{1,0:T(8,128)(2,1)S(1)} collective-permute-done((bf16[64,1152]{1,0:T(8,128)(2,1)S(1)}, bf16[64,1152]{1,0:T(8,128)(2,1)S(1)}, u32[]{:S(2)}, u32[]{:S(2)}) %collective-permute-start.2) | collective-permute-done | bytes 147488 | tf_op jit(solution)/shard_map/ppermute | solution.py:118
  18.6 2.2 %collective-permute-start.3 = (bf16[128,1152]{1,0:T(8,128)(2,1)S(1)}, bf16[128,1152]{1,0:T(8,128)(2,1)S(1)}, u32[]{:S(2)}, u32[]{:S(2)}) collective-permute-start(bf16[128,1152]{1,0:T(8,128)(2,1)S(1)} %pad_maximum_fusion), channel_id=1, source_target_pairs={{0,4},{1,3},{2,6},{3,1},{4,0},{5,7},{6,2},{7,5},{8,12},{9,11},{10,... | collective-permute-start | bytes 884744 | tf_op jit(solution)/shard_map/ppermute | solution.py:118
  20.8 4.7 %collective-permute-done.3 = bf16[128,1152]{1,0:T(8,128)(2,1)S(1)} collective-permute-done((bf16[128,1152]{1,0:T(8,128)(2,1)S(1)}, bf16[128,1152]{1,0:T(8,128)(2,1)S(1)}, u32[]{:S(2)}, u32[]{:S(2)}) %collective-permute-start.3) | collective-permute-done | bytes 294944 | tf_op jit(solution)/shard_map/ppermute | solution.py:118
  25.5 0.0 copy-start.2
  25.5 0.1 collective-permute-start.4
  25.6 2.0 %collective-permute-done.4.refs_2_ = bf16[256,1152]{1,0:T(8,128)(2,1)S(1)} collective-permute-done((bf16[256,1152]{1,0:T(8,128)(2,1)S(1)}, bf16[256,1152]{1,0:T(8,128)(2,1)S(1)}, u32[]{:S(2)}, u32[]{:S(2)}) %collective-permute-start.4) | collective-permute-done | bytes 589856 | tf_op jit(solution)/shard_map/ppermute | solution.py:118
  27.6 0.0 copy-done.2
  27.6 0.0 copy-start.3
  27.6 0.8 %copy-done.3 = bf16[256,1152]{1,0:T(8,128)(2,1)} copy-done((bf16[256,1152]{1,0:T(8,128)(2,1)}, bf16[256,1152]{1,0:T(8,128)(2,1)S(1)}, u32[]{:S(2)}) %copy-start.3) | copy-done | bytes 589848
  28.4 3.7 %shard_map.41 = (f32[1]{0:T(128)}, bf16[16,1024]{1,0:T(8,128)(2,1)}) custom-call(bf16[16,1152]{1,0:T(8,128)(2,1)} %copy-done.1, bf16[256,1152]{1,0:T(8,128)(2,1)} %copy-done.2, bf16[256,1152]{1,0:T(8,128)(2,1)} %copy-done.3), custom_call_target="tpu_custom_call" | custom-call | flops 536870912 | bytes 1048576 | tf_op jit(solution)/shard_map/pallas_call | solution.py:123
  (9 shorter events, 0.1 us)
Async XLA Ops:
  0.6 0.7 %copy-start.4 = (s32[16]{0:T(128)S(1)}, s32[16]{0:T(128)}, u32[]{:S(2)}) copy-start(s32[16]{0:T(128)} %param.3) | copy-start | bytes 196
  1.4 5.8 %copy-start = (bf16[16,1024]{1,0:T(8,128)(2,1)S(1)}, bf16[16,1024]{1,0:T(8,128)(2,1)}, u32[]{:S(2)}) copy-start(bf16[16,1024]{1,0:T(8,128)(2,1)} %param.2) | copy-start | bytes 98308
  2.2 5.0 %copy-start.1 = (bf16[16,1152]{1,0:T(8,128)(2,1)}, bf16[16,1152]{1,0:T(8,128)(2,1)S(1)}, u32[]{:S(2)}) copy-start(bf16[16,1152]{1,0:T(8,128)(2,1)S(1)} %get-tuple-element.7.refs_0_) | copy-start | bytes 110596
  2.2 5.0 %collective-permute-start = (bf16[16,1152]{1,0:T(8,128)(2,1)S(1)}, bf16[16,1152]{1,0:T(8,128)(2,1)S(1)}, u32[]{:S(2)}, u32[]{:S(2)}) collective-permute-start(bf16[16,1152]{1,0:T(8,128)(2,1)S(1)} %get-tuple-element.7.refs_0_), channel_id=1, source_target_pairs={{0,8},{1,9},{2,10},{3,11},{4,12},{5,13},{6,14},{7,15},{8,0},{9,1},... | collective-permute-start | bytes 110600 | tf_op jit(solution)/shard_map/ppermute | solution.py:118
  7.2 5.4 %collective-permute-start.1 = (bf16[32,1152]{1,0:T(8,128)(2,1)S(1)}, bf16[32,1152]{1,0:T(8,128)(2,1)S(1)}, u32[]{:S(2)}, u32[]{:S(2)}) collective-permute-start(bf16[32,1152]{1,0:T(8,128)(2,1)S(1)} %pad_maximum_fusion.2), channel_id=1, source_target_pairs={{0,16},{1,17},{2,18},{3,19},{4,20},{5,21},{6,22},{7,23},{8,24},{9,... | collective-permute-start | bytes 221192 | tf_op jit(solution)/shard_map/ppermute | solution.py:118
  12.7 5.9 %collective-permute-start.2 = (bf16[64,1152]{1,0:T(8,128)(2,1)S(1)}, bf16[64,1152]{1,0:T(8,128)(2,1)S(1)}, u32[]{:S(2)}, u32[]{:S(2)}) collective-permute-start(bf16[64,1152]{1,0:T(8,128)(2,1)S(1)} %pad_maximum_fusion.1), channel_id=1, source_target_pairs={{0,2},{1,5},{2,0},{3,7},{4,6},{5,1},{6,4},{7,3},{8,10},{9,13},{10,... | collective-permute-start | bytes 442376 | tf_op jit(solution)/shard_map/ppermute | solution.py:118
  18.6 6.9 %collective-permute-start.3 = (bf16[128,1152]{1,0:T(8,128)(2,1)S(1)}, bf16[128,1152]{1,0:T(8,128)(2,1)S(1)}, u32[]{:S(2)}, u32[]{:S(2)}) collective-permute-start(bf16[128,1152]{1,0:T(8,128)(2,1)S(1)} %pad_maximum_fusion), channel_id=1, source_target_pairs={{0,4},{1,3},{2,6},{3,1},{4,0},{5,7},{6,2},{7,5},{8,12},{9,11},{10,... | collective-permute-start | bytes 884744 | tf_op jit(solution)/shard_map/ppermute | solution.py:118
  25.5 2.1 %copy-start.2 = (bf16[256,1152]{1,0:T(8,128)(2,1)}, bf16[256,1152]{1,0:T(8,128)(2,1)S(1)}, u32[]{:S(2)}) copy-start(bf16[256,1152]{1,0:T(8,128)(2,1)S(1)} %constant_dynamic-update-slice_fusion.refs_1_) | copy-start | bytes 1769476
  25.5 2.1 %collective-permute-start.4 = (bf16[256,1152]{1,0:T(8,128)(2,1)S(1)}, bf16[256,1152]{1,0:T(8,128)(2,1)S(1)}, u32[]{:S(2)}, u32[]{:S(2)}) collective-permute-start(bf16[256,1152]{1,0:T(8,128)(2,1)S(1)} %constant_dynamic-update-slice_fusion.refs_1_), channel_id=1, source_target_pairs={{0,1},{1,0},{2,3},{3,2},{4,5},{5,4},{6,7},{7,6},{8,9},{9,8},{10,11... | collective-permute-start | bytes 1769480 | tf_op jit(solution)/shard_map/ppermute | solution.py:118
  27.6 0.8 %copy-start.3 = (bf16[256,1152]{1,0:T(8,128)(2,1)}, bf16[256,1152]{1,0:T(8,128)(2,1)S(1)}, u32[]{:S(2)}) copy-start(bf16[256,1152]{1,0:T(8,128)(2,1)S(1)} %collective-permute-done.4.refs_2_) | copy-start | bytes 1769476

commit v2 on v1

--- a/solution.py
+++ b/solution.py
@@ -10,15 +10,17 @@
 RADIX = 256
 
 
-def stage_bits(bits, parity):
+def phases(bits):
     far = [b for b in range(bits) if b >= 3]
     near = [b for b in (1, 2) if b < bits]
-    return far + (near if parity == 0 else near[::-1]) + [0]
+    return [far[k : k + 2] for k in range(0, len(far), 2)] + [near, [0]]
 
 
-def swap_pairs(devices, stage):
-    bits = devices.bit_length() - 1
-    return [(i, i ^ (1 << stage_bits(bits, i & 1)[stage])) for i in range(devices)]
+def exchange(devices, group, held):
+    masks = [0]
+    for b in group:
+        masks += [m | (1 << b) for m in masks]
+    return [held] + [lax.ppermute(held, AXES, [(i, i ^ m) for i in range(devices)]) for m in masks[1:]]
 
 
 def loss_and_grad(width, own_ref, near_ref, far_ref, loss_ref, grad_ref, lse_ref, inv_ref):
@@ -114,10 +116,9 @@
     coded = jnp.where(lane == 0, ids % RADIX, jnp.where(lane == 1, ids // RADIX, 0))
     held = jnp.concatenate([embeddings, coded.astype(jnp.bfloat16)], axis=1)
     own = held
-    for stage in range(bits):
-        came = lax.ppermute(held, AXES, swap_pairs(devices, stage))
-        if stage < bits - 1:
-            held = jnp.concatenate([held, came], axis=0)
+    for group in phases(bits)[:-1]:
+        held = jnp.concatenate(exchange(devices, group, held), axis=0)
+    held, came = exchange(devices, [0], held)
     total = rows * devices
     vmem = pl.BlockSpec(memory_space=pltpu.VMEM)
     loss, grad = pl.pallas_call(
@@ -129,6 +130,7 @@
         in_specs=[vmem, vmem, vmem],
         out_specs=(pl.BlockSpec(memory_space=pltpu.SMEM), vmem),
         scratch_shapes=[pltpu.VMEM((1, total), jnp.float32), pltpu.VMEM((1, total), jnp.float32)],
+        compiler_params=pltpu.CompilerParams(vmem_limit_bytes=(8 << 20) + 8 * total * width),
         cost_estimate=pl.CostEstimate(
             flops=2 * total * total * width, bytes_accessed=2 * total * width, transcendentals=total * total
         ),

time: 32.3 us -> 27.7 us (0.86)
  waiting for transfers between devices: 14.9 us -> 13.4 us
  Pallas kernels: 3.71 us -> 2.49 us
  starting transfers between devices: 10.3 us -> 9.27 us
  local copies, waits for them, and re-layouts: 1.53 us -> 0.72 us
    ppermute x5 -> x7, waiting for transfers between devices: 14.9 us -> 13.4 us  [exchange(): lax.ppermute(held, AXES, [(i, i ^ m) for i in range(devices)])]
    pallas_call x1, Pallas kernels: 3.71 us -> 2.49 us  [on_device(): pl.pallas_call(lambda *refs: loss_and_grad(width, *refs), out_shape=(jax....]
    ppermute x5 -> x7, starting transfers between devices: 10.3 us -> 9.27 us  [exchange(): lax.ppermute(held, AXES, [(i, i ^ m) for i in range(devices)])]
    unnamed x13 -> x9, local copies, waits for them, and re-layouts: 1.5 us -> 0.7 us
  transfers between devices with their start and end apart: 5 -> 7, of which waited for: 5 -> 5; matrix products, arithmetic and copies ran while one was open for 0% -> 0% of each run, Pallas kernels for 0% -> 0%
where the time goes in v2:
time: 27.7 us; the launch traced here: 27.5 us
  waiting for transfers between devices  13.4 us (48%)
  starting transfers between devices  9.27 us (33%)
  Pallas kernels  2.49 us (9%)
  other arithmetic  0.94 us (3%)
  local copies, waits for them, and re-layouts  0.72 us (3%)
  between operations  0.68 us (2%)
    ppermute x7, waiting for transfers between devices, exchange(): lax.ppermute(held, AXES, [(i, i ^ m) for i in range(devices)])  13.4 us
    ppermute x7, starting transfers between devices, exchange(): lax.ppermute(held, AXES, [(i, i ^ m) for i in range(devices)])  9.27 us
    pallas_call x1, Pallas kernels, on_device(): pl.pallas_call(lambda *refs: loss_and_grad(width, *refs), out_shape=(jax....  2.49 us
    unnamed x1, other arithmetic  0.84 us
    unnamed x9, local copies, waits for them, and re-layouts  0.7 us
  transfers between devices with their start and end apart: 7, of which 5 were waited for; matrix products, arithmetic and copies ran while one was open for 0% of the time, Pallas kernels for 0%

profile of v2, /device:TPU:0, one launch (start us, length us, event | category | flops | bytes accessed | tf_op | source)
XLA Modules:
  0.0 27.5 jit_solution(12850090811066680728)
XLA Ops:
  0.6 0.0 copy-start.1
  0.7 0.6 %copy-done.1 = s32[16]{0:T(128)S(1)} copy-done((s32[16]{0:T(128)S(1)}, s32[16]{0:T(128)}, u32[]{:S(2)}) %copy-start.1) | copy-done | bytes 88
  1.3 0.1 select_convert_fusion
  1.4 0.0 copy-start
  1.4 0.8 %constant_dynamic-update-slice_fusion.6 = (bf16[256,1152]{1,0:T(8,128)(2,1)S(1)}, bf16[16,1152]{1,0:T(8,128)(2,1)S(1)}) fusion(bf16[16,128]{1,0:T(8,128)(2,1)S(1)} %select_convert_fusion, bf16[16,1024]{1,0:T(8,128)(2,1)} %param.2), kind=kLoop, calls=%fused_computation.8 | loop fusion | flops 73727 | bytes 110592
  2.2 3.1 %collective-permute-start = (bf16[16,1152]{1,0:T(8,128)(2,1)S(1)}, bf16[16,1152]{1,0:T(8,128)(2,1)S(1)}, u32[]{:S(2)}, u32[]{:S(2)}) collective-permute-start(bf16[16,1152]{1,0:T(8,128)(2,1)S(1)} %get-tuple-element.7.refs_0_), channel_id=1, source_target_pairs={{0,8},{1,9},{2,10},{3,11},{4,12},{5,13},{6,14},{7,15},{8,0},{9,1},... | collective-permute-start | bytes 110600 | tf_op jit(solution)/shard_map/ppermute | solution.py:23
  5.3 2.6 %collective-permute-start.1 = (bf16[16,1152]{1,0:T(8,128)(2,1)S(1)}, bf16[16,1152]{1,0:T(8,128)(2,1)S(1)}, u32[]{:S(2)}, u32[]{:S(2)}) collective-permute-start(bf16[16,1152]{1,0:T(8,128)(2,1)S(1)} %get-tuple-element.7.refs_0_), channel_id=1, source_target_pairs={{0,16},{1,17},{2,18},{3,19},{4,20},{5,21},{6,22},{7,23},{8,24},{9,... | collective-permute-start | bytes 110600 | tf_op jit(solution)/shard_map/ppermute | solution.py:23
  7.9 0.0 collective-permute-start.2
  7.9 0.0 collective-permute-done
  7.9 2.9 %collective-permute-done.1 = bf16[16,1152]{1,0:T(8,128)(2,1)S(1)} collective-permute-done((bf16[16,1152]{1,0:T(8,128)(2,1)S(1)}, bf16[16,1152]{1,0:T(8,128)(2,1)S(1)}, u32[]{:S(2)}, u32[]{:S(2)}) %collective-permute-start.1) | collective-permute-done | bytes 36896 | tf_op jit(solution)/shard_map/ppermute | solution.py:23
  10.8 2.8 %collective-permute-done.2 = bf16[16,1152]{1,0:T(8,128)(2,1)S(1)} collective-permute-done((bf16[16,1152]{1,0:T(8,128)(2,1)S(1)}, bf16[16,1152]{1,0:T(8,128)(2,1)S(1)}, u32[]{:S(2)}, u32[]{:S(2)}) %collective-permute-start.2) | collective-permute-done | bytes 36896 | tf_op jit(solution)/shard_map/ppermute | solution.py:23
  13.6 0.0 copy-done
  13.6 1.6 %collective-permute-start.3 = (bf16[64,1152]{1,0:T(8,128)(2,1)S(1)}, bf16[64,1152]{1,0:T(8,128)(2,1)S(1)}, u32[]{:S(2)}, u32[]{:S(2)}) collective-permute-start(bf16[64,1152]{1,0:T(8,128)(2,1)S(1)} %pad_maximum_fusion), channel_id=1, source_target_pairs={{0,2},{1,3},{2,0},{3,1},{4,6},{5,7},{6,4},{7,5},{8,10},{9,11},{10,... | collective-permute-start | bytes 442376 | tf_op jit(solution)/shard_map/ppermute | solution.py:23
  15.2 1.5 %collective-permute-start.4 = (bf16[64,1152]{1,0:T(8,128)(2,1)S(1)}, bf16[64,1152]{1,0:T(8,128)(2,1)S(1)}, u32[]{:S(2)}, u32[]{:S(2)}) collective-permute-start(bf16[64,1152]{1,0:T(8,128)(2,1)S(1)} %pad_maximum_fusion), channel_id=1, source_target_pairs={{0,4},{1,5},{2,6},{3,7},{4,0},{5,1},{6,2},{7,3},{8,12},{9,13},{10,... | collective-permute-start | bytes 442376 | tf_op jit(solution)/shard_map/ppermute | solution.py:23
  16.7 0.5 %collective-permute-start.5 = (bf16[64,1152]{1,0:T(8,128)(2,1)S(1)}, bf16[64,1152]{1,0:T(8,128)(2,1)S(1)}, u32[]{:S(2)}, u32[]{:S(2)}) collective-permute-start(bf16[64,1152]{1,0:T(8,128)(2,1)S(1)} %pad_maximum_fusion), channel_id=1, source_target_pairs={{0,6},{1,7},{2,4},{3,5},{4,2},{5,3},{6,0},{7,1},{8,14},{9,15},{10,... | collective-permute-start | bytes 442376 | tf_op jit(solution)/shard_map/ppermute | solution.py:23
  17.2 2.9 %collective-permute-done.3 = bf16[64,1152]{1,0:T(8,128)(2,1)S(1)} collective-permute-done((bf16[64,1152]{1,0:T(8,128)(2,1)S(1)}, bf16[64,1152]{1,0:T(8,128)(2,1)S(1)}, u32[]{:S(2)}, u32[]{:S(2)}) %collective-permute-start.3) | collective-permute-done | bytes 147488 | tf_op jit(solution)/shard_map/ppermute | solution.py:23
  20.1 2.8 %collective-permute-done.4 = bf16[64,1152]{1,0:T(8,128)(2,1)S(1)} collective-permute-done((bf16[64,1152]{1,0:T(8,128)(2,1)S(1)}, bf16[64,1152]{1,0:T(8,128)(2,1)S(1)}, u32[]{:S(2)}, u32[]{:S(2)}) %collective-permute-start.4) | collective-permute-done | bytes 147488 | tf_op jit(solution)/shard_map/ppermute | solution.py:23
  22.9 0.0 collective-permute-done.5
  22.9 0.1 collective-permute-start.6
  23.0 2.0 %collective-permute-done.6.refs_2_ = bf16[256,1152]{1,0:T(8,128)(2,1)S(1)} collective-permute-done((bf16[256,1152]{1,0:T(8,128)(2,1)S(1)}, bf16[256,1152]{1,0:T(8,128)(2,1)S(1)}, u32[]{:S(2)}, u32[]{:S(2)}) %collective-permute-start.6) | collective-permute-done | bytes 589856 | tf_op jit(solution)/shard_map/ppermute | solution.py:23
  25.0 2.5 %shard_map.41 = (f32[1]{0:T(128)}, bf16[16,1024]{1,0:T(8,128)(2,1)}) custom-call(bf16[16,1152]{1,0:T(8,128)(2,1)S(1)} %get-tuple-element.7.refs_0_, bf16[256,1152]{1,0:T(8,128)(2,1)S(1)} %constant_dynamic-update-slice_fusion.refs_1_, bf16[256,1152]{1,0:T(8,128)(2,1)S(1)} %collective-permute-done.6.refs_2_), custom_call_target="tpu_custom_call" | custom-call | flops 536870912 | bytes 1048576 | tf_op jit(solution)/shard_map/pallas_call | solution.py:124
  (9 shorter events, 0.1 us)
Async XLA Ops:
  0.6 0.7 %copy-start.1 = (s32[16]{0:T(128)S(1)}, s32[16]{0:T(128)}, u32[]{:S(2)}) copy-start(s32[16]{0:T(128)} %param.3) | copy-start | bytes 196
  1.4 12.2 %copy-start = (bf16[16,1024]{1,0:T(8,128)(2,1)S(1)}, bf16[16,1024]{1,0:T(8,128)(2,1)}, u32[]{:S(2)}) copy-start(bf16[16,1024]{1,0:T(8,128)(2,1)} %param.2) | copy-start | bytes 98308
  2.2 5.6 %collective-permute-start = (bf16[16,1152]{1,0:T(8,128)(2,1)S(1)}, bf16[16,1152]{1,0:T(8,128)(2,1)S(1)}, u32[]{:S(2)}, u32[]{:S(2)}) collective-permute-start(bf16[16,1152]{1,0:T(8,128)(2,1)S(1)} %get-tuple-element.7.refs_0_), channel_id=1, source_target_pairs={{0,8},{1,9},{2,10},{3,11},{4,12},{5,13},{6,14},{7,15},{8,0},{9,1},... | collective-permute-start | bytes 110600 | tf_op jit(solution)/shard_map/ppermute | solution.py:23
  5.3 5.5 %collective-permute-start.1 = (bf16[16,1152]{1,0:T(8,128)(2,1)S(1)}, bf16[16,1152]{1,0:T(8,128)(2,1)S(1)}, u32[]{:S(2)}, u32[]{:S(2)}) collective-permute-start(bf16[16,1152]{1,0:T(8,128)(2,1)S(1)} %get-tuple-element.7.refs_0_), channel_id=1, source_target_pairs={{0,16},{1,17},{2,18},{3,19},{4,20},{5,21},{6,22},{7,23},{8,24},{9,... | collective-permute-start | bytes 110600 | tf_op jit(solution)/shard_map/ppermute | solution.py:23
  7.9 5.8 %collective-permute-start.2 = (bf16[16,1152]{1,0:T(8,128)(2,1)S(1)}, bf16[16,1152]{1,0:T(8,128)(2,1)S(1)}, u32[]{:S(2)}, u32[]{:S(2)}) collective-permute-start(bf16[16,1152]{1,0:T(8,128)(2,1)S(1)} %get-tuple-element.7.refs_0_), channel_id=1, source_target_pairs={{0,24},{1,25},{2,26},{3,27},{4,28},{5,29},{6,30},{7,31},{8,16},{9,... | collective-permute-start | bytes 110600 | tf_op jit(solution)/shard_map/ppermute | solution.py:23
  13.6 6.4 %collective-permute-start.3 = (bf16[64,1152]{1,0:T(8,128)(2,1)S(1)}, bf16[64,1152]{1,0:T(8,128)(2,1)S(1)}, u32[]{:S(2)}, u32[]{:S(2)}) collective-permute-start(bf16[64,1152]{1,0:T(8,128)(2,1)S(1)} %pad_maximum_fusion), channel_id=1, source_target_pairs={{0,2},{1,3},{2,0},{3,1},{4,6},{5,7},{6,4},{7,5},{8,10},{9,11},{10,... | collective-permute-start | bytes 442376 | tf_op jit(solution)/shard_map/ppermute | solution.py:23
  15.2 7.7 %collective-permute-start.4 = (bf16[64,1152]{1,0:T(8,128)(2,1)S(1)}, bf16[64,1152]{1,0:T(8,128)(2,1)S(1)}, u32[]{:S(2)}, u32[]{:S(2)}) collective-permute-start(bf16[64,1152]{1,0:T(8,128)(2,1)S(1)} %pad_maximum_fusion), channel_id=1, source_target_pairs={{0,4},{1,5},{2,6},{3,7},{4,0},{5,1},{6,2},{7,3},{8,12},{9,13},{10,... | collective-permute-start | bytes 442376 | tf_op jit(solution)/shard_map/ppermute | solution.py:23
  16.7 6.2 %collective-permute-start.5 = (bf16[64,1152]{1,0:T(8,128)(2,1)S(1)}, bf16[64,1152]{1,0:T(8,128)(2,1)S(1)}, u32[]{:S(2)}, u32[]{:S(2)}) collective-permute-start(bf16[64,1152]{1,0:T(8,128)(2,1)S(1)} %pad_maximum_fusion), channel_id=1, source_target_pairs={{0,6},{1,7},{2,4},{3,5},{4,2},{5,3},{6,0},{7,1},{8,14},{9,15},{10,... | collective-permute-start | bytes 442376 | tf_op jit(solution)/shard_map/ppermute | solution.py:23
  22.9 2.1 %collective-permute-start.6 = (bf16[256,1152]{1,0:T(8,128)(2,1)S(1)}, bf16[256,1152]{1,0:T(8,128)(2,1)S(1)}, u32[]{:S(2)}, u32[]{:S(2)}) collective-permute-start(bf16[256,1152]{1,0:T(8,128)(2,1)S(1)} %constant_dynamic-update-slice_fusion.refs_1_), channel_id=1, source_target_pairs={{0,1},{1,0},{2,3},{3,2},{4,5},{5,4},{6,7},{7,6},{8,9},{9,8},{10,11... | collective-permute-start | bytes 1769480 | tf_op jit(solution)/shard_map/ppermute | solution.py:23

commit v3 on v2

v3 whole, which is shorter than its diff:
```python
import jax
import jax.numpy as jnp
from jax import lax
from jax.experimental import pallas as pl
from jax.experimental.pallas import tpu as pltpu
from jax.sharding import PartitionSpec as P

AXES = ("row", "col")
LANES = 128
RADIX = 256


def bit_groups(bits):
    return [b for b in reversed(range(bits)) if b >= 3], [b for b in (1, 2) if b < bits]


def masks_of(group):
    masks = [0]
    for b in group:
        masks += [m | (1 << b) for m in masks]
    return masks[1:]


def swap(devices, mask, held):
    return lax.ppermute(held, AXES, [(i, i ^ mask) for i in range(devices)])


def gather_rows(devices, held):
    far, near = bit_groups(devices.bit_length() - 1)
    for b in far[:-1]:
        held = jnp.concatenate([held, swap(devices, 1 << b | 1, held)], axis=0)
    late = swap(devices, 1 << far[-1] | 1, held)
    parts = [held, late]
    for part in (held, late):
        parts += [swap(devices, m | 1, part) for m in masks_of(near)]
    return jnp.concatenate(parts, axis=0)


def pack(rows_hbm, ids_hbm, out_ref, rows_ref, ids_ref, sems):
    rows, width = rows_ref.shape
    copies = [
        pltpu.make_async_copy(ids_hbm, ids_ref, sems.at[0]),
        pltpu.make_async_copy(rows_hbm, rows_ref, sems.at[1]),
    ]
    for copy in copies:
        copy.start()
    copies[0].wait()
    down = lax.broadcasted_iota(jnp.int32, (rows, rows), 0)
    across = lax.broadcasted_iota(jnp.int32, (rows, rows), 1)
    wide = jnp.broadcast_to(ids_ref[...], (rows, rows))
    ids = jnp.sum(jnp.where(down == across, wide, 0), axis=1, keepdims=True)
    lane = lax.broadcasted_iota(jnp.int32, (rows, LANES), 1)
    low, high = ids & (RADIX - 1), ids >> 8
    coded = jnp.where(lane == 0, low, jnp.where(lane == 1, high, 0))
    out_ref[:, width:] = coded.astype(jnp.float32).astype(jnp.bfloat16)
    copies[1].wait()
    out_ref[:, :width] = rows_ref[...]


def dot_nt(a, b):
    return lax.dot_general(a, b, (((1,), (1,)), ((), ())), preferred_element_type=jnp.float32)


def digits(rows):
    lane = lax.broadcasted_iota(jnp.int32, (rows, LANES), 1)
    return jnp.where(lane == 0, 1.0, jnp.where(lane == 1, float(RADIX), 0.0)).astype(jnp.bfloat16)


def block_stats(width, rows_ref, cols_ref, start, block, own, keep):
    scale = 1.0 / jnp.sqrt(jnp.float32(width))
    cols = cols_ref[pl.ds(start, block), :width]
    col_ids = dot_nt(digits(16), cols_ref[pl.ds(start, block), width:])[:1]
    parts = []
    for first in range(0, rows_ref.shape[0], block):
        s = dot_nt(rows_ref[first : first + block, :width], cols) * scale
        positive = dot_nt(rows_ref[first : first + block, width:], digits(block)) == col_ids
        masked = s
        if rows_ref is cols_ref:
            row_pos = first + lax.broadcasted_iota(jnp.int32, (block, block), 0)
            selfs = row_pos == start + lax.broadcasted_iota(jnp.int32, (block, block), 1)
            positive = jnp.logical_and(positive, jnp.logical_not(selfs))
            masked = jnp.where(selfs, jnp.float32(-1e30), s)
        if first == 0:
            keep(masked[:own], positive[:own])
        top = jnp.max(masked, axis=0, keepdims=True)
        add = jnp.sum(jnp.exp(masked - top), axis=0, keepdims=True)
        possum = jnp.sum(jnp.where(positive, s, 0.0), axis=0, keepdims=True)
        count = jnp.sum(jnp.where(positive, 1.0, 0.0), axis=0, keepdims=True)
        parts.append((top, add, possum, count))
    return merge(parts)


def merge(parts):
    peak = parts[0][0]
    for p in parts[1:]:
        peak = jnp.maximum(peak, p[0])
    added = sum(p[1] * jnp.exp(p[0] - peak) for p in parts)
    return peak, added, sum(p[2] for p in parts), sum(p[3] for p in parts)


def over_blocks(half, block, body, carry):
    if half == block:
        return body(0, carry)
    return lax.fori_loop(
        0, half // block, lambda k, v: body(pl.multiple_of(k * block, block), v), carry
    )


def near_stats(width, own, near_ref, stats_ref, scores_ref, positive_ref):
    half = near_ref.shape[0]
    block = min(half, 256)

    def body(start, carry):
        at = pl.ds(start, block)

        def keep(scores, positive):
            scores_ref[:, at] = scores
            positive_ref[:, at] = jnp.where(positive, 1.0, 0.0)

        stats = block_stats(width, near_ref, near_ref, start, block, own, keep)
        for k, value in enumerate(stats):
            stats_ref[k : k + 1, at] = value
        return carry

    over_blocks(half, block, body, 0)


def loss_and_grad(
    width, own, near_ref, far_ref, stats_ref, near_scores_ref, near_positive_ref,
    loss_ref, grad_ref, lse_ref, inv_ref, scores_ref, positive_ref,
):
    half = near_ref.shape[0]
    total = 2 * half
    block = min(half, 256)
    scale = 1.0 / jnp.sqrt(jnp.float32(width))
    scores_ref[:, :half] = near_scores_ref[...]
    positive_ref[:, :half] = near_positive_ref[...]

    def finish(at, stats, loss):
        peak, added, possum, count = stats
        inverse = 1.0 / count
        lse = peak + jnp.log(added)
        lse_ref[:, at] = lse
        inv_ref[:, at] = inverse
        return loss + jnp.sum(lse - possum * inverse)

    def near_columns(start, loss):
        at = pl.ds(start, block)
        had = tuple(stats_ref[k : k + 1, at] for k in range(4))
        more = block_stats(width, far_ref, near_ref, start, block, own, lambda *_: None)
        return finish(at, merge([had, more]), loss)

    def far_columns(start, loss):
        at = pl.ds(half + start, block)

        def keep(scores, positive):
            scores_ref[:, at] = scores
            positive_ref[:, at] = jnp.where(positive, 1.0, 0.0)

        first = block_stats(width, near_ref, far_ref, start, block, own, keep)
        second = block_stats(width, far_ref, far_ref, start, block, own, lambda *_: None)
        return finish(at, merge([first, second]), loss)

    loss = over_blocks(half, block, far_columns, jnp.float32(0.0))
    loss = over_blocks(half, block, near_columns, loss)
    loss_ref[0] = loss / total

    masked = scores_ref[...]
    positive = positive_ref[...]
    peak = jnp.max(masked, axis=1, keepdims=True)
    lse = peak + jnp.log(jnp.sum(jnp.exp(masked - peak), axis=1, keepdims=True))
    inverse = 1.0 / jnp.sum(positive, axis=1, keepdims=True)
    weight = (jnp.exp(masked - lse) - positive * inverse) / total
    mirrored = (jnp.exp(masked - lse_ref[...]) - positive * inv_ref[...]) / total
    both = jnp.concatenate([weight, mirrored], axis=0).astype(jnp.bfloat16)
    out = jnp.zeros((2 * own, width), jnp.float32)
    for k, ref in enumerate((near_ref, far_ref)):
        out += jnp.dot(
            both[:, k * half : (k + 1) * half], ref[:, :width], preferred_element_type=jnp.float32
        )
    grad_ref[...] = (scale * (out[:own] + out[own:])).astype(jnp.bfloat16)


def on_device(devices, embeddings, group_ids):
    rows, width = embeddings.shape
    total = rows * devices
    half = total // 2
    vmem = pl.BlockSpec(memory_space=pltpu.VMEM)
    params = pltpu.CompilerParams(vmem_limit_bytes=(8 << 20) + 8 * total * width)
    held = pl.pallas_call(
        pack,
        out_shape=jax.ShapeDtypeStruct((rows, width + LANES), jnp.bfloat16),
        in_specs=[pl.BlockSpec(memory_space=pltpu.HBM)] * 2,
        out_specs=vmem,
        scratch_shapes=[
            pltpu.VMEM((rows, width), jnp.bfloat16),
            pltpu.VMEM((1, rows), jnp.int32),
            pltpu.SemaphoreType.DMA((2,)),
        ],
        compiler_params=pltpu.CompilerParams(vmem_limit_bytes=60 << 20),
    )(embeddings, group_ids[None, :])
    near = gather_rows(devices, held)
    far = swap(devices, 1, near)
    stats = pl.pallas_call(
        lambda *refs: near_stats(width, rows, *refs),
        out_shape=(
            jax.ShapeDtypeStruct((4, half), jnp.float32),
            jax.ShapeDtypeStruct((rows, half), jnp.float32),
            jax.ShapeDtypeStruct((rows, half), jnp.float32),
        ),
        in_specs=[vmem],
        out_specs=(vmem, vmem, vmem),
        compiler_params=params,
        cost_estimate=pl.CostEstimate(
            flops=2 * half * half * width, bytes_accessed=2 * half * width, transcendentals=half * half
        ),
    )(near)
    loss, grad = pl.pallas_call(
        lambda *refs: loss_and_grad(width, rows, *refs),
        out_shape=(
            jax.ShapeDtypeStruct((1,), jnp.float32),
            jax.ShapeDtypeStruct((rows, width), jnp.bfloat16),
        ),
        in_specs=[vmem] * 5,
        out_specs=(pl.BlockSpec(memory_space=pltpu.SMEM), vmem),
        scratch_shapes=[
            pltpu.VMEM((1, total), jnp.float32),
            pltpu.VMEM((1, total), jnp.float32),
            pltpu.VMEM((rows, total), jnp.float32),
            pltpu.VMEM((rows, total), jnp.float32),
        ],
        compiler_params=params,
        cost_estimate=pl.CostEstimate(
            flops=6 * half * half * width, bytes_accessed=2 * total * width, transcendentals=3 * half * half
        ),
    )(near, far, *stats)
    return (loss[0], grad)


def solution(mesh):
    in_specs = (P(AXES, None), P(AXES))
    out_specs = (P(), P(AXES, None))
    devices = mesh.shape["row"] * mesh.shape["col"]

    def body(embeddings, group_ids):
        return on_device(devices, embeddings, group_ids)

    return jax.shard_map(body, mesh=mesh, in_specs=in_specs, out_specs=out_specs, check_vma=False)
```

time: 27.7 us -> 25.3 us (0.913)
  waiting for transfers between devices: 13.4 us -> 7.22 us
  starting transfers between devices: 9.27 us -> 12.3 us
  Pallas kernels: 2.49 us -> 3.88 us
  other arithmetic: 0.94 us -> 0.01 us
    ppermute x7 -> x9, waiting for transfers between devices: 13.4 us -> 7.22 us  [swap(): return lax.ppermute(held, AXES, [(i, i ^ mask) for i in range(devices)])]
    ppermute x7 -> x9, starting transfers between devices: 9.27 us -> 12.3 us  [swap(): return lax.ppermute(held, AXES, [(i, i ^ mask) for i in range(devices)])]
    pallas_call x1 -> x3, Pallas kernels: 2.49 us -> 3.88 us  [the longest x1 2.01 us: on_device(): pl.pallas_call(lambda *refs: loss_and_grad(width, rows, *refs), out_shape...]
    unnamed x1 -> x0, other arithmetic: 0.84 us -> none
    unnamed x9 -> x10, local copies, waits for them, and re-layouts: 0.7 us -> 0.9 us
  transfers between devices with their start and end apart: 7 -> 9, of which waited for: 5 -> 6; matrix products, arithmetic and copies ran while one was open for 0% -> 4% of each run, Pallas kernels for 0% -> 2%
where the time goes in v3:
time: 25.3 us; the launch traced here: 25 us
  starting transfers between devices  12.3 us (49%)
  waiting for transfers between devices  7.22 us (29%)
  Pallas kernels  3.88 us (15%)
  local copies, waits for them, and re-layouts  0.91 us (4%)
  between operations  0.68 us (3%)
    ppermute x9, starting transfers between devices, swap(): return lax.ppermute(held, AXES, [(i, i ^ mask) for i in range(devices)])  12.3 us
    ppermute x9, waiting for transfers between devices, swap(): return lax.ppermute(held, AXES, [(i, i ^ mask) for i in range(devices)])  7.22 us
    pallas_call x1, Pallas kernels, on_device(): pl.pallas_call(lambda *refs: loss_and_grad(width, rows, *refs), out_shape...  2.01 us
    pallas_call x1, Pallas kernels, on_device(): pl.pallas_call(pack, out_shape=jax.ShapeDtypeStruct((rows, width + LANES)...  1.39 us
    unnamed x10, local copies, waits for them, and re-layouts  0.9 us
  transfers between devices with their start and end apart: 9, of which 6 were waited for; matrix products, arithmetic and copies ran while one was open for 4% of the time, Pallas kernels for 2%

profile of v3, /device:TPU:0, one launch (start us, length us, event | category | flops | bytes accessed | tf_op | source)
XLA Modules:
  0.0 25.0 jit_solution(14649506045717097218)
XLA Ops:
  0.6 1.4 %shard_map.41 = bf16[16,1152]{1,0:T(8,128)(2,1)} custom-call(bf16[16,1024]{1,0:T(8,128)(2,1)} %rows_hbm.1, s32[1,16]{1,0:T(1,128)} %bitcast.2), custom_call_target="tpu_custom_call" | custom-call | tf_op jit(solution)/shard_map/pallas_call | solution.py:190
  2.0 0.0 copy-start
  2.0 3.6 %collective-permute-start = (bf16[16,1152]{1,0:T(8,128)(2,1)}, bf16[16,1152]{1,0:T(8,128)(2,1)S(1)}, u32[]{:S(2)}, u32[]{:S(2)}) collective-permute-start(bf16[16,1152]{1,0:T(8,128)(2,1)} %shard_map.41), channel_id=1, source_target_pairs={{0,17},{1,16},{2,19},{3,18},{4,21},{5,20},{6,23},{7,22},{8,25},{9,... | collective-permute-start | bytes 110600 | tf_op jit(solution)/shard_map/ppermute | solution.py:25
  5.6 0.8 %constant_dynamic-update-slice_fusion.8 = bf16[256,1152]{1,0:T(8,128)(2,1)S(1)} fusion(bf16[16,1152]{1,0:T(8,128)(2,1)} %shard_map.41), kind=kLoop, calls=%fused_computation.9 | loop fusion | bytes 73728
  6.4 1.4 %collective-permute-done = bf16[16,1152]{1,0:T(8,128)(2,1)S(1)} collective-permute-done((bf16[16,1152]{1,0:T(8,128)(2,1)}, bf16[16,1152]{1,0:T(8,128)(2,1)S(1)}, u32[]{:S(2)}, u32[]{:S(2)}) %collective-permute-start) | collective-permute-done | bytes 36896 | tf_op jit(solution)/shard_map/ppermute | solution.py:25
  7.8 0.0 copy-done
  7.8 1.9 %collective-permute-start.1 = (bf16[32,1152]{1,0:T(8,128)(2,1)S(1)}, bf16[32,1152]{1,0:T(8,128)(2,1)S(1)}, u32[]{:S(2)}, u32[]{:S(2)}) collective-permute-start(bf16[32,1152]{1,0:T(8,128)(2,1)S(1)} %pad_maximum_fusion), channel_id=1, source_target_pairs={{0,9},{1,8},{2,11},{3,10},{4,13},{5,12},{6,15},{7,14},{8,1},{9,0},... | collective-permute-start | bytes 221192 | tf_op jit(solution)/shard_map/ppermute | solution.py:25
  9.7 1.5 %collective-permute-start.2 = (bf16[32,1152]{1,0:T(8,128)(2,1)S(1)}, bf16[32,1152]{1,0:T(8,128)(2,1)S(1)}, u32[]{:S(2)}, u32[]{:S(2)}) collective-permute-start(bf16[32,1152]{1,0:T(8,128)(2,1)S(1)} %pad_maximum_fusion), channel_id=1, source_target_pairs={{0,3},{1,2},{2,1},{3,0},{4,7},{5,6},{6,5},{7,4},{8,11},{9,10},{10,... | collective-permute-start | bytes 221192 | tf_op jit(solution)/shard_map/ppermute | solution.py:25
  11.2 1.2 %collective-permute-start.3 = (bf16[32,1152]{1,0:T(8,128)(2,1)S(1)}, bf16[32,1152]{1,0:T(8,128)(2,1)S(1)}, u32[]{:S(2)}, u32[]{:S(2)}) collective-permute-start(bf16[32,1152]{1,0:T(8,128)(2,1)S(1)} %pad_maximum_fusion), channel_id=1, source_target_pairs={{0,5},{1,4},{2,7},{3,6},{4,1},{5,0},{6,3},{7,2},{8,13},{9,12},{10,... | collective-permute-start | bytes 221192 | tf_op jit(solution)/shard_map/ppermute | solution.py:25
  12.4 0.5 %collective-permute-start.4 = (bf16[32,1152]{1,0:T(8,128)(2,1)S(1)}, bf16[32,1152]{1,0:T(8,128)(2,1)S(1)}, u32[]{:S(2)}, u32[]{:S(2)}) collective-permute-start(bf16[32,1152]{1,0:T(8,128)(2,1)S(1)} %pad_maximum_fusion), channel_id=1, source_target_pairs={{0,7},{1,6},{2,5},{3,4},{4,3},{5,2},{6,1},{7,0},{8,15},{9,14},{10,... | collective-permute-start | bytes 221192 | tf_op jit(solution)/shard_map/ppermute | solution.py:25
  12.9 0.0 collective-permute-done.1
  12.9 1.3 %collective-permute-start.5 = (bf16[32,1152]{1,0:T(8,128)(2,1)S(1)}, bf16[32,1152]{1,0:T(8,128)(2,1)S(1)}, u32[]{:S(2)}, u32[]{:S(2)}) collective-permute-start(bf16[32,1152]{1,0:T(8,128)(2,1)S(1)} %collective-permute-done.1), channel_id=1, source_target_pairs={{0,3},{1,2},{2,1},{3,0},{4,7},{5,6},{6,5},{7,4},{8,11},{9,10},{10,... | collective-permute-start | bytes 221192 | tf_op jit(solution)/shard_map/ppermute | solution.py:25
  14.2 1.5 %collective-permute-start.6 = (bf16[32,1152]{1,0:T(8,128)(2,1)S(1)}, bf16[32,1152]{1,0:T(8,128)(2,1)S(1)}, u32[]{:S(2)}, u32[]{:S(2)}) collective-permute-start(bf16[32,1152]{1,0:T(8,128)(2,1)S(1)} %collective-permute-done.1), channel_id=1, source_target_pairs={{0,5},{1,4},{2,7},{3,6},{4,1},{5,0},{6,3},{7,2},{8,13},{9,12},{10,... | collective-permute-start | bytes 221192 | tf_op jit(solution)/shard_map/ppermute | solution.py:25
  15.7 0.0 collective-permute-done.2
  15.7 0.7 %collective-permute-start.7 = (bf16[32,1152]{1,0:T(8,128)(2,1)S(1)}, bf16[32,1152]{1,0:T(8,128)(2,1)S(1)}, u32[]{:S(2)}, u32[]{:S(2)}) collective-permute-start(bf16[32,1152]{1,0:T(8,128)(2,1)S(1)} %collective-permute-done.1), channel_id=1, source_target_pairs={{0,7},{1,6},{2,5},{3,4},{4,3},{5,2},{6,1},{7,0},{8,15},{9,14},{10,... | collective-permute-start | bytes 221192 | tf_op jit(solution)/shard_map/ppermute | solution.py:25
  16.4 0.0 collective-permute-done.3
  16.5 0.9 %collective-permute-done.4 = bf16[32,1152]{1,0:T(8,128)(2,1)S(1)} collective-permute-done((bf16[32,1152]{1,0:T(8,128)(2,1)S(1)}, bf16[32,1152]{1,0:T(8,128)(2,1)S(1)}, u32[]{:S(2)}, u32[]{:S(2)}) %collective-permute-start.4) | collective-permute-done | bytes 73760 | tf_op jit(solution)/shard_map/ppermute | solution.py:25
  17.3 0.6 %collective-permute-done.5 = bf16[32,1152]{1,0:T(8,128)(2,1)S(1)} collective-permute-done((bf16[32,1152]{1,0:T(8,128)(2,1)S(1)}, bf16[32,1152]{1,0:T(8,128)(2,1)S(1)}, u32[]{:S(2)}, u32[]{:S(2)}) %collective-permute-start.5) | collective-permute-done | bytes 73760 | tf_op jit(solution)/shard_map/ppermute | solution.py:25
  18.0 1.3 %collective-permute-done.6 = bf16[32,1152]{1,0:T(8,128)(2,1)S(1)} collective-permute-done((bf16[32,1152]{1,0:T(8,128)(2,1)S(1)}, bf16[32,1152]{1,0:T(8,128)(2,1)S(1)}, u32[]{:S(2)}, u32[]{:S(2)}) %collective-permute-start.6) | collective-permute-done | bytes 73760 | tf_op jit(solution)/shard_map/ppermute | solution.py:25
  19.3 1.7 %collective-permute-done.7 = bf16[32,1152]{1,0:T(8,128)(2,1)S(1)} collective-permute-done((bf16[32,1152]{1,0:T(8,128)(2,1)S(1)}, bf16[32,1152]{1,0:T(8,128)(2,1)S(1)}, u32[]{:S(2)}, u32[]{:S(2)}) %collective-permute-start.7) | collective-permute-done | bytes 73760 | tf_op jit(solution)/shard_map/ppermute | solution.py:25
  21.0 0.2 collective-permute-start.8
  21.2 0.5 %shard_map.42 = (f32[4,256]{1,0:T(4,128)S(1)}, f32[16,256]{1,0:T(8,128)S(1)}, f32[16,256]{1,0:T(8,128)S(1)}) custom-call(bf16[256,1152]{1,0:T(8,128)(2,1)S(1)} %constant_dynamic-update-slice_fusion.refs_0_), custom_call_target="tpu_custom_call" | custom-call | flops 134217728 | bytes 524288 | tf_op jit(solution)/shard_map/pallas_call | solution.py:204
  21.6 1.4 %collective-permute-done.8.refs_1_ = bf16[256,1152]{1,0:T(8,128)(2,1)S(1)} collective-permute-done((bf16[256,1152]{1,0:T(8,128)(2,1)S(1)}, bf16[256,1152]{1,0:T(8,128)(2,1)S(1)}, u32[]{:S(2)}, u32[]{:S(2)}) %collective-permute-start.8) | collective-permute-done | bytes 589856 | tf_op jit(solution)/shard_map/ppermute | solution.py:25
  23.0 2.0 %shard_map.43 = (f32[1]{0:T(128)}, bf16[16,1024]{1,0:T(8,128)(2,1)}) custom-call(bf16[256,1152]{1,0:T(8,128)(2,1)S(1)} %constant_dynamic-update-slice_fusion.refs_0_, bf16[256,1152]{1,0:T(8,128)(2,1)S(1)} %collective-permute-done.8.refs_1_, f32[4,256]{1,0:T(4,128)S(1)} %get-tuple-element.7.refs_2_, f32[16,256]{1,0:T(8,128)S(1)} %get-tuple-element.8.refs_3_, ...), custom_call_target="tpu_custom_call" | custom-call | flops 402653184 | bytes 1048576 | tf_op jit(solution)/shard_map/pallas_call | solution.py:218
  (9 shorter events, 0.1 us)
Async XLA Ops:
  2.0 5.8 %copy-start = (bf16[16,1152]{1,0:T(8,128)(2,1)S(1)}, bf16[16,1152]{1,0:T(8,128)(2,1)}, u32[]{:S(2)}) copy-start(bf16[16,1152]{1,0:T(8,128)(2,1)} %shard_map.41) | copy-start | bytes 110596
  2.0 5.7 %collective-permute-start = (bf16[16,1152]{1,0:T(8,128)(2,1)}, bf16[16,1152]{1,0:T(8,128)(2,1)S(1)}, u32[]{:S(2)}, u32[]{:S(2)}) collective-permute-start(bf16[16,1152]{1,0:T(8,128)(2,1)} %shard_map.41), channel_id=1, source_target_pairs={{0,17},{1,16},{2,19},{3,18},{4,21},{5,20},{6,23},{7,22},{8,25},{9,... | collective-permute-start | bytes 110600 | tf_op jit(solution)/shard_map/ppermute | solution.py:25
  7.8 5.1 %collective-permute-start.1 = (bf16[32,1152]{1,0:T(8,128)(2,1)S(1)}, bf16[32,1152]{1,0:T(8,128)(2,1)S(1)}, u32[]{:S(2)}, u32[]{:S(2)}) collective-permute-start(bf16[32,1152]{1,0:T(8,128)(2,1)S(1)} %pad_maximum_fusion), channel_id=1, source_target_pairs={{0,9},{1,8},{2,11},{3,10},{4,13},{5,12},{6,15},{7,14},{8,1},{9,0},... | collective-permute-start | bytes 221192 | tf_op jit(solution)/shard_map/ppermute | solution.py:25
  9.7 6.0 %collective-permute-start.2 = (bf16[32,1152]{1,0:T(8,128)(2,1)S(1)}, bf16[32,1152]{1,0:T(8,128)(2,1)S(1)}, u32[]{:S(2)}, u32[]{:S(2)}) collective-permute-start(bf16[32,1152]{1,0:T(8,128)(2,1)S(1)} %pad_maximum_fusion), channel_id=1, source_target_pairs={{0,3},{1,2},{2,1},{3,0},{4,7},{5,6},{6,5},{7,4},{8,11},{9,10},{10,... | collective-permute-start | bytes 221192 | tf_op jit(solution)/shard_map/ppermute | solution.py:25
  11.2 5.3 %collective-permute-start.3 = (bf16[32,1152]{1,0:T(8,128)(2,1)S(1)}, bf16[32,1152]{1,0:T(8,128)(2,1)S(1)}, u32[]{:S(2)}, u32[]{:S(2)}) collective-permute-start(bf16[32,1152]{1,0:T(8,128)(2,1)S(1)} %pad_maximum_fusion), channel_id=1, source_target_pairs={{0,5},{1,4},{2,7},{3,6},{4,1},{5,0},{6,3},{7,2},{8,13},{9,12},{10,... | collective-permute-start | bytes 221192 | tf_op jit(solution)/shard_map/ppermute | solution.py:25
  12.4 4.9 %collective-permute-start.4 = (bf16[32,1152]{1,0:T(8,128)(2,1)S(1)}, bf16[32,1152]{1,0:T(8,128)(2,1)S(1)}, u32[]{:S(2)}, u32[]{:S(2)}) collective-permute-start(bf16[32,1152]{1,0:T(8,128)(2,1)S(1)} %pad_maximum_fusion), channel_id=1, source_target_pairs={{0,7},{1,6},{2,5},{3,4},{4,3},{5,2},{6,1},{7,0},{8,15},{9,14},{10,... | collective-permute-start | bytes 221192 | tf_op jit(solution)/shard_map/ppermute | solution.py:25
  12.9 5.1 %collective-permute-start.5 = (bf16[32,1152]{1,0:T(8,128)(2,1)S(1)}, bf16[32,1152]{1,0:T(8,128)(2,1)S(1)}, u32[]{:S(2)}, u32[]{:S(2)}) collective-permute-start(bf16[32,1152]{1,0:T(8,128)(2,1)S(1)} %collective-permute-done.1), channel_id=1, source_target_pairs={{0,3},{1,2},{2,1},{3,0},{4,7},{5,6},{6,5},{7,4},{8,11},{9,10},{10,... | collective-permute-start | bytes 221192 | tf_op jit(solution)/shard_map/ppermute | solution.py:25
  14.2 5.1 %collective-permute-start.6 = (bf16[32,1152]{1,0:T(8,128)(2,1)S(1)}, bf16[32,1152]{1,0:T(8,128)(2,1)S(1)}, u32[]{:S(2)}, u32[]{:S(2)}) collective-permute-start(bf16[32,1152]{1,0:T(8,128)(2,1)S(1)} %collective-permute-done.1), channel_id=1, source_target_pairs={{0,5},{1,4},{2,7},{3,6},{4,1},{5,0},{6,3},{7,2},{8,13},{9,12},{10,... | collective-permute-start | bytes 221192 | tf_op jit(solution)/shard_map/ppermute | solution.py:25
  15.7 5.2 %collective-permute-start.7 = (bf16[32,1152]{1,0:T(8,128)(2,1)S(1)}, bf16[32,1152]{1,0:T(8,128)(2,1)S(1)}, u32[]{:S(2)}, u32[]{:S(2)}) collective-permute-start(bf16[32,1152]{1,0:T(8,128)(2,1)S(1)} %collective-permute-done.1), channel_id=1, source_target_pairs={{0,7},{1,6},{2,5},{3,4},{4,3},{5,2},{6,1},{7,0},{8,15},{9,14},{10,... | collective-permute-start | bytes 221192 | tf_op jit(solution)/shard_map/ppermute | solution.py:25
  21.0 2.1 %collective-permute-start.8 = (bf16[256,1152]{1,0:T(8,128)(2,1)S(1)}, bf16[256,1152]{1,0:T(8,128)(2,1)S(1)}, u32[]{:S(2)}, u32[]{:S(2)}) collective-permute-start(bf16[256,1152]{1,0:T(8,128)(2,1)S(1)} %constant_dynamic-update-slice_fusion.refs_0_), channel_id=1, source_target_pairs={{0,1},{1,0},{2,3},{3,2},{4,5},{5,4},{6,7},{7,6},{8,9},{9,8},{10,11... | collective-permute-start | bytes 1769480 | tf_op jit(solution)/shard_map/ppermute | solution.py:25

commit v4 on v3

--- a/solution.py
+++ b/solution.py
@@ -29,11 +29,12 @@
     far, near = bit_groups(devices.bit_length() - 1)
     for b in far[:-1]:
         held = jnp.concatenate([held, swap(devices, 1 << b | 1, held)], axis=0)
-    late = swap(devices, 1 << far[-1] | 1, held)
-    parts = [held, late]
-    for part in (held, late):
-        parts += [swap(devices, m | 1, part) for m in masks_of(near)]
-    return jnp.concatenate(parts, axis=0)
+    last = 1 << far[-1] | 1
+    late = swap(devices, last, held)
+    across = swap(devices, 7, held)
+    both = jnp.concatenate([held, late], axis=0)
+    parts = [both] + [swap(devices, m, both) for m in (3, 5)]
+    return jnp.concatenate(parts + [across, swap(devices, last, across)], axis=0)
 
 
 def pack(rows_hbm, ids_hbm, out_ref, rows_ref, ids_ref, sems):
@@ -189,7 +190,7 @@
     params = pltpu.CompilerParams(vmem_limit_bytes=(8 << 20) + 8 * total * width)
     held = pl.pallas_call(
         pack,
-        out_shape=jax.ShapeDtypeStruct((rows, width + LANES), jnp.bfloat16),
+        out_shape=pltpu.VMEM((rows, width + LANES), jnp.bfloat16),
         in_specs=[pl.BlockSpec(memory_space=pltpu.HBM)] * 2,
         out_specs=vmem,
         scratch_shapes=[

time: 25.3 us -> 23.2 us (0.917)
  waiting for transfers between devices: 7.22 us -> 5.78 us
  local copies, waits for them, and re-layouts: 0.91 us -> 0.09 us
  starting transfers between devices: 12.3 us -> 13 us
  Pallas kernels: 3.88 us -> 3.3 us
    ppermute x9 -> x7, waiting for transfers between devices: 7.22 us -> 5.78 us  [swap(): return lax.ppermute(held, AXES, [(i, i ^ mask) for i in range(devices)])]
    unnamed x10 -> x6, local copies, waits for them, and re-layouts: 0.9 us -> 0.08 us
    ppermute x9 -> x7, starting transfers between devices: 12.3 us -> 13 us  [swap(): return lax.ppermute(held, AXES, [(i, i ^ mask) for i in range(devices)])]
    pallas_call x1, Pallas kernels: 1.39 us -> 0.79 us  [on_device(): pl.pallas_call(pack, out_shape=pltpu.VMEM((rows, width + LANES), jnp.bflo...]
  transfers between devices with their start and end apart: 9 -> 7, of which waited for: 6 -> 5; matrix products, arithmetic and copies ran while one was open for 4% -> 0% of each run, Pallas kernels for 2% -> 2%
where the time goes in v4:
time: 23.2 us; the launch traced here: 22.9 us
  starting transfers between devices  13 us (56%)
  waiting for transfers between devices  5.78 us (25%)
  Pallas kernels  3.3 us (14%)
  between operations  0.66 us (3%)
    ppermute x7, starting transfers between devices, swap(): return lax.ppermute(held, AXES, [(i, i ^ mask) for i in range(devices)])  13 us
    ppermute x7, waiting for transfers between devices, swap(): return lax.ppermute(held, AXES, [(i, i ^ mask) for i in range(devices)])  5.78 us
    pallas_call x1, Pallas kernels, on_device(): pl.pallas_call(lambda *refs: loss_and_grad(width, rows, *refs), out_shape...  2.03 us
    pallas_call x1, Pallas kernels, on_device(): pl.pallas_call(pack, out_shape=pltpu.VMEM((rows, width + LANES), jnp.bflo...  0.79 us
    pallas_call x1, Pallas kernels, on_device(): pl.pallas_call(lambda *refs: near_stats(width, rows, *refs), out_shape=(j...  0.48 us
  transfers between devices with their start and end apart: 7, of which 5 were waited for; matrix products, arithmetic and copies ran while one was open for 0% of the time, Pallas kernels for 2%

profile of v4, /device:TPU:0, one launch (start us, length us, event | category | flops | bytes accessed | tf_op | source)
XLA Modules:
  0.0 22.9 jit_solution(10376718522890753640)
XLA Ops:
  0.6 0.8 %shard_map.41 = bf16[16,1152]{1,0:T(8,128)(2,1)S(1)} custom-call(bf16[16,1024]{1,0:T(8,128)(2,1)} %rows_hbm.1, s32[1,16]{1,0:T(1,128)} %bitcast.2), custom_call_target="tpu_custom_call" | custom-call | tf_op jit(solution)/shard_map/pallas_call | solution.py:191
  1.4 3.6 %collective-permute-start = (bf16[16,1152]{1,0:T(8,128)(2,1)S(1)}, bf16[16,1152]{1,0:T(8,128)(2,1)S(1)}, u32[]{:S(2)}, u32[]{:S(2)}) collective-permute-start(bf16[16,1152]{1,0:T(8,128)(2,1)S(1)} %shard_map.41), channel_id=1, source_target_pairs={{0,17},{1,16},{2,19},{3,18},{4,21},{5,20},{6,23},{7,22},{8,25},{9,... | collective-permute-start | bytes 110600 | tf_op jit(solution)/shard_map/ppermute | solution.py:25
  5.0 1.9 %collective-permute-done = bf16[16,1152]{1,0:T(8,128)(2,1)S(1)} collective-permute-done((bf16[16,1152]{1,0:T(8,128)(2,1)S(1)}, bf16[16,1152]{1,0:T(8,128)(2,1)S(1)}, u32[]{:S(2)}, u32[]{:S(2)}) %collective-permute-start) | collective-permute-done | bytes 36896 | tf_op jit(solution)/shard_map/ppermute | solution.py:25
  6.9 1.8 %collective-permute-start.1 = (bf16[32,1152]{1,0:T(8,128)(2,1)S(1)}, bf16[32,1152]{1,0:T(8,128)(2,1)S(1)}, u32[]{:S(2)}, u32[]{:S(2)}) collective-permute-start(bf16[32,1152]{1,0:T(8,128)(2,1)S(1)} %pad_maximum_fusion.1), channel_id=1, source_target_pairs={{0,9},{1,8},{2,11},{3,10},{4,13},{5,12},{6,15},{7,14},{8,1},{9,0},... | collective-permute-start | bytes 221192 | tf_op jit(solution)/shard_map/ppermute | solution.py:25
  8.7 2.4 %collective-permute-start.4 = (bf16[32,1152]{1,0:T(8,128)(2,1)S(1)}, bf16[32,1152]{1,0:T(8,128)(2,1)S(1)}, u32[]{:S(2)}, u32[]{:S(2)}) collective-permute-start(bf16[32,1152]{1,0:T(8,128)(2,1)S(1)} %pad_maximum_fusion.1), channel_id=1, source_target_pairs={{0,7},{1,6},{2,5},{3,4},{4,3},{5,2},{6,1},{7,0},{8,15},{9,14},{10,... | collective-permute-start | bytes 221192 | tf_op jit(solution)/shard_map/ppermute | solution.py:25
  11.2 0.0 collective-permute-done.1
  11.2 1.8 %collective-permute-start.2 = (bf16[64,1152]{1,0:T(8,128)(2,1)S(1)}, bf16[64,1152]{1,0:T(8,128)(2,1)S(1)}, u32[]{:S(2)}, u32[]{:S(2)}) collective-permute-start(bf16[64,1152]{1,0:T(8,128)(2,1)S(1)} %pad_maximum_fusion), channel_id=1, source_target_pairs={{0,3},{1,2},{2,1},{3,0},{4,7},{5,6},{6,5},{7,4},{8,11},{9,10},{10,... | collective-permute-start | bytes 442376 | tf_op jit(solution)/shard_map/ppermute | solution.py:25
  13.0 1.5 %collective-permute-start.3 = (bf16[64,1152]{1,0:T(8,128)(2,1)S(1)}, bf16[64,1152]{1,0:T(8,128)(2,1)S(1)}, u32[]{:S(2)}, u32[]{:S(2)}) collective-permute-start(bf16[64,1152]{1,0:T(8,128)(2,1)S(1)} %pad_maximum_fusion), channel_id=1, source_target_pairs={{0,5},{1,4},{2,7},{3,6},{4,1},{5,0},{6,3},{7,2},{8,13},{9,12},{10,... | collective-permute-start | bytes 442376 | tf_op jit(solution)/shard_map/ppermute | solution.py:25
  14.5 0.0 collective-permute-done.4
  14.5 1.6 %collective-permute-start.5 = (bf16[32,1152]{1,0:T(8,128)(2,1)S(1)}, bf16[32,1152]{1,0:T(8,128)(2,1)S(1)}, u32[]{:S(2)}, u32[]{:S(2)}) collective-permute-start(bf16[32,1152]{1,0:T(8,128)(2,1)S(1)} %collective-permute-done.4), channel_id=1, source_target_pairs={{0,9},{1,8},{2,11},{3,10},{4,13},{5,12},{6,15},{7,14},{8,1},{9,0},... | collective-permute-start | bytes 221192 | tf_op jit(solution)/shard_map/ppermute | solution.py:25
  16.1 0.8 %collective-permute-done.2 = bf16[64,1152]{1,0:T(8,128)(2,1)S(1)} collective-permute-done((bf16[64,1152]{1,0:T(8,128)(2,1)S(1)}, bf16[64,1152]{1,0:T(8,128)(2,1)S(1)}, u32[]{:S(2)}, u32[]{:S(2)}) %collective-permute-start.2) | collective-permute-done | bytes 147488 | tf_op jit(solution)/shard_map/ppermute | solution.py:25
  16.9 1.6 %collective-permute-done.3 = bf16[64,1152]{1,0:T(8,128)(2,1)S(1)} collective-permute-done((bf16[64,1152]{1,0:T(8,128)(2,1)S(1)}, bf16[64,1152]{1,0:T(8,128)(2,1)S(1)}, u32[]{:S(2)}, u32[]{:S(2)}) %collective-permute-start.3) | collective-permute-done | bytes 147488 | tf_op jit(solution)/shard_map/ppermute | solution.py:25
  18.6 0.2 collective-permute-done.5
  18.8 0.3 %collective-permute-start.6 = (bf16[256,1152]{1,0:T(8,128)(2,1)S(1)}, bf16[256,1152]{1,0:T(8,128)(2,1)S(1)}, u32[]{:S(2)}, u32[]{:S(2)}) collective-permute-start(bf16[256,1152]{1,0:T(8,128)(2,1)S(1)} %constant_dynamic-update-slice_fusion.refs_0_), channel_id=1, source_target_pairs={{0,1},{1,0},{2,3},{3,2},{4,5},{5,4},{6,7},{7,6},{8,9},{9,8},{10,11... | collective-permute-start | bytes 1769480 | tf_op jit(solution)/shard_map/ppermute | solution.py:25
  19.1 0.5 %shard_map.42 = (f32[4,256]{1,0:T(4,128)S(1)}, f32[16,256]{1,0:T(8,128)S(1)}, f32[16,256]{1,0:T(8,128)S(1)}) custom-call(bf16[256,1152]{1,0:T(8,128)(2,1)S(1)} %constant_dynamic-update-slice_fusion.refs_0_), custom_call_target="tpu_custom_call" | custom-call | flops 134217728 | bytes 524288 | tf_op jit(solution)/shard_map/pallas_call | solution.py:205
  19.6 1.3 %collective-permute-done.6.refs_1_ = bf16[256,1152]{1,0:T(8,128)(2,1)S(1)} collective-permute-done((bf16[256,1152]{1,0:T(8,128)(2,1)S(1)}, bf16[256,1152]{1,0:T(8,128)(2,1)S(1)}, u32[]{:S(2)}, u32[]{:S(2)}) %collective-permute-start.6) | collective-permute-done | bytes 589856 | tf_op jit(solution)/shard_map/ppermute | solution.py:25
  20.9 2.0 %shard_map.43 = (f32[1]{0:T(128)}, bf16[16,1024]{1,0:T(8,128)(2,1)}) custom-call(bf16[256,1152]{1,0:T(8,128)(2,1)S(1)} %constant_dynamic-update-slice_fusion.refs_0_, bf16[256,1152]{1,0:T(8,128)(2,1)S(1)} %collective-permute-done.6.refs_1_, f32[4,256]{1,0:T(4,128)S(1)} %get-tuple-element.7.refs_2_, f32[16,256]{1,0:T(8,128)S(1)} %get-tuple-element.8.refs_3_, ...), custom_call_target="tpu_custom_call" | custom-call | flops 402653184 | bytes 1048576 | tf_op jit(solution)/shard_map/pallas_call | solution.py:219
  (9 shorter events, 0.1 us)
Async XLA Ops:
  1.4 5.4 %collective-permute-start = (bf16[16,1152]{1,0:T(8,128)(2,1)S(1)}, bf16[16,1152]{1,0:T(8,128)(2,1)S(1)}, u32[]{:S(2)}, u32[]{:S(2)}) collective-permute-start(bf16[16,1152]{1,0:T(8,128)(2,1)S(1)} %shard_map.41), channel_id=1, source_target_pairs={{0,17},{1,16},{2,19},{3,18},{4,21},{5,20},{6,23},{7,22},{8,25},{9,... | collective-permute-start | bytes 110600 | tf_op jit(solution)/shard_map/ppermute | solution.py:25
  6.9 4.3 %collective-permute-start.1 = (bf16[32,1152]{1,0:T(8,128)(2,1)S(1)}, bf16[32,1152]{1,0:T(8,128)(2,1)S(1)}, u32[]{:S(2)}, u32[]{:S(2)}) collective-permute-start(bf16[32,1152]{1,0:T(8,128)(2,1)S(1)} %pad_maximum_fusion.1), channel_id=1, source_target_pairs={{0,9},{1,8},{2,11},{3,10},{4,13},{5,12},{6,15},{7,14},{8,1},{9,0},... | collective-permute-start | bytes 221192 | tf_op jit(solution)/shard_map/ppermute | solution.py:25
  8.7 5.8 %collective-permute-start.4 = (bf16[32,1152]{1,0:T(8,128)(2,1)S(1)}, bf16[32,1152]{1,0:T(8,128)(2,1)S(1)}, u32[]{:S(2)}, u32[]{:S(2)}) collective-permute-start(bf16[32,1152]{1,0:T(8,128)(2,1)S(1)} %pad_maximum_fusion.1), channel_id=1, source_target_pairs={{0,7},{1,6},{2,5},{3,4},{4,3},{5,2},{6,1},{7,0},{8,15},{9,14},{10,... | collective-permute-start | bytes 221192 | tf_op jit(solution)/shard_map/ppermute | solution.py:25
  11.2 5.7 %collective-permute-start.2 = (bf16[64,1152]{1,0:T(8,128)(2,1)S(1)}, bf16[64,1152]{1,0:T(8,128)(2,1)S(1)}, u32[]{:S(2)}, u32[]{:S(2)}) collective-permute-start(bf16[64,1152]{1,0:T(8,128)(2,1)S(1)} %pad_maximum_fusion), channel_id=1, source_target_pairs={{0,3},{1,2},{2,1},{3,0},{4,7},{5,6},{6,5},{7,4},{8,11},{9,10},{10,... | collective-permute-start | bytes 442376 | tf_op jit(solution)/shard_map/ppermute | solution.py:25
  13.0 5.6 %collective-permute-start.3 = (bf16[64,1152]{1,0:T(8,128)(2,1)S(1)}, bf16[64,1152]{1,0:T(8,128)(2,1)S(1)}, u32[]{:S(2)}, u32[]{:S(2)}) collective-permute-start(bf16[64,1152]{1,0:T(8,128)(2,1)S(1)} %pad_maximum_fusion), channel_id=1, source_target_pairs={{0,5},{1,4},{2,7},{3,6},{4,1},{5,0},{6,3},{7,2},{8,13},{9,12},{10,... | collective-permute-start | bytes 442376 | tf_op jit(solution)/shard_map/ppermute | solution.py:25
  14.5 4.3 %collective-permute-start.5 = (bf16[32,1152]{1,0:T(8,128)(2,1)S(1)}, bf16[32,1152]{1,0:T(8,128)(2,1)S(1)}, u32[]{:S(2)}, u32[]{:S(2)}) collective-permute-start(bf16[32,1152]{1,0:T(8,128)(2,1)S(1)} %collective-permute-done.4), channel_id=1, source_target_pairs={{0,9},{1,8},{2,11},{3,10},{4,13},{5,12},{6,15},{7,14},{8,1},{9,0},... | collective-permute-start | bytes 221192 | tf_op jit(solution)/shard_map/ppermute | solution.py:25
  18.8 2.1 %collective-permute-start.6 = (bf16[256,1152]{1,0:T(8,128)(2,1)S(1)}, bf16[256,1152]{1,0:T(8,128)(2,1)S(1)}, u32[]{:S(2)}, u32[]{:S(2)}) collective-permute-start(bf16[256,1152]{1,0:T(8,128)(2,1)S(1)} %constant_dynamic-update-slice_fusion.refs_0_), channel_id=1, source_target_pairs={{0,1},{1,0},{2,3},{3,2},{4,5},{5,4},{6,7},{7,6},{8,9},{9,8},{10,11... | collective-permute-start | bytes 1769480 | tf_op jit(solution)/shard_map/ppermute | solution.py:25

commit v5 on v4

v5 whole, which is shorter than its diff:
```python
import jax
import jax.numpy as jnp
from jax import lax
from jax.experimental import pallas as pl
from jax.experimental.pallas import tpu as pltpu
from jax.sharding import PartitionSpec as P

AXES = ("row", "col")
LANES = 128
RADIX = 256


def bit_groups(bits):
    return [b for b in reversed(range(bits)) if b >= 3], [b for b in (1, 2) if b < bits]


def masks_of(group):
    masks = [0]
    for b in group:
        masks += [m | (1 << b) for m in masks]
    return masks[1:]


def swap(devices, mask, held):
    return lax.ppermute(held, AXES, [(i, i ^ mask) for i in range(devices)])


def gather_rows(devices, held):
    far, near = bit_groups(devices.bit_length() - 1)
    for b in far[:-1]:
        held = jnp.concatenate([held, swap(devices, 1 << b | 1, held)], axis=0)
    last = 1 << far[-1] | 1
    first, second = (1 << b | 1 for b in near)
    beyond = swap(devices, last, held)
    across = swap(devices, first | second, held)
    held = jnp.concatenate([held, beyond], axis=0)
    one = jnp.concatenate([held, swap(devices, first, held)], axis=0)
    two = swap(devices, second, held)
    two = jnp.concatenate([two, across, swap(devices, last, across)], axis=0)
    other = swap(devices, 1, one)
    return jnp.concatenate([one, other, two], axis=0), swap(devices, 1, two)


def pack(rows_hbm, ids_hbm, out_ref, rows_ref, ids_ref, sems):
    rows, width = rows_ref.shape
    copies = [
        pltpu.make_async_copy(ids_hbm, ids_ref, sems.at[0]),
        pltpu.make_async_copy(rows_hbm, rows_ref, sems.at[1]),
    ]
    for copy in copies:
        copy.start()
    copies[0].wait()
    down = lax.broadcasted_iota(jnp.int32, (rows, rows), 0)
    across = lax.broadcasted_iota(jnp.int32, (rows, rows), 1)
    wide = jnp.broadcast_to(ids_ref[...], (rows, rows))
    ids = jnp.sum(jnp.where(down == across, wide, 0), axis=1, keepdims=True)
    lane = lax.broadcasted_iota(jnp.int32, (rows, LANES), 1)
    low, high = ids & (RADIX - 1), ids >> 8
    coded = jnp.where(lane == 0, low, jnp.where(lane == 1, high, 0))
    out_ref[:, width:] = coded.astype(jnp.float32).astype(jnp.bfloat16)
    copies[1].wait()
    out_ref[:, :width] = rows_ref[...]


def dot_nt(a, b):
    return lax.dot_general(a, b, (((1,), (1,)), ((), ())), preferred_element_type=jnp.float32)


def digits(rows):
    lane = lax.broadcasted_iota(jnp.int32, (rows, LANES), 1)
    return jnp.where(lane == 0, 1.0, jnp.where(lane == 1, float(RADIX), 0.0)).astype(jnp.bfloat16)


def span(rows):
    return rows if rows <= 384 else 256


def block_stats(width, rows_ref, cols_ref, start, own, keep, product=None):
    scale = 1.0 / jnp.sqrt(jnp.float32(width))
    across, down = span(cols_ref.shape[0]), span(rows_ref.shape[0])
    cols = cols_ref[pl.ds(start, across), :width]
    col_ids = dot_nt(digits(16), cols_ref[pl.ds(start, across), width:])[:1]
    parts = []
    for first in range(0, rows_ref.shape[0], down):
        s = dot_nt(rows_ref[first : first + down, :width], cols) if product is None else product
        s = s * scale
        row_ids = dot_nt(rows_ref[first : first + down, width:], digits(LANES))
        positive = jnp.concatenate([row_ids] * (across // LANES), axis=1) == col_ids
        masked = s
        if rows_ref is cols_ref:
            row_pos = first + lax.broadcasted_iota(jnp.int32, (down, across), 0)
            selfs = row_pos == start + lax.broadcasted_iota(jnp.int32, (down, across), 1)
            positive = jnp.logical_and(positive, jnp.logical_not(selfs))
            masked = jnp.where(selfs, jnp.float32(-1e30), s)
        if first == 0:
            keep(masked[:own], positive[:own])
        top = jnp.max(masked, axis=0, keepdims=True)
        add = jnp.sum(jnp.exp(masked - top), axis=0, keepdims=True)
        possum = jnp.sum(jnp.where(positive, s, 0.0), axis=0, keepdims=True)
        count = jnp.sum(jnp.where(positive, 1.0, 0.0), axis=0, keepdims=True)
        parts.append((top, add, possum, count))
    return merge(parts)


def merge(parts):
    peak = parts[0][0]
    for p in parts[1:]:
        peak = jnp.maximum(peak, p[0])
    added = sum(p[1] * jnp.exp(p[0] - peak) for p in parts)
    return peak, added, sum(p[2] for p in parts), sum(p[3] for p in parts)


def over_blocks(rows, body, carry):
    block = span(rows)
    if rows == block:
        return body(0, carry)
    return lax.fori_loop(
        0, rows // block, lambda k, v: body(pl.multiple_of(k * block, block), v), carry
    )


def early_stats(width, own, early_ref, stats_ref, scores_ref, positive_ref):
    early = early_ref.shape[0]

    def body(start, carry):
        at = pl.ds(start, span(early))

        def keep(scores, positive):
            scores_ref[:, at] = scores
            positive_ref[:, at] = jnp.where(positive, 1.0, 0.0)

        stats = block_stats(width, early_ref, early_ref, start, own, keep)
        for k, value in enumerate(stats):
            stats_ref[k : k + 1, at] = value
        return carry

    over_blocks(early, body, 0)


def loss_and_grad(
    width, own, early_ref, late_ref, stats_ref, early_scores_ref, early_positive_ref,
    loss_hbm, grad_hbm, lse_ref, inv_ref, scores_ref, positive_ref, loss_ref, grad_ref, sems,
):
    early, late = early_ref.shape[0], late_ref.shape[0]
    total = early + late
    scale = 1.0 / jnp.sqrt(jnp.float32(width))
    scores_ref[:, :early] = early_scores_ref[...]
    positive_ref[:, :early] = early_positive_ref[...]

    def finish(at, stats, loss):
        peak, added, possum, count = stats
        inverse = 1.0 / count
        lse = peak + jnp.log(added)
        lse_ref[:, at] = lse
        inv_ref[:, at] = inverse
        return loss + jnp.sum(lse - possum * inverse)

    def early_columns(start, loss):
        at = pl.ds(start, span(early))
        had = tuple(stats_ref[k : k + 1, at] for k in range(4))
        turned = None if product is None else product.T
        more = block_stats(width, late_ref, early_ref, start, own, lambda *_: None, turned)
        return finish(at, merge([had, more]), loss)

    def late_columns(start, loss):
        at = pl.ds(early + start, span(late))

        def keep(scores, positive):
            scores_ref[:, at] = scores
            positive_ref[:, at] = jnp.where(positive, 1.0, 0.0)

        first = block_stats(width, early_ref, late_ref, start, own, keep, product)
        second = block_stats(width, late_ref, late_ref, start, own, lambda *_: None)
        return finish(at, merge([first, second]), loss)

    product = None
    if span(early) == early and span(late) == late:
        product = dot_nt(early_ref[:, :width], late_ref[:, :width])
    loss = over_blocks(late, late_columns, jnp.float32(0.0))
    loss = over_blocks(early, early_columns, loss)
    loss_ref[...] = jnp.full((1, 1), loss / total)
    copies = [pltpu.make_async_copy(loss_ref, loss_hbm, sems.at[0])]
    copies[0].start()

    masked = scores_ref[...]
    positive = positive_ref[...]
    peak = jnp.max(masked, axis=1, keepdims=True)
    lse = peak + jnp.log(jnp.sum(jnp.exp(masked - peak), axis=1, keepdims=True))
    inverse = 1.0 / jnp.sum(positive, axis=1, keepdims=True)
    weight = (jnp.exp(masked - lse) - positive * inverse) / total
    mirrored = (jnp.exp(masked - lse_ref[...]) - positive * inv_ref[...]) / total
    both = jnp.concatenate([weight, mirrored], axis=0).astype(jnp.bfloat16)
    parts = 2
    for k in range(parts):
        at = pl.ds(k * width // parts, width // parts)
        out = jnp.dot(both[:, :early], early_ref[:, at], preferred_element_type=jnp.float32)
        out += jnp.dot(both[:, early:], late_ref[:, at], preferred_element_type=jnp.float32)
        grad_ref[:, at] = (scale * (out[:own] + out[own:])).astype(jnp.bfloat16)
        copies.append(
            pltpu.make_async_copy(grad_ref.at[:, at], grad_hbm.at[:, at], sems.at[1 + k])
        )
        copies[-1].start()
    for copy in copies:
        copy.wait()


def on_device(devices, embeddings, group_ids):
    rows, width = embeddings.shape
    total = rows * devices
    vmem = pl.BlockSpec(memory_space=pltpu.VMEM)
    params = pltpu.CompilerParams(vmem_limit_bytes=(8 << 20) + 8 * total * width)
    held = pl.pallas_call(
        pack,
        out_shape=pltpu.VMEM((rows, width + LANES), jnp.bfloat16),
        in_specs=[pl.BlockSpec(memory_space=pltpu.HBM)] * 2,
        out_specs=vmem,
        scratch_shapes=[
            pltpu.VMEM((rows, width), jnp.bfloat16),
            pltpu.VMEM((1, rows), jnp.int32),
            pltpu.SemaphoreType.DMA((2,)),
        ],
        compiler_params=pltpu.CompilerParams(vmem_limit_bytes=60 << 20),
    )(embeddings, group_ids[None, :])
    early_rows, late_rows = gather_rows(devices, held)
    early, late = early_rows.shape[0], late_rows.shape[0]
    stats = pl.pallas_call(
        lambda *refs: early_stats(width, rows, *refs),
        out_shape=(
            jax.ShapeDtypeStruct((4, early), jnp.float32),
            jax.ShapeDtypeStruct((rows, early), jnp.float32),
            jax.ShapeDtypeStruct((rows, early), jnp.float32),
        ),
        in_specs=[vmem],
        out_specs=(vmem, vmem, vmem),
        compiler_params=params,
        cost_estimate=pl.CostEstimate(
            flops=2 * early * early * width, bytes_accessed=2 * early * width, transcendentals=early * early
        ),
    )(early_rows)
    loss, grad = pl.pallas_call(
        lambda *refs: loss_and_grad(width, rows, *refs),
        out_shape=(
            jax.ShapeDtypeStruct((1, 1), jnp.float32),
            jax.ShapeDtypeStruct((rows, width), jnp.bfloat16),
        ),
        in_specs=[vmem] * 5,
        out_specs=[pl.BlockSpec(memory_space=pltpu.HBM)] * 2,
        scratch_shapes=[
            pltpu.VMEM((1, total), jnp.float32),
            pltpu.VMEM((1, total), jnp.float32),
            pltpu.VMEM((rows, total), jnp.float32),
            pltpu.VMEM((rows, total), jnp.float32),
            pltpu.VMEM((1, 1), jnp.float32),
            pltpu.VMEM((rows, width), jnp.bfloat16),
            pltpu.SemaphoreType.DMA((3,)),
        ],
        compiler_params=params,
        cost_estimate=pl.CostEstimate(
            flops=4 * total * late * width, bytes_accessed=2 * total * width, transcendentals=2 * total * late
        ),
    )(early_rows, late_rows, *stats)
    return (loss[0, 0], grad)


def solution(mesh):
    in_specs = (P(AXES, None), P(AXES))
    out_specs = (P(), P(AXES, None))
    devices = mesh.shape["row"] * mesh.shape["col"]

    def body(embeddings, group_ids):
        return on_device(devices, embeddings, group_ids)

    return jax.shard_map(body, mesh=mesh, in_specs=in_specs, out_specs=out_specs, check_vma=False)
```

time: 23.2 us -> 22.4 us (0.966)
  waiting for transfers between devices: 5.78 us -> 4.28 us
  starting transfers between devices: 13 us -> 13.6 us
    ppermute x7 -> x8, waiting for transfers between devices: 5.78 us -> 4.28 us  [swap(): return lax.ppermute(held, AXES, [(i, i ^ mask) for i in range(devices)])]
    ppermute x7 -> x8, starting transfers between devices: 13 us -> 13.6 us  [swap(): return lax.ppermute(held, AXES, [(i, i ^ mask) for i in range(devices)])]
    pallas_call x1, Pallas kernels: 2.03 us -> 1.63 us  [on_device(): pl.pallas_call(lambda *refs: loss_and_grad(width, rows, *refs), out_shape...]
    pallas_call x1, Pallas kernels: 0.48 us -> 0.86 us  [on_device(): pl.pallas_call(lambda *refs: early_stats(width, rows, *refs), out_shape=(...]
  transfers between devices with their start and end apart: 7 -> 8, of which waited for: 5 -> 4; matrix products, arithmetic and copies ran while one was open for 0% -> 1% of each run, Pallas kernels for 2% -> 4%
where the time goes in v5:
time: 22.4 us; the launch traced here: 22.1 us
  starting transfers between devices  13.6 us (61%)
  waiting for transfers between devices  4.28 us (19%)
  Pallas kernels  3.28 us (15%)
  between operations  0.69 us (3%)
    ppermute x8, starting transfers between devices, swap(): return lax.ppermute(held, AXES, [(i, i ^ mask) for i in range(devices)])  13.6 us
    ppermute x8, waiting for transfers between devices, swap(): return lax.ppermute(held, AXES, [(i, i ^ mask) for i in range(devices)])  4.28 us
    pallas_call x1, Pallas kernels, on_device(): pl.pallas_call(lambda *refs: loss_and_grad(width, rows, *refs), out_shape...  1.63 us
    pallas_call x1, Pallas kernels, on_device(): pl.pallas_call(lambda *refs: early_stats(width, rows, *refs), out_shape=(...  0.86 us
    pallas_call x1, Pallas kernels, on_device(): pl.pallas_call(pack, out_shape=pltpu.VMEM((rows, width + LANES), jnp.bflo...  0.79 us
  transfers between devices with their start and end apart: 8, of which 4 were waited for; matrix products, arithmetic and copies ran while one was open for 1% of the time, Pallas kernels for 4%

profile of v5, /device:TPU:0, one launch (start us, length us, event | category | flops | bytes accessed | tf_op | source)
XLA Modules:
  0.0 22.1 jit_solution(1110671982477280995)
XLA Ops:
  0.6 0.8 %shard_map.41 = bf16[16,1152]{1,0:T(8,128)(2,1)S(1)} custom-call(bf16[16,1024]{1,0:T(8,128)(2,1)} %rows_hbm.1, s32[1,16]{1,0:T(1,128)} %bitcast.2), custom_call_target="tpu_custom_call" | custom-call | tf_op jit(solution)/shard_map/pallas_call | solution.py:212
  1.4 3.6 %collective-permute-start = (bf16[16,1152]{1,0:T(8,128)(2,1)S(1)}, bf16[16,1152]{1,0:T(8,128)(2,1)S(1)}, u32[]{:S(2)}, u32[]{:S(2)}) collective-permute-start(bf16[16,1152]{1,0:T(8,128)(2,1)S(1)} %shard_map.41), channel_id=1, source_target_pairs={{0,17},{1,16},{2,19},{3,18},{4,21},{5,20},{6,23},{7,22},{8,25},{9,... | collective-permute-start | bytes 110600 | tf_op jit(solution)/shard_map/ppermute | solution.py:25
  5.0 1.9 %collective-permute-done = bf16[16,1152]{1,0:T(8,128)(2,1)S(1)} collective-permute-done((bf16[16,1152]{1,0:T(8,128)(2,1)S(1)}, bf16[16,1152]{1,0:T(8,128)(2,1)S(1)}, u32[]{:S(2)}, u32[]{:S(2)}) %collective-permute-start) | collective-permute-done | bytes 36896 | tf_op jit(solution)/shard_map/ppermute | solution.py:25
  6.9 1.8 %collective-permute-start.1 = (bf16[32,1152]{1,0:T(8,128)(2,1)S(1)}, bf16[32,1152]{1,0:T(8,128)(2,1)S(1)}, u32[]{:S(2)}, u32[]{:S(2)}) collective-permute-start(bf16[32,1152]{1,0:T(8,128)(2,1)S(1)} %pad_maximum_fusion.3), channel_id=1, source_target_pairs={{0,9},{1,8},{2,11},{3,10},{4,13},{5,12},{6,15},{7,14},{8,1},{9,0},... | collective-permute-start | bytes 221192 | tf_op jit(solution)/shard_map/ppermute | solution.py:25
  8.7 2.4 %collective-permute-start.5 = (bf16[32,1152]{1,0:T(8,128)(2,1)S(1)}, bf16[32,1152]{1,0:T(8,128)(2,1)S(1)}, u32[]{:S(2)}, u32[]{:S(2)}) collective-permute-start(bf16[32,1152]{1,0:T(8,128)(2,1)S(1)} %pad_maximum_fusion.3), channel_id=1, source_target_pairs={{0,7},{1,6},{2,5},{3,4},{4,3},{5,2},{6,1},{7,0},{8,15},{9,14},{10,... | collective-permute-start | bytes 221192 | tf_op jit(solution)/shard_map/ppermute | solution.py:25
  11.2 0.0 collective-permute-done.1
  11.2 1.8 %collective-permute-start.2 = (bf16[64,1152]{1,0:T(8,128)(2,1)S(1)}, bf16[64,1152]{1,0:T(8,128)(2,1)S(1)}, u32[]{:S(2)}, u32[]{:S(2)}) collective-permute-start(bf16[64,1152]{1,0:T(8,128)(2,1)S(1)} %pad_maximum_fusion.2), channel_id=1, source_target_pairs={{0,3},{1,2},{2,1},{3,0},{4,7},{5,6},{6,5},{7,4},{8,11},{9,10},{10,... | collective-permute-start | bytes 442376 | tf_op jit(solution)/shard_map/ppermute | solution.py:25
  13.0 1.5 %collective-permute-start.4 = (bf16[64,1152]{1,0:T(8,128)(2,1)S(1)}, bf16[64,1152]{1,0:T(8,128)(2,1)S(1)}, u32[]{:S(2)}, u32[]{:S(2)}) collective-permute-start(bf16[64,1152]{1,0:T(8,128)(2,1)S(1)} %pad_maximum_fusion.2), channel_id=1, source_target_pairs={{0,5},{1,4},{2,7},{3,6},{4,1},{5,0},{6,3},{7,2},{8,13},{9,12},{10,... | collective-permute-start | bytes 442376 | tf_op jit(solution)/shard_map/ppermute | solution.py:25
  14.5 0.0 collective-permute-done.5
  14.5 1.6 %collective-permute-start.6 = (bf16[32,1152]{1,0:T(8,128)(2,1)S(1)}, bf16[32,1152]{1,0:T(8,128)(2,1)S(1)}, u32[]{:S(2)}, u32[]{:S(2)}) collective-permute-start(bf16[32,1152]{1,0:T(8,128)(2,1)S(1)} %collective-permute-done.5), channel_id=1, source_target_pairs={{0,9},{1,8},{2,11},{3,10},{4,13},{5,12},{6,15},{7,14},{8,1},{9,0},... | collective-permute-start | bytes 221192 | tf_op jit(solution)/shard_map/ppermute | solution.py:25
  16.1 0.8 %collective-permute-done.2 = bf16[64,1152]{1,0:T(8,128)(2,1)S(1)} collective-permute-done((bf16[64,1152]{1,0:T(8,128)(2,1)S(1)}, bf16[64,1152]{1,0:T(8,128)(2,1)S(1)}, u32[]{:S(2)}, u32[]{:S(2)}) %collective-permute-start.2) | collective-permute-done | bytes 147488 | tf_op jit(solution)/shard_map/ppermute | solution.py:25
  17.0 0.7 %collective-permute-start.3 = (bf16[128,1152]{1,0:T(8,128)(2,1)S(1)}, bf16[128,1152]{1,0:T(8,128)(2,1)S(1)}, u32[]{:S(2)}, u32[]{:S(2)}) collective-permute-start(bf16[128,1152]{1,0:T(8,128)(2,1)S(1)} %pad_maximum_fusion), channel_id=1, source_target_pairs={{0,1},{1,0},{2,3},{3,2},{4,5},{5,4},{6,7},{7,6},{8,9},{9,8},{10,11... | collective-permute-start | bytes 884744 | tf_op jit(solution)/shard_map/ppermute | solution.py:25
  17.6 1.2 %collective-permute-done.6 = bf16[32,1152]{1,0:T(8,128)(2,1)S(1)} collective-permute-done((bf16[32,1152]{1,0:T(8,128)(2,1)S(1)}, bf16[32,1152]{1,0:T(8,128)(2,1)S(1)}, u32[]{:S(2)}, u32[]{:S(2)}) %collective-permute-start.6) | collective-permute-done | bytes 73760 | tf_op jit(solution)/shard_map/ppermute | solution.py:25
  18.8 0.0 collective-permute-done.4
  18.8 0.2 %collective-permute-start.7 = (bf16[128,1152]{1,0:T(8,128)(2,1)S(1)}, bf16[128,1152]{1,0:T(8,128)(2,1)S(1)}, u32[]{:S(2)}, u32[]{:S(2)}) collective-permute-start(bf16[128,1152]{1,0:T(8,128)(2,1)S(1)} %pad_maximum_fusion.1), channel_id=1, source_target_pairs={{0,1},{1,0},{2,3},{3,2},{4,5},{5,4},{6,7},{7,6},{8,9},{9,8},{10,11... | collective-permute-start | bytes 884744 | tf_op jit(solution)/shard_map/ppermute | solution.py:25
  19.1 0.0 collective-permute-done.3
  19.2 0.9 %shard_map.42 = (f32[4,384]{1,0:T(4,128)S(1)}, f32[16,384]{1,0:T(8,128)S(1)}, f32[16,384]{1,0:T(8,128)S(1)}) custom-call(bf16[384,1152]{1,0:T(8,128)(2,1)S(1)} %constant_dynamic-update-slice_fusion.refs_0_), custom_call_target="tpu_custom_call" | custom-call | flops 301989888 | bytes 786432 | tf_op jit(solution)/shard_map/pallas_call | solution.py:226
  20.0 0.4 %collective-permute-done.7.refs_1_ = bf16[128,1152]{1,0:T(8,128)(2,1)S(1)} collective-permute-done((bf16[128,1152]{1,0:T(8,128)(2,1)S(1)}, bf16[128,1152]{1,0:T(8,128)(2,1)S(1)}, u32[]{:S(2)}, u32[]{:S(2)}) %collective-permute-start.7) | collective-permute-done | bytes 294944 | tf_op jit(solution)/shard_map/ppermute | solution.py:25
  20.5 1.6 %shard_map.43 = (f32[1,1]{1,0:T(1,128)}, bf16[16,1024]{1,0:T(8,128)(2,1)}) custom-call(bf16[384,1152]{1,0:T(8,128)(2,1)S(1)} %constant_dynamic-update-slice_fusion.refs_0_, bf16[128,1152]{1,0:T(8,128)(2,1)S(1)} %collective-permute-done.7.refs_1_, f32[4,384]{1,0:T(4,128)S(1)} %get-tuple-element.7.refs_2_, f32[16,384]{1,0:T(8,128)S(1)} %get-tuple-element.8.refs_3_, ...), custom_call_target="tpu_custom_call" | custom-call | flops 268435456 | bytes 1048576 | tf_op jit(solution)/shard_map/pallas_call | solution.py:240
  (12 shorter events, 0.2 us)
Async XLA Ops:
  1.4 5.4 %collective-permute-start = (bf16[16,1152]{1,0:T(8,128)(2,1)S(1)}, bf16[16,1152]{1,0:T(8,128)(2,1)S(1)}, u32[]{:S(2)}, u32[]{:S(2)}) collective-permute-start(bf16[16,1152]{1,0:T(8,128)(2,1)S(1)} %shard_map.41), channel_id=1, source_target_pairs={{0,17},{1,16},{2,19},{3,18},{4,21},{5,20},{6,23},{7,22},{8,25},{9,... | collective-permute-start | bytes 110600 | tf_op jit(solution)/shard_map/ppermute | solution.py:25
  6.9 4.3 %collective-permute-start.1 = (bf16[32,1152]{1,0:T(8,128)(2,1)S(1)}, bf16[32,1152]{1,0:T(8,128)(2,1)S(1)}, u32[]{:S(2)}, u32[]{:S(2)}) collective-permute-start(bf16[32,1152]{1,0:T(8,128)(2,1)S(1)} %pad_maximum_fusion.3), channel_id=1, source_target_pairs={{0,9},{1,8},{2,11},{3,10},{4,13},{5,12},{6,15},{7,14},{8,1},{9,0},... | collective-permute-start | bytes 221192 | tf_op jit(solution)/shard_map/ppermute | solution.py:25
  8.7 5.8 %collective-permute-start.5 = (bf16[32,1152]{1,0:T(8,128)(2,1)S(1)}, bf16[32,1152]{1,0:T(8,128)(2,1)S(1)}, u32[]{:S(2)}, u32[]{:S(2)}) collective-permute-start(bf16[32,1152]{1,0:T(8,128)(2,1)S(1)} %pad_maximum_fusion.3), channel_id=1, source_target_pairs={{0,7},{1,6},{2,5},{3,4},{4,3},{5,2},{6,1},{7,0},{8,15},{9,14},{10,... | collective-permute-start | bytes 221192 | tf_op jit(solution)/shard_map/ppermute | solution.py:25
  11.2 5.7 %collective-permute-start.2 = (bf16[64,1152]{1,0:T(8,128)(2,1)S(1)}, bf16[64,1152]{1,0:T(8,128)(2,1)S(1)}, u32[]{:S(2)}, u32[]{:S(2)}) collective-permute-start(bf16[64,1152]{1,0:T(8,128)(2,1)S(1)} %pad_maximum_fusion.2), channel_id=1, source_target_pairs={{0,3},{1,2},{2,1},{3,0},{4,7},{5,6},{6,5},{7,4},{8,11},{9,10},{10,... | collective-permute-start | bytes 442376 | tf_op jit(solution)/shard_map/ppermute | solution.py:25
  13.0 5.8 %collective-permute-start.4 = (bf16[64,1152]{1,0:T(8,128)(2,1)S(1)}, bf16[64,1152]{1,0:T(8,128)(2,1)S(1)}, u32[]{:S(2)}, u32[]{:S(2)}) collective-permute-start(bf16[64,1152]{1,0:T(8,128)(2,1)S(1)} %pad_maximum_fusion.2), channel_id=1, source_target_pairs={{0,5},{1,4},{2,7},{3,6},{4,1},{5,0},{6,3},{7,2},{8,13},{9,12},{10,... | collective-permute-start | bytes 442376 | tf_op jit(solution)/shard_map/ppermute | solution.py:25
  14.5 4.3 %collective-permute-start.6 = (bf16[32,1152]{1,0:T(8,128)(2,1)S(1)}, bf16[32,1152]{1,0:T(8,128)(2,1)S(1)}, u32[]{:S(2)}, u32[]{:S(2)}) collective-permute-start(bf16[32,1152]{1,0:T(8,128)(2,1)S(1)} %collective-permute-done.5), channel_id=1, source_target_pairs={{0,9},{1,8},{2,11},{3,10},{4,13},{5,12},{6,15},{7,14},{8,1},{9,0},... | collective-permute-start | bytes 221192 | tf_op jit(solution)/shard_map/ppermute | solution.py:25
  17.0 2.1 %collective-permute-start.3 = (bf16[128,1152]{1,0:T(8,128)(2,1)S(1)}, bf16[128,1152]{1,0:T(8,128)(2,1)S(1)}, u32[]{:S(2)}, u32[]{:S(2)}) collective-permute-start(bf16[128,1152]{1,0:T(8,128)(2,1)S(1)} %pad_maximum_fusion), channel_id=1, source_target_pairs={{0,1},{1,0},{2,3},{3,2},{4,5},{5,4},{6,7},{7,6},{8,9},{9,8},{10,11... | collective-permute-start | bytes 884744 | tf_op jit(solution)/shard_map/ppermute | solution.py:25
  18.8 1.6 %collective-permute-start.7 = (bf16[128,1152]{1,0:T(8,128)(2,1)S(1)}, bf16[128,1152]{1,0:T(8,128)(2,1)S(1)}, u32[]{:S(2)}, u32[]{:S(2)}) collective-permute-start(bf16[128,1152]{1,0:T(8,128)(2,1)S(1)} %pad_maximum_fusion.1), channel_id=1, source_target_pairs={{0,1},{1,0},{2,3},{3,2},{4,5},{5,4},{6,7},{7,6},{8,9},{9,8},{10,11... | collective-permute-start | bytes 884744 | tf_op jit(solution)/shard_map/ppermute | solution.py:25

commit v6 on v5

--- a/solution.py
+++ b/solution.py
@@ -25,27 +25,34 @@
     return lax.ppermute(held, AXES, [(i, i ^ mask) for i in range(devices)])
 
 
+def rotate(devices, bits, back, held):
+    low, high = (1 << b for b in bits)
+    after = {0: low, low: low | high, low | high: high, high: 0}
+    pairs = [(i, i & ~(low | high) | after[i & (low | high)]) for i in range(devices)]
+    pairs = [(i ^ 1, j) for i, j in pairs]
+    return lax.ppermute(held, AXES, [(j, i) if back else (i, j) for i, j in pairs])
+
+
 def gather_rows(devices, held):
     far, near = bit_groups(devices.bit_length() - 1)
     for b in far[:-1]:
         held = jnp.concatenate([held, swap(devices, 1 << b | 1, held)], axis=0)
     last = 1 << far[-1] | 1
-    first, second = (1 << b | 1 for b in near)
     beyond = swap(devices, last, held)
-    across = swap(devices, first | second, held)
+    across = swap(devices, sum(1 << b for b in near), held)
     held = jnp.concatenate([held, beyond], axis=0)
-    one = jnp.concatenate([held, swap(devices, first, held)], axis=0)
-    two = swap(devices, second, held)
+    one = jnp.concatenate([held, rotate(devices, near, False, held)], axis=0)
+    two = rotate(devices, near, True, held)
     two = jnp.concatenate([two, across, swap(devices, last, across)], axis=0)
     other = swap(devices, 1, one)
     return jnp.concatenate([one, other, two], axis=0), swap(devices, 1, two)
 
 
-def pack(rows_hbm, ids_hbm, out_ref, rows_ref, ids_ref, sems):
-    rows, width = rows_ref.shape
+def pack(rows_hbm, ids_hbm, out_ref, ids_ref, sems):
+    rows, width = rows_hbm.shape
     copies = [
         pltpu.make_async_copy(ids_hbm, ids_ref, sems.at[0]),
-        pltpu.make_async_copy(rows_hbm, rows_ref, sems.at[1]),
+        pltpu.make_async_copy(rows_hbm, out_ref.at[:, :width], sems.at[1]),
     ]
     for copy in copies:
         copy.start()
@@ -59,7 +66,6 @@
     coded = jnp.where(lane == 0, low, jnp.where(lane == 1, high, 0))
     out_ref[:, width:] = coded.astype(jnp.float32).astype(jnp.bfloat16)
     copies[1].wait()
-    out_ref[:, :width] = rows_ref[...]
 
 
 def dot_nt(a, b):
@@ -75,15 +81,19 @@
     return rows if rows <= 384 else 256
 
 
-def block_stats(width, rows_ref, cols_ref, start, own, keep, product=None):
+def block_stats(width, rows_ref, cols_ref, start, own, keep, products=None):
     scale = 1.0 / jnp.sqrt(jnp.float32(width))
     across, down = span(cols_ref.shape[0]), span(rows_ref.shape[0])
+    if products is not None:
+        down, across = products[0].shape
     cols = cols_ref[pl.ds(start, across), :width]
     col_ids = dot_nt(digits(16), cols_ref[pl.ds(start, across), width:])[:1]
     parts = []
     for first in range(0, rows_ref.shape[0], down):
-        s = dot_nt(rows_ref[first : first + down, :width], cols) if product is None else product
-        s = s * scale
+        if products is None:
+            s = dot_nt(rows_ref[first : first + down, :width], cols) * scale
+        else:
+            s = products[first // down] * scale
         row_ids = dot_nt(rows_ref[first : first + down, width:], digits(LANES))
         positive = jnp.concatenate([row_ids] * (across // LANES), axis=1) == col_ids
         masked = s
@@ -155,11 +165,10 @@
         inv_ref[:, at] = inverse
         return loss + jnp.sum(lse - possum * inverse)
 
-    def early_columns(start, loss):
-        at = pl.ds(start, span(early))
+    def early_columns(start, loss, products=None):
+        at = pl.ds(start, span(early) if products is None else products[0].shape[1])
         had = tuple(stats_ref[k : k + 1, at] for k in range(4))
-        turned = None if product is None else product.T
-        more = block_stats(width, late_ref, early_ref, start, own, lambda *_: None, turned)
+        more = block_stats(width, late_ref, early_ref, start, own, lambda *_: None, products)
         return finish(at, merge([had, more]), loss)
 
     def late_columns(start, loss):
@@ -169,15 +178,22 @@
             scores_ref[:, at] = scores
             positive_ref[:, at] = jnp.where(positive, 1.0, 0.0)
 
-        first = block_stats(width, early_ref, late_ref, start, own, keep, product)
+        first = block_stats(width, early_ref, late_ref, start, own, keep, products)
         second = block_stats(width, late_ref, late_ref, start, own, lambda *_: None)
         return finish(at, merge([first, second]), loss)
 
-    product = None
+    products = None
     if span(early) == early and span(late) == late:
-        product = dot_nt(early_ref[:, :width], late_ref[:, :width])
+        products = [
+            dot_nt(early_ref[k : k + LANES, :width], late_ref[:, :width])
+            for k in range(0, early, LANES)
+        ]
     loss = over_blocks(late, late_columns, jnp.float32(0.0))
-    loss = over_blocks(early, early_columns, loss)
+    if products is None:
+        loss = over_blocks(early, early_columns, loss)
+    else:
+        for k, product in enumerate(products):
+            loss = early_columns(k * LANES, loss, [product.T])
     loss_ref[...] = jnp.full((1, 1), loss / total)
     copies = [pltpu.make_async_copy(loss_ref, loss_hbm, sems.at[0])]
     copies[0].start()
@@ -215,7 +231,6 @@
         in_specs=[pl.BlockSpec(memory_space=pltpu.HBM)] * 2,
         out_specs=vmem,
         scratch_shapes=[
-            pltpu.VMEM((rows, width), jnp.bfloat16),
             pltpu.VMEM((1, rows), jnp.int32),
             pltpu.SemaphoreType.DMA((2,)),
         ],

time: 22.4 us -> 22.3 us (level)
  the two profiles are of different devices: /device:TPU:0 before, /device:TPU:27 now
where the time goes in v6:
time: 22.3 us; the launch traced here: 22.1 us
  waiting for transfers between devices  12.9 us (58%)
  starting transfers between devices  5.12 us (23%)
  Pallas kernels  3.22 us (14%)
  between operations  0.7 us (3%)
    ppermute x6, waiting for transfers between devices, swap(): return lax.ppermute(held, AXES, [(i, i ^ mask) for i in range(devices)])  8.57 us
    ppermute x2, waiting for transfers between devices, rotate(): lax.ppermute(held, AXES, [(j, i) if back else (i, j) for i, j in pairs])  4.34 us
    ppermute x6, starting transfers between devices, swap(): return lax.ppermute(held, AXES, [(i, i ^ mask) for i in range(devices)])  3.32 us
    ppermute x2, starting transfers between devices, rotate(): lax.ppermute(held, AXES, [(j, i) if back else (i, j) for i, j in pairs])  1.8 us
    pallas_call x1, Pallas kernels, on_device(): pl.pallas_call(lambda *refs: loss_and_grad(width, rows, *refs), out_shape...  1.57 us
    pallas_call x1, Pallas kernels, on_device(): pl.pallas_call(lambda *refs: early_stats(width, rows, *refs), out_shape=(...  0.86 us
    pallas_call x1, Pallas kernels, on_device(): pl.pallas_call(pack, out_shape=pltpu.VMEM((rows, width + LANES), jnp.bflo...  0.79 us
  transfers between devices with their start and end apart: 8, of which 6 were waited for; matrix products, arithmetic and copies ran while one was open for 1% of the time, Pallas kernels for 4%

profile of v6, /device:TPU:27, one launch (start us, length us, event | category | flops | bytes accessed | tf_op | source)
XLA Modules:
  0.0 22.1 jit_solution(17218603996809546973)
XLA Ops:
  0.6 0.8 %shard_map.41 = bf16[16,1152]{1,0:T(8,128)(2,1)S(1)} custom-call(bf16[16,1024]{1,0:T(8,128)(2,1)} %rows_hbm.1, s32[1,16]{1,0:T(1,128)} %bitcast.2), custom_call_target="tpu_custom_call" | custom-call | tf_op jit(solution)/shard_map/pallas_call | solution.py:228
  1.4 0.7 %collective-permute-start = (bf16[16,1152]{1,0:T(8,128)(2,1)S(1)}, bf16[16,1152]{1,0:T(8,128)(2,1)S(1)}, u32[]{:S(2)}, u32[]{:S(2)}) collective-permute-start(bf16[16,1152]{1,0:T(8,128)(2,1)S(1)} %shard_map.41), channel_id=1, source_target_pairs={{0,17},{1,16},{2,19},{3,18},{4,21},{5,20},{6,23},{7,22},{8,25},{9,... | collective-permute-start | bytes 110600 | tf_op jit(solution)/shard_map/ppermute | solution.py:25
  2.1 5.0 %collective-permute-done = bf16[16,1152]{1,0:T(8,128)(2,1)S(1)} collective-permute-done((bf16[16,1152]{1,0:T(8,128)(2,1)S(1)}, bf16[16,1152]{1,0:T(8,128)(2,1)S(1)}, u32[]{:S(2)}, u32[]{:S(2)}) %collective-permute-start) | collective-permute-done | bytes 36896 | tf_op jit(solution)/shard_map/ppermute | solution.py:25
  7.1 0.0 collective-permute-start.1
  7.1 1.3 %collective-permute-start.5 = (bf16[32,1152]{1,0:T(8,128)(2,1)S(1)}, bf16[32,1152]{1,0:T(8,128)(2,1)S(1)}, u32[]{:S(2)}, u32[]{:S(2)}) collective-permute-start(bf16[32,1152]{1,0:T(8,128)(2,1)S(1)} %pad_maximum_fusion.3), channel_id=1, source_target_pairs={{0,6},{1,7},{2,4},{3,5},{4,2},{5,3},{6,0},{7,1},{8,14},{9,15},{10,... | collective-permute-start | bytes 221192 | tf_op jit(solution)/shard_map/ppermute | solution.py:25
  8.4 3.3 %collective-permute-done.1 = bf16[32,1152]{1,0:T(8,128)(2,1)S(1)} collective-permute-done((bf16[32,1152]{1,0:T(8,128)(2,1)S(1)}, bf16[32,1152]{1,0:T(8,128)(2,1)S(1)}, u32[]{:S(2)}, u32[]{:S(2)}) %collective-permute-start.1) | collective-permute-done | bytes 73760 | tf_op jit(solution)/shard_map/ppermute | solution.py:25
  11.7 1.3 %collective-permute-start.2 = (bf16[64,1152]{1,0:T(8,128)(2,1)S(1)}, bf16[64,1152]{1,0:T(8,128)(2,1)S(1)}, u32[]{:S(2)}, u32[]{:S(2)}) collective-permute-start(bf16[64,1152]{1,0:T(8,128)(2,1)S(1)} %pad_maximum_fusion.2), channel_id=1, source_target_pairs={{1,2},{0,3},{3,6},{2,7},{5,0},{4,1},{7,4},{6,5},{9,10},{8,11},{11,... | collective-permute-start | bytes 442376 | tf_op jit(solution)/shard_map/ppermute | solution.py:33
  13.0 0.5 %collective-permute-start.4 = (bf16[64,1152]{1,0:T(8,128)(2,1)S(1)}, bf16[64,1152]{1,0:T(8,128)(2,1)S(1)}, u32[]{:S(2)}, u32[]{:S(2)}) collective-permute-start(bf16[64,1152]{1,0:T(8,128)(2,1)S(1)} %pad_maximum_fusion.2), channel_id=1, source_target_pairs={{2,1},{3,0},{6,3},{7,2},{0,5},{1,4},{4,7},{5,6},{10,9},{11,8},{14,... | collective-permute-start | bytes 442376 | tf_op jit(solution)/shard_map/ppermute | solution.py:33
  13.5 0.0 collective-permute-done.5
  13.5 0.8 %collective-permute-start.6 = (bf16[32,1152]{1,0:T(8,128)(2,1)S(1)}, bf16[32,1152]{1,0:T(8,128)(2,1)S(1)}, u32[]{:S(2)}, u32[]{:S(2)}) collective-permute-start(bf16[32,1152]{1,0:T(8,128)(2,1)S(1)} %collective-permute-done.5), channel_id=1, source_target_pairs={{0,9},{1,8},{2,11},{3,10},{4,13},{5,12},{6,15},{7,14},{8,1},{9,0},... | collective-permute-start | bytes 221192 | tf_op jit(solution)/shard_map/ppermute | solution.py:25
  14.4 3.3 %collective-permute-done.2 = bf16[64,1152]{1,0:T(8,128)(2,1)S(1)} collective-permute-done((bf16[64,1152]{1,0:T(8,128)(2,1)S(1)}, bf16[64,1152]{1,0:T(8,128)(2,1)S(1)}, u32[]{:S(2)}, u32[]{:S(2)}) %collective-permute-start.2) | collective-permute-done | bytes 147488 | tf_op jit(solution)/shard_map/ppermute | solution.py:33
  17.7 0.1 collective-permute-start.3
  17.7 0.1 collective-permute-done.6
  17.8 1.1 %collective-permute-done.4 = bf16[64,1152]{1,0:T(8,128)(2,1)S(1)} collective-permute-done((bf16[64,1152]{1,0:T(8,128)(2,1)S(1)}, bf16[64,1152]{1,0:T(8,128)(2,1)S(1)}, u32[]{:S(2)}, u32[]{:S(2)}) %collective-permute-start.4) | collective-permute-done | bytes 147488 | tf_op jit(solution)/shard_map/ppermute | solution.py:33
  18.9 0.5 %collective-permute-start.7 = (bf16[128,1152]{1,0:T(8,128)(2,1)S(1)}, bf16[128,1152]{1,0:T(8,128)(2,1)S(1)}, u32[]{:S(2)}, u32[]{:S(2)}) collective-permute-start(bf16[128,1152]{1,0:T(8,128)(2,1)S(1)} %pad_maximum_fusion.1), channel_id=1, source_target_pairs={{0,1},{1,0},{2,3},{3,2},{4,5},{5,4},{6,7},{7,6},{8,9},{9,8},{10,11... | collective-permute-start | bytes 884744 | tf_op jit(solution)/shard_map/ppermute | solution.py:25
  19.4 0.0 collective-permute-done.3
  19.5 0.9 %shard_map.42 = (f32[4,384]{1,0:T(4,128)S(1)}, f32[16,384]{1,0:T(8,128)S(1)}, f32[16,384]{1,0:T(8,128)S(1)}) custom-call(bf16[384,1152]{1,0:T(8,128)(2,1)S(1)} %constant_dynamic-update-slice_fusion.refs_0_), custom_call_target="tpu_custom_call" | custom-call | flops 301989888 | bytes 786432 | tf_op jit(solution)/shard_map/pallas_call | solution.py:241
  20.4 0.2 collective-permute-done.7.refs_1_
  20.6 1.6 %shard_map.43 = (f32[1,1]{1,0:T(1,128)}, bf16[16,1024]{1,0:T(8,128)(2,1)}) custom-call(bf16[384,1152]{1,0:T(8,128)(2,1)S(1)} %constant_dynamic-update-slice_fusion.refs_0_, bf16[128,1152]{1,0:T(8,128)(2,1)S(1)} %collective-permute-done.7.refs_1_, f32[4,384]{1,0:T(4,128)S(1)} %get-tuple-element.7.refs_2_, f32[16,384]{1,0:T(8,128)S(1)} %get-tuple-element.8.refs_3_, ...), custom_call_target="tpu_custom_call" | custom-call | flops 268435456 | bytes 1048576 | tf_op jit(solution)/shard_map/pallas_call | solution.py:255
  (12 shorter events, 0.2 us)
Async XLA Ops:
  1.4 5.7 %collective-permute-start = (bf16[16,1152]{1,0:T(8,128)(2,1)S(1)}, bf16[16,1152]{1,0:T(8,128)(2,1)S(1)}, u32[]{:S(2)}, u32[]{:S(2)}) collective-permute-start(bf16[16,1152]{1,0:T(8,128)(2,1)S(1)} %shard_map.41), channel_id=1, source_target_pairs={{0,17},{1,16},{2,19},{3,18},{4,21},{5,20},{6,23},{7,22},{8,25},{9,... | collective-permute-start | bytes 110600 | tf_op jit(solution)/shard_map/ppermute | solution.py:25
  7.1 4.6 %collective-permute-start.1 = (bf16[32,1152]{1,0:T(8,128)(2,1)S(1)}, bf16[32,1152]{1,0:T(8,128)(2,1)S(1)}, u32[]{:S(2)}, u32[]{:S(2)}) collective-permute-start(bf16[32,1152]{1,0:T(8,128)(2,1)S(1)} %pad_maximum_fusion.3), channel_id=1, source_target_pairs={{0,9},{1,8},{2,11},{3,10},{4,13},{5,12},{6,15},{7,14},{8,1},{9,0},... | collective-permute-start | bytes 221192 | tf_op jit(solution)/shard_map/ppermute | solution.py:25
  7.1 6.4 %collective-permute-start.5 = (bf16[32,1152]{1,0:T(8,128)(2,1)S(1)}, bf16[32,1152]{1,0:T(8,128)(2,1)S(1)}, u32[]{:S(2)}, u32[]{:S(2)}) collective-permute-start(bf16[32,1152]{1,0:T(8,128)(2,1)S(1)} %pad_maximum_fusion.3), channel_id=1, source_target_pairs={{0,6},{1,7},{2,4},{3,5},{4,2},{5,3},{6,0},{7,1},{8,14},{9,15},{10,... | collective-permute-start | bytes 221192 | tf_op jit(solution)/shard_map/ppermute | solution.py:25
  11.7 5.9 %collective-permute-start.2 = (bf16[64,1152]{1,0:T(8,128)(2,1)S(1)}, bf16[64,1152]{1,0:T(8,128)(2,1)S(1)}, u32[]{:S(2)}, u32[]{:S(2)}) collective-permute-start(bf16[64,1152]{1,0:T(8,128)(2,1)S(1)} %pad_maximum_fusion.2), channel_id=1, source_target_pairs={{1,2},{0,3},{3,6},{2,7},{5,0},{4,1},{7,4},{6,5},{9,10},{8,11},{11,... | collective-permute-start | bytes 442376 | tf_op jit(solution)/shard_map/ppermute | solution.py:33
  13.0 5.9 %collective-permute-start.4 = (bf16[64,1152]{1,0:T(8,128)(2,1)S(1)}, bf16[64,1152]{1,0:T(8,128)(2,1)S(1)}, u32[]{:S(2)}, u32[]{:S(2)}) collective-permute-start(bf16[64,1152]{1,0:T(8,128)(2,1)S(1)} %pad_maximum_fusion.2), channel_id=1, source_target_pairs={{2,1},{3,0},{6,3},{7,2},{0,5},{1,4},{4,7},{5,6},{10,9},{11,8},{14,... | collective-permute-start | bytes 442376 | tf_op jit(solution)/shard_map/ppermute | solution.py:33
  13.5 4.3 %collective-permute-start.6 = (bf16[32,1152]{1,0:T(8,128)(2,1)S(1)}, bf16[32,1152]{1,0:T(8,128)(2,1)S(1)}, u32[]{:S(2)}, u32[]{:S(2)}) collective-permute-start(bf16[32,1152]{1,0:T(8,128)(2,1)S(1)} %collective-permute-done.5), channel_id=1, source_target_pairs={{0,9},{1,8},{2,11},{3,10},{4,13},{5,12},{6,15},{7,14},{8,1},{9,0},... | collective-permute-start | bytes 221192 | tf_op jit(solution)/shard_map/ppermute | solution.py:25
  17.7 1.7 %collective-permute-start.3 = (bf16[128,1152]{1,0:T(8,128)(2,1)S(1)}, bf16[128,1152]{1,0:T(8,128)(2,1)S(1)}, u32[]{:S(2)}, u32[]{:S(2)}) collective-permute-start(bf16[128,1152]{1,0:T(8,128)(2,1)S(1)} %pad_maximum_fusion), channel_id=1, source_target_pairs={{0,1},{1,0},{2,3},{3,2},{4,5},{5,4},{6,7},{7,6},{8,9},{9,8},{10,11... | collective-permute-start | bytes 884744 | tf_op jit(solution)/shard_map/ppermute | solution.py:25
  18.9 1.7 %collective-permute-start.7 = (bf16[128,1152]{1,0:T(8,128)(2,1)S(1)}, bf16[128,1152]{1,0:T(8,128)(2,1)S(1)}, u32[]{:S(2)}, u32[]{:S(2)}) collective-permute-start(bf16[128,1152]{1,0:T(8,128)(2,1)S(1)} %pad_maximum_fusion.1), channel_id=1, source_target_pairs={{0,1},{1,0},{2,3},{3,2},{4,5},{5,4},{6,7},{7,6},{8,9},{9,8},{10,11... | collective-permute-start | bytes 884744 | tf_op jit(solution)/shard_map/ppermute | solution.py:25

commit v7 on v6

--- a/solution.py
+++ b/solution.py
@@ -8,6 +8,7 @@
 AXES = ("row", "col")
 LANES = 128
 RADIX = 256
+LOG2E = 1.4426950408889634
 
 
 def bit_groups(bits):
@@ -30,7 +31,10 @@
     after = {0: low, low: low | high, low | high: high, high: 0}
     pairs = [(i, i & ~(low | high) | after[i & (low | high)]) for i in range(devices)]
     pairs = [(i ^ 1, j) for i, j in pairs]
-    return lax.ppermute(held, AXES, [(j, i) if back else (i, j) for i, j in pairs])
+    ahead = {i: j for i, j in pairs}
+    behind = {j: i for i, j in pairs}
+    turned = [(i, (ahead if (i & 1) == back else behind)[i]) for i in range(devices)]
+    return lax.ppermute(held, AXES, turned)
 
 
 def gather_rows(devices, held):
@@ -44,8 +48,9 @@
     one = jnp.concatenate([held, rotate(devices, near, False, held)], axis=0)
     two = rotate(devices, near, True, held)
     two = jnp.concatenate([two, across, swap(devices, last, across)], axis=0)
-    other = swap(devices, 1, one)
-    return jnp.concatenate([one, other, two], axis=0), swap(devices, 1, two)
+    half = swap(devices, 1, one)
+    rest = swap(devices, 1, two)
+    return jnp.concatenate([one, two], axis=0), half, rest
 
 
 def pack(rows_hbm, ids_hbm, out_ref, ids_ref, sems):
@@ -81,8 +86,7 @@
     return rows if rows <= 384 else 256
 
 
-def block_stats(width, rows_ref, cols_ref, start, own, keep, products=None):
-    scale = 1.0 / jnp.sqrt(jnp.float32(width))
+def block_stats(width, rows_ref, cols_ref, start, own, keep, products=None, weigh=1):
     across, down = span(cols_ref.shape[0]), span(rows_ref.shape[0])
     if products is not None:
         down, across = products[0].shape
@@ -91,9 +95,9 @@
     parts = []
     for first in range(0, rows_ref.shape[0], down):
         if products is None:
-            s = dot_nt(rows_ref[first : first + down, :width], cols) * scale
+            s = dot_nt(rows_ref[first : first + down, :width], cols)
         else:
-            s = products[first // down] * scale
+            s = products[first // down]
         row_ids = dot_nt(rows_ref[first : first + down, width:], digits(LANES))
         positive = jnp.concatenate([row_ids] * (across // LANES), axis=1) == col_ids
         masked = s
@@ -105,18 +109,24 @@
         if first == 0:
             keep(masked[:own], positive[:own])
         top = jnp.max(masked, axis=0, keepdims=True)
-        add = jnp.sum(jnp.exp(masked - top), axis=0, keepdims=True)
-        possum = jnp.sum(jnp.where(positive, s, 0.0), axis=0, keepdims=True)
+        add = jnp.sum(power(masked - top, width), axis=0, keepdims=True)
+        possum = jnp.zeros_like(top)
+        if weigh:
+            possum = weigh * jnp.sum(jnp.where(positive, s, 0.0), axis=0, keepdims=True)
         count = jnp.sum(jnp.where(positive, 1.0, 0.0), axis=0, keepdims=True)
         parts.append((top, add, possum, count))
-    return merge(parts)
-
-
-def merge(parts):
+    return merge(parts, width)
+
+
+def power(raw, width):
+    return jnp.exp2(raw * (LOG2E / jnp.sqrt(jnp.float32(width))))
+
+
+def merge(parts, width):
     peak = parts[0][0]
     for p in parts[1:]:
         peak = jnp.maximum(peak, p[0])
-    added = sum(p[1] * jnp.exp(p[0] - peak) for p in parts)
+    added = sum(p[1] * power(p[0] - peak, width) for p in parts)
     return peak, added, sum(p[2] for p in parts), sum(p[3] for p in parts)
 
 
@@ -129,58 +139,46 @@
     )
 
 
-def early_stats(width, own, early_ref, stats_ref, scores_ref, positive_ref):
-    early = early_ref.shape[0]
+def keep_in(scores_ref, positive_ref, at):
+    def keep(scores, positive):
+        scores_ref[:, at] = scores
+        positive_ref[:, at] = jnp.where(positive, 1.0, 0.0)
+
+    return keep
+
+
+def near_stats(width, own, near_ref, stats_ref, scores_ref, positive_ref):
+    near = near_ref.shape[0]
 
     def body(start, carry):
-        at = pl.ds(start, span(early))
-
-        def keep(scores, positive):
-            scores_ref[:, at] = scores
-            positive_ref[:, at] = jnp.where(positive, 1.0, 0.0)
-
-        stats = block_stats(width, early_ref, early_ref, start, own, keep)
+        at = pl.ds(start, span(near))
+        keep = keep_in(scores_ref, positive_ref, at)
+        stats = block_stats(width, near_ref, near_ref, start, own, keep)
         for k, value in enumerate(stats):
             stats_ref[k : k + 1, at] = value
         return carry
 
-    over_blocks(early, body, 0)
-
-
-def loss_and_grad(
-    width, own, early_ref, late_ref, stats_ref, early_scores_ref, early_positive_ref,
-    loss_hbm, grad_hbm, lse_ref, inv_ref, scores_ref, positive_ref, loss_ref, grad_ref, sems,
-):
+    over_blocks(near, body, 0)
+
+
+def extend(width, own, early_ref, late_ref, had, scores_ref, positive_ref, emit, carry):
     early, late = early_ref.shape[0], late_ref.shape[0]
-    total = early + late
-    scale = 1.0 / jnp.sqrt(jnp.float32(width))
-    scores_ref[:, :early] = early_scores_ref[...]
-    positive_ref[:, :early] = early_positive_ref[...]
-
-    def finish(at, stats, loss):
-        peak, added, possum, count = stats
-        inverse = 1.0 / count
-        lse = peak + jnp.log(added)
-        lse_ref[:, at] = lse
-        inv_ref[:, at] = inverse
-        return loss + jnp.sum(lse - possum * inverse)
-
-    def early_columns(start, loss, products=None):
+    had_stats, had_scores, had_positive = had
+    scores_ref[:, :early] = had_scores[...]
+    positive_ref[:, :early] = had_positive[...]
+
+    def early_columns(start, carry, products=None):
         at = pl.ds(start, span(early) if products is None else products[0].shape[1])
-        had = tuple(stats_ref[k : k + 1, at] for k in range(4))
-        more = block_stats(width, late_ref, early_ref, start, own, lambda *_: None, products)
-        return finish(at, merge([had, more]), loss)
-
-    def late_columns(start, loss):
+        first = tuple(had_stats[k : k + 1, at] for k in range(4))
+        more = block_stats(width, late_ref, early_ref, start, own, lambda *_: None, products, 0)
+        return emit(at, merge([first, more], width), carry)
+
+    def late_columns(start, carry):
         at = pl.ds(early + start, span(late))
-
-        def keep(scores, positive):
-            scores_ref[:, at] = scores
-            positive_ref[:, at] = jnp.where(positive, 1.0, 0.0)
-
-        first = block_stats(width, early_ref, late_ref, start, own, keep, products)
+        keep = keep_in(scores_ref, positive_ref, at)
+        first = block_stats(width, early_ref, late_ref, start, own, keep, products, 2)
         second = block_stats(width, late_ref, late_ref, start, own, lambda *_: None)
-        return finish(at, merge([first, second]), loss)
+        return emit(at, merge([first, second], width), carry)
 
     products = None
     if span(early) == early and span(late) == late:
@@ -188,17 +186,52 @@
             dot_nt(early_ref[k : k + LANES, :width], late_ref[:, :width])
             for k in range(0, early, LANES)
         ]
-    loss = over_blocks(late, late_columns, jnp.float32(0.0))
+    carry = over_blocks(late, late_columns, carry)
     if products is None:
-        loss = over_blocks(early, early_columns, loss)
-    else:
-        for k, product in enumerate(products):
-            loss = early_columns(k * LANES, loss, [product.T])
+        return over_blocks(early, early_columns, carry)
+    for k, product in enumerate(products):
+        carry = early_columns(k * LANES, carry, [product.T])
+    return carry
+
+
+def more_stats(
+    width, own, early_ref, late_ref, had_stats, had_scores, had_positive,
+    stats_ref, scores_ref, positive_ref,
+):
+    def emit(at, stats, carry):
+        for k, value in enumerate(stats):
+            stats_ref[k : k + 1, at] = value
+        return carry
+
+    had = (had_stats, had_scores, had_positive)
+    extend(width, own, early_ref, late_ref, had, scores_ref, positive_ref, emit, 0)
+
+
+def loss_and_grad(
+    width, own, early_ref, late_ref, had_stats, had_scores, had_positive,
+    loss_hbm, grad_hbm, lse_ref, inv_ref, scores_ref, positive_ref, loss_ref, grad_ref, sems,
+):
+    early, late = early_ref.shape[0], late_ref.shape[0]
+    total = early + late
+    scale = 1.0 / jnp.sqrt(jnp.float32(width))
+
+    def emit(at, stats, loss):
+        peak, added, possum, count = stats
+        inverse = 1.0 / count
+        lse = scale * peak + jnp.log(added)
+        lse_ref[:, at] = lse
+        inv_ref[:, at] = inverse
+        return loss + jnp.sum(lse - scale * possum * inverse)
+
+    had = (had_stats, had_scores, had_positive)
+    loss = extend(
+        width, own, early_ref, late_ref, had, scores_ref, positive_ref, emit, jnp.float32(0.0)
+    )
     loss_ref[...] = jnp.full((1, 1), loss / total)
     copies = [pltpu.make_async_copy(loss_ref, loss_hbm, sems.at[0])]
     copies[0].start()
 
-    masked = scores_ref[...]
+    masked = scores_ref[...] * scale
     positive = positive_ref[...]
     peak = jnp.max(masked, axis=1, keepdims=True)
     lse = peak + jnp.log(jnp.sum(jnp.exp(masked - peak), axis=1, keepdims=True))
@@ -236,22 +269,35 @@
         ],
         compiler_params=pltpu.CompilerParams(vmem_limit_bytes=60 << 20),
     )(embeddings, group_ids[None, :])
-    early_rows, late_rows = gather_rows(devices, held)
-    early, late = early_rows.shape[0], late_rows.shape[0]
+    near, half, rest = gather_rows(devices, held)
+
+    def stats_shape(columns):
+        return tuple(jax.ShapeDtypeStruct((k, columns), jnp.float32) for k in (4, rows, rows))
+
+    def cost(products):
+        return pl.CostEstimate(
+            flops=2 * products * width, bytes_accessed=2 * total * width, transcendentals=products
+        )
+
+    first = near.shape[0]
     stats = pl.pallas_call(
-        lambda *refs: early_stats(width, rows, *refs),
-        out_shape=(
-            jax.ShapeDtypeStruct((4, early), jnp.float32),
-            jax.ShapeDtypeStruct((rows, early), jnp.float32),
-            jax.ShapeDtypeStruct((rows, early), jnp.float32),
-        ),
+        lambda *refs: near_stats(width, rows, *refs),
+        out_shape=stats_shape(first),
         in_specs=[vmem],
         out_specs=(vmem, vmem, vmem),
         compiler_params=params,
-        cost_estimate=pl.CostEstimate(
-            flops=2 * early * early * width, bytes_accessed=2 * early * width, transcendentals=early * early
-        ),
-    )(early_rows)
+        cost_estimate=cost(first * first),
+    )(near)
+    early = first + half.shape[0]
+    stats = pl.pallas_call(
+        lambda *refs: more_stats(width, rows, *refs),
+        out_shape=stats_shape(early),
+        in_specs=[vmem] * 5,
+        out_specs=(vmem, vmem, vmem),
+        compiler_params=params,
+        cost_estimate=cost(early * early - first * first),
+    )(near, half, *stats)
+    early_rows = jnp.concatenate([near, half], axis=0)
     loss, grad = pl.pallas_call(
         lambda *refs: loss_and_grad(width, rows, *refs),
         out_shape=(
@@ -270,10 +316,8 @@
             pltpu.SemaphoreType.DMA((3,)),
         ],
         compiler_params=params,
-        cost_estimate=pl.CostEstimate(
-            flops=4 * total * late * width, bytes_accessed=2 * total * width, transcendentals=2 * total * late
-        ),
-    )(early_rows, late_rows, *stats)
+        cost_estimate=cost(total * total - early * early),
+    )(early_rows, rest, *stats)
     return (loss[0, 0], grad)
 
 

time: 22.3 us -> 22.2 us (level)
  the two profiles are of different devices: /device:TPU:27 before, /device:TPU:0 now
where the time goes in v7:
time: 22.2 us; the launch traced here: 22 us
  starting transfers between devices  13.4 us (60%)
  waiting for transfers between devices  4.33 us (20%)
  Pallas kernels  3.35 us (15%)
  between operations  0.7 us (3%)
    ppermute x6, starting transfers between devices, swap(): return lax.ppermute(held, AXES, [(i, i ^ mask) for i in range(devices)])  10.1 us
    ppermute x6, waiting for transfers between devices, swap(): return lax.ppermute(held, AXES, [(i, i ^ mask) for i in range(devices)])  3.88 us
    ppermute x2, starting transfers between devices, rotate(): return lax.ppermute(held, AXES, turned)  3.3 us
    pallas_call x1, Pallas kernels, on_device(): pl.pallas_call(lambda *refs: loss_and_grad(width, rows, *refs), out_shape...  1.55 us
    pallas_call x1, Pallas kernels, on_device(): pl.pallas_call(pack, out_shape=pltpu.VMEM((rows, width + LANES), jnp.bflo...  0.79 us
    pallas_call x1, Pallas kernels, on_device(): pl.pallas_call(lambda *refs: more_stats(width, rows, *refs), out_shape=st...  0.55 us
    pallas_call x1, Pallas kernels, on_device(): pl.pallas_call(lambda *refs: near_stats(width, rows, *refs), out_shape=st...  0.46 us
    ppermute x2, waiting for transfers between devices, rotate(): return lax.ppermute(held, AXES, turned)  0.46 us
  transfers between devices with their start and end apart: 8, of which 4 were waited for; matrix products, arithmetic and copies ran while one was open for 1% of the time, Pallas kernels for 5%

profile of v7, /device:TPU:0, one launch (start us, length us, event | category | flops | bytes accessed | tf_op | source)
XLA Modules:
  0.0 22.0 jit_solution(6127268269259222635)
XLA Ops:
  0.6 0.8 %shard_map.41 = bf16[16,1152]{1,0:T(8,128)(2,1)S(1)} custom-call(bf16[16,1024]{1,0:T(8,128)(2,1)} %rows_hbm.1, s32[1,16]{1,0:T(1,128)} %bitcast.2), custom_call_target="tpu_custom_call" | custom-call | tf_op jit(solution)/shard_map/pallas_call | solution.py:261
  1.4 3.6 %collective-permute-start = (bf16[16,1152]{1,0:T(8,128)(2,1)S(1)}, bf16[16,1152]{1,0:T(8,128)(2,1)S(1)}, u32[]{:S(2)}, u32[]{:S(2)}) collective-permute-start(bf16[16,1152]{1,0:T(8,128)(2,1)S(1)} %shard_map.41), channel_id=1, source_target_pairs={{0,17},{1,16},{2,19},{3,18},{4,21},{5,20},{6,23},{7,22},{8,25},{9,... | collective-permute-start | bytes 110600 | tf_op jit(solution)/shard_map/ppermute | solution.py:26
  5.0 1.9 %collective-permute-done = bf16[16,1152]{1,0:T(8,128)(2,1)S(1)} collective-permute-done((bf16[16,1152]{1,0:T(8,128)(2,1)S(1)}, bf16[16,1152]{1,0:T(8,128)(2,1)S(1)}, u32[]{:S(2)}, u32[]{:S(2)}) %collective-permute-start) | collective-permute-done | bytes 36896 | tf_op jit(solution)/shard_map/ppermute | solution.py:26
  6.9 1.8 %collective-permute-start.1 = (bf16[32,1152]{1,0:T(8,128)(2,1)S(1)}, bf16[32,1152]{1,0:T(8,128)(2,1)S(1)}, u32[]{:S(2)}, u32[]{:S(2)}) collective-permute-start(bf16[32,1152]{1,0:T(8,128)(2,1)S(1)} %pad_maximum_fusion.3), channel_id=1, source_target_pairs={{0,9},{1,8},{2,11},{3,10},{4,13},{5,12},{6,15},{7,14},{8,1},{9,0},... | collective-permute-start | bytes 221192 | tf_op jit(solution)/shard_map/ppermute | solution.py:26
  8.7 2.4 %collective-permute-start.4 = (bf16[32,1152]{1,0:T(8,128)(2,1)S(1)}, bf16[32,1152]{1,0:T(8,128)(2,1)S(1)}, u32[]{:S(2)}, u32[]{:S(2)}) collective-permute-start(bf16[32,1152]{1,0:T(8,128)(2,1)S(1)} %pad_maximum_fusion.3), channel_id=1, source_target_pairs={{0,6},{1,7},{2,4},{3,5},{4,2},{5,3},{6,0},{7,1},{8,14},{9,15},{10,... | collective-permute-start | bytes 221192 | tf_op jit(solution)/shard_map/ppermute | solution.py:26
  11.2 0.0 collective-permute-done.1
  11.2 1.8 %collective-permute-start.2 = (bf16[64,1152]{1,0:T(8,128)(2,1)S(1)}, bf16[64,1152]{1,0:T(8,128)(2,1)S(1)}, u32[]{:S(2)}, u32[]{:S(2)}) collective-permute-start(bf16[64,1152]{1,0:T(8,128)(2,1)S(1)} %pad_maximum_fusion.2), channel_id=1, source_target_pairs={{0,3},{1,4},{2,7},{3,0},{4,1},{5,6},{6,5},{7,2},{8,11},{9,12},{10,... | collective-permute-start | bytes 442376 | tf_op jit(solution)/shard_map/ppermute | solution.py:37
  13.0 1.5 %collective-permute-start.3 = (bf16[64,1152]{1,0:T(8,128)(2,1)S(1)}, bf16[64,1152]{1,0:T(8,128)(2,1)S(1)}, u32[]{:S(2)}, u32[]{:S(2)}) collective-permute-start(bf16[64,1152]{1,0:T(8,128)(2,1)S(1)} %pad_maximum_fusion.2), channel_id=1, source_target_pairs={{0,5},{1,2},{2,1},{3,6},{4,7},{5,0},{6,3},{7,4},{8,13},{9,10},{10,... | collective-permute-start | bytes 442376 | tf_op jit(solution)/shard_map/ppermute | solution.py:37
  14.5 0.0 collective-permute-done.4
  14.5 1.3 %collective-permute-start.5 = (bf16[32,1152]{1,0:T(8,128)(2,1)S(1)}, bf16[32,1152]{1,0:T(8,128)(2,1)S(1)}, u32[]{:S(2)}, u32[]{:S(2)}) collective-permute-start(bf16[32,1152]{1,0:T(8,128)(2,1)S(1)} %collective-permute-done.4), channel_id=1, source_target_pairs={{0,9},{1,8},{2,11},{3,10},{4,13},{5,12},{6,15},{7,14},{8,1},{9,0},... | collective-permute-start | bytes 221192 | tf_op jit(solution)/shard_map/ppermute | solution.py:26
  15.8 0.5 %collective-permute-done.2 = bf16[64,1152]{1,0:T(8,128)(2,1)S(1)} collective-permute-done((bf16[64,1152]{1,0:T(8,128)(2,1)S(1)}, bf16[64,1152]{1,0:T(8,128)(2,1)S(1)}, u32[]{:S(2)}, u32[]{:S(2)}) %collective-permute-start.2) | collective-permute-done | bytes 147488 | tf_op jit(solution)/shard_map/ppermute | solution.py:37
  16.3 0.8 %collective-permute-start.6 = (bf16[128,1152]{1,0:T(8,128)(2,1)S(1)}, bf16[128,1152]{1,0:T(8,128)(2,1)S(1)}, u32[]{:S(2)}, u32[]{:S(2)}) collective-permute-start(bf16[128,1152]{1,0:T(8,128)(2,1)S(1)} %pad_maximum_fusion), channel_id=1, source_target_pairs={{0,1},{1,0},{2,3},{3,2},{4,5},{5,4},{6,7},{7,6},{8,9},{9,8},{10,11... | collective-permute-start | bytes 884744 | tf_op jit(solution)/shard_map/ppermute | solution.py:26
  17.1 1.7 %collective-permute-done.5 = bf16[32,1152]{1,0:T(8,128)(2,1)S(1)} collective-permute-done((bf16[32,1152]{1,0:T(8,128)(2,1)S(1)}, bf16[32,1152]{1,0:T(8,128)(2,1)S(1)}, u32[]{:S(2)}, u32[]{:S(2)}) %collective-permute-start.5) | collective-permute-done | bytes 73760 | tf_op jit(solution)/shard_map/ppermute | solution.py:26
  18.8 0.0 collective-permute-done.3
  18.8 0.2 collective-permute-start.7
  19.1 0.5 %shard_map.42 = (f32[4,256]{1,0:T(4,128)S(1)}, f32[16,256]{1,0:T(8,128)S(1)}, f32[16,256]{1,0:T(8,128)S(1)}) custom-call(bf16[256,1152]{1,0:T(8,128)(2,1)S(1)} %get-tuple-element.22.refs_0_), custom_call_target="tpu_custom_call" | custom-call | flops 134217728 | bytes 1048576 | tf_op jit(solution)/shard_map/pallas_call | solution.py:283
  19.6 0.0 collective-permute-done.6.refs_1_
  19.6 0.5 %shard_map.43 = (f32[4,384]{1,0:T(4,128)S(1)}, f32[16,384]{1,0:T(8,128)S(1)}, f32[16,384]{1,0:T(8,128)S(1)}) custom-call(bf16[256,1152]{1,0:T(8,128)(2,1)S(1)} %get-tuple-element.22.refs_0_, bf16[128,1152]{1,0:T(8,128)(2,1)S(1)} %collective-permute-done.6.refs_1_, f32[4,256]{1,0:T(4,128)S(1)} %get-tuple-element.10.refs_2_, ...), custom_call_target="tpu_custom_call" | custom-call | flops 167772160 | bytes 1048576 | tf_op jit(solution)/shard_map/pallas_call | solution.py:292
  20.2 0.3 %collective-permute-done.7.refs_1_ = bf16[128,1152]{1,0:T(8,128)(2,1)S(1)} collective-permute-done((bf16[128,1152]{1,0:T(8,128)(2,1)S(1)}, bf16[128,1152]{1,0:T(8,128)(2,1)S(1)}, u32[]{:S(2)}, u32[]{:S(2)}) %collective-permute-start.7) | collective-permute-done | bytes 294944 | tf_op jit(solution)/shard_map/ppermute | solution.py:26
  20.4 1.6 %shard_map.44 = (f32[1,1]{1,0:T(1,128)}, bf16[16,1024]{1,0:T(8,128)(2,1)}) custom-call(bf16[384,1152]{1,0:T(8,128)(2,1)S(1)} %constant_dynamic-update-slice_fusion.refs_0_, bf16[128,1152]{1,0:T(8,128)(2,1)S(1)} %collective-permute-done.7.refs_1_, f32[4,384]{1,0:T(4,128)S(1)} %get-tuple-element.13.refs_2_, f32[16,384]{1,0:T(8,128)S(1)} %get-tuple-element.14.refs_3_, ...), custom_call_target="tpu_custom_call" | custom-call | flops 234881024 | bytes 1048576 | tf_op jit(solution)/shard_map/pallas_call | solution.py:301
  (12 shorter events, 0.2 us)
Async XLA Ops:
  1.4 5.4 %collective-permute-start = (bf16[16,1152]{1,0:T(8,128)(2,1)S(1)}, bf16[16,1152]{1,0:T(8,128)(2,1)S(1)}, u32[]{:S(2)}, u32[]{:S(2)}) collective-permute-start(bf16[16,1152]{1,0:T(8,128)(2,1)S(1)} %shard_map.41), channel_id=1, source_target_pairs={{0,17},{1,16},{2,19},{3,18},{4,21},{5,20},{6,23},{7,22},{8,25},{9,... | collective-permute-start | bytes 110600 | tf_op jit(solution)/shard_map/ppermute | solution.py:26
  6.9 4.3 %collective-permute-start.1 = (bf16[32,1152]{1,0:T(8,128)(2,1)S(1)}, bf16[32,1152]{1,0:T(8,128)(2,1)S(1)}, u32[]{:S(2)}, u32[]{:S(2)}) collective-permute-start(bf16[32,1152]{1,0:T(8,128)(2,1)S(1)} %pad_maximum_fusion.3), channel_id=1, source_target_pairs={{0,9},{1,8},{2,11},{3,10},{4,13},{5,12},{6,15},{7,14},{8,1},{9,0},... | collective-permute-start | bytes 221192 | tf_op jit(solution)/shard_map/ppermute | solution.py:26
  8.7 5.8 %collective-permute-start.4 = (bf16[32,1152]{1,0:T(8,128)(2,1)S(1)}, bf16[32,1152]{1,0:T(8,128)(2,1)S(1)}, u32[]{:S(2)}, u32[]{:S(2)}) collective-permute-start(bf16[32,1152]{1,0:T(8,128)(2,1)S(1)} %pad_maximum_fusion.3), channel_id=1, source_target_pairs={{0,6},{1,7},{2,4},{3,5},{4,2},{5,3},{6,0},{7,1},{8,14},{9,15},{10,... | collective-permute-start | bytes 221192 | tf_op jit(solution)/shard_map/ppermute | solution.py:26
  11.2 5.1 %collective-permute-start.2 = (bf16[64,1152]{1,0:T(8,128)(2,1)S(1)}, bf16[64,1152]{1,0:T(8,128)(2,1)S(1)}, u32[]{:S(2)}, u32[]{:S(2)}) collective-permute-start(bf16[64,1152]{1,0:T(8,128)(2,1)S(1)} %pad_maximum_fusion.2), channel_id=1, source_target_pairs={{0,3},{1,4},{2,7},{3,0},{4,1},{5,6},{6,5},{7,2},{8,11},{9,12},{10,... | collective-permute-start | bytes 442376 | tf_op jit(solution)/shard_map/ppermute | solution.py:37
  13.0 5.8 %collective-permute-start.3 = (bf16[64,1152]{1,0:T(8,128)(2,1)S(1)}, bf16[64,1152]{1,0:T(8,128)(2,1)S(1)}, u32[]{:S(2)}, u32[]{:S(2)}) collective-permute-start(bf16[64,1152]{1,0:T(8,128)(2,1)S(1)} %pad_maximum_fusion.2), channel_id=1, source_target_pairs={{0,5},{1,2},{2,1},{3,6},{4,7},{5,0},{6,3},{7,4},{8,13},{9,10},{10,... | collective-permute-start | bytes 442376 | tf_op jit(solution)/shard_map/ppermute | solution.py:37
  14.5 4.3 %collective-permute-start.5 = (bf16[32,1152]{1,0:T(8,128)(2,1)S(1)}, bf16[32,1152]{1,0:T(8,128)(2,1)S(1)}, u32[]{:S(2)}, u32[]{:S(2)}) collective-permute-start(bf16[32,1152]{1,0:T(8,128)(2,1)S(1)} %collective-permute-done.4), channel_id=1, source_target_pairs={{0,9},{1,8},{2,11},{3,10},{4,13},{5,12},{6,15},{7,14},{8,1},{9,0},... | collective-permute-start | bytes 221192 | tf_op jit(solution)/shard_map/ppermute | solution.py:26
  16.3 3.3 %collective-permute-start.6 = (bf16[128,1152]{1,0:T(8,128)(2,1)S(1)}, bf16[128,1152]{1,0:T(8,128)(2,1)S(1)}, u32[]{:S(2)}, u32[]{:S(2)}) collective-permute-start(bf16[128,1152]{1,0:T(8,128)(2,1)S(1)} %pad_maximum_fusion), channel_id=1, source_target_pairs={{0,1},{1,0},{2,3},{3,2},{4,5},{5,4},{6,7},{7,6},{8,9},{9,8},{10,11... | collective-permute-start | bytes 884744 | tf_op jit(solution)/shard_map/ppermute | solution.py:26
  18.8 1.6 %collective-permute-start.7 = (bf16[128,1152]{1,0:T(8,128)(2,1)S(1)}, bf16[128,1152]{1,0:T(8,128)(2,1)S(1)}, u32[]{:S(2)}, u32[]{:S(2)}) collective-permute-start(bf16[128,1152]{1,0:T(8,128)(2,1)S(1)} %pad_maximum_fusion.1), channel_id=1, source_target_pairs={{0,1},{1,0},{2,3},{3,2},{4,5},{5,4},{6,7},{7,6},{8,9},{9,8},{10,11... | collective-permute-start | bytes 884744 | tf_op jit(solution)/shard_map/ppermute | solution.py:26

commit v8 on v7

--- a/solution.py
+++ b/solution.py
@@ -86,7 +86,7 @@
     return rows if rows <= 384 else 256
 
 
-def block_stats(width, rows_ref, cols_ref, start, own, keep, products=None, weigh=1):
+def block_stats(width, rows_ref, cols_ref, start, own, keep, products=None):
     across, down = span(cols_ref.shape[0]), span(rows_ref.shape[0])
     if products is not None:
         down, across = products[0].shape
@@ -110,9 +110,7 @@
             keep(masked[:own], positive[:own])
         top = jnp.max(masked, axis=0, keepdims=True)
         add = jnp.sum(power(masked - top, width), axis=0, keepdims=True)
-        possum = jnp.zeros_like(top)
-        if weigh:
-            possum = weigh * jnp.sum(jnp.where(positive, s, 0.0), axis=0, keepdims=True)
+        possum = jnp.sum(jnp.where(positive, s, 0.0), axis=0, keepdims=True)
         count = jnp.sum(jnp.where(positive, 1.0, 0.0), axis=0, keepdims=True)
         parts.append((top, add, possum, count))
     return merge(parts, width)
@@ -170,13 +168,13 @@
     def early_columns(start, carry, products=None):
         at = pl.ds(start, span(early) if products is None else products[0].shape[1])
         first = tuple(had_stats[k : k + 1, at] for k in range(4))
-        more = block_stats(width, late_ref, early_ref, start, own, lambda *_: None, products, 0)
+        more = block_stats(width, late_ref, early_ref, start, own, lambda *_: None, products)
         return emit(at, merge([first, more], width), carry)
 
     def late_columns(start, carry):
         at = pl.ds(early + start, span(late))
         keep = keep_in(scores_ref, positive_ref, at)
-        first = block_stats(width, early_ref, late_ref, start, own, keep, products, 2)
+        first = block_stats(width, early_ref, late_ref, start, own, keep, products)
         second = block_stats(width, late_ref, late_ref, start, own, lambda *_: None)
         return emit(at, merge([first, second], width), carry)
 

time: 22.2 us -> 22.2 us (level)
  no operation moved by 1% of the time
where the time goes in v8:
time: 22.2 us; the launch traced here: 22 us
  starting transfers between devices  13.4 us (60%)
  waiting for transfers between devices  4.32 us (19%)
  Pallas kernels  3.36 us (15%)
  between operations  0.7 us (3%)
    ppermute x6, starting transfers between devices, swap(): return lax.ppermute(held, AXES, [(i, i ^ mask) for i in range(devices)])  10.1 us
    ppermute x6, waiting for transfers between devices, swap(): return lax.ppermute(held, AXES, [(i, i ^ mask) for i in range(devices)])  3.87 us
    ppermute x2, starting transfers between devices, rotate(): return lax.ppermute(held, AXES, turned)  3.3 us
    pallas_call x1, Pallas kernels, on_device(): pl.pallas_call(lambda *refs: loss_and_grad(width, rows, *refs), out_shape...  1.56 us
    pallas_call x1, Pallas kernels, on_device(): pl.pallas_call(pack, out_shape=pltpu.VMEM((rows, width + LANES), jnp.bflo...  0.79 us
    pallas_call x1, Pallas kernels, on_device(): pl.pallas_call(lambda *refs: more_stats(width, rows, *refs), out_shape=st...  0.55 us
    pallas_call x1, Pallas kernels, on_device(): pl.pallas_call(lambda *refs: near_stats(width, rows, *refs), out_shape=st...  0.46 us
    ppermute x2, waiting for transfers between devices, rotate(): return lax.ppermute(held, AXES, turned)  0.46 us
  transfers between devices with their start and end apart: 8, of which 4 were waited for; matrix products, arithmetic and copies ran while one was open for 1% of the time, Pallas kernels for 5%

profile of v8, /device:TPU:0, one launch (start us, length us, event | category | flops | bytes accessed | tf_op | source)
XLA Modules:
  0.0 22.0 jit_solution(16549803826040114064)
XLA Ops:
  0.6 0.8 %shard_map.41 = bf16[16,1152]{1,0:T(8,128)(2,1)S(1)} custom-call(bf16[16,1024]{1,0:T(8,128)(2,1)} %rows_hbm.1, s32[1,16]{1,0:T(1,128)} %bitcast.2), custom_call_target="tpu_custom_call" | custom-call | tf_op jit(solution)/shard_map/pallas_call | solution.py:259
  1.4 3.6 %collective-permute-start = (bf16[16,1152]{1,0:T(8,128)(2,1)S(1)}, bf16[16,1152]{1,0:T(8,128)(2,1)S(1)}, u32[]{:S(2)}, u32[]{:S(2)}) collective-permute-start(bf16[16,1152]{1,0:T(8,128)(2,1)S(1)} %shard_map.41), channel_id=1, source_target_pairs={{0,17},{1,16},{2,19},{3,18},{4,21},{5,20},{6,23},{7,22},{8,25},{9,... | collective-permute-start | bytes 110600 | tf_op jit(solution)/shard_map/ppermute | solution.py:26
  5.0 1.9 %collective-permute-done = bf16[16,1152]{1,0:T(8,128)(2,1)S(1)} collective-permute-done((bf16[16,1152]{1,0:T(8,128)(2,1)S(1)}, bf16[16,1152]{1,0:T(8,128)(2,1)S(1)}, u32[]{:S(2)}, u32[]{:S(2)}) %collective-permute-start) | collective-permute-done | bytes 36896 | tf_op jit(solution)/shard_map/ppermute | solution.py:26
  6.9 1.8 %collective-permute-start.1 = (bf16[32,1152]{1,0:T(8,128)(2,1)S(1)}, bf16[32,1152]{1,0:T(8,128)(2,1)S(1)}, u32[]{:S(2)}, u32[]{:S(2)}) collective-permute-start(bf16[32,1152]{1,0:T(8,128)(2,1)S(1)} %pad_maximum_fusion.3), channel_id=1, source_target_pairs={{0,9},{1,8},{2,11},{3,10},{4,13},{5,12},{6,15},{7,14},{8,1},{9,0},... | collective-permute-start | bytes 221192 | tf_op jit(solution)/shard_map/ppermute | solution.py:26
  8.7 2.4 %collective-permute-start.4 = (bf16[32,1152]{1,0:T(8,128)(2,1)S(1)}, bf16[32,1152]{1,0:T(8,128)(2,1)S(1)}, u32[]{:S(2)}, u32[]{:S(2)}) collective-permute-start(bf16[32,1152]{1,0:T(8,128)(2,1)S(1)} %pad_maximum_fusion.3), channel_id=1, source_target_pairs={{0,6},{1,7},{2,4},{3,5},{4,2},{5,3},{6,0},{7,1},{8,14},{9,15},{10,... | collective-permute-start | bytes 221192 | tf_op jit(solution)/shard_map/ppermute | solution.py:26
  11.2 0.0 collective-permute-done.1
  11.2 1.8 %collective-permute-start.2 = (bf16[64,1152]{1,0:T(8,128)(2,1)S(1)}, bf16[64,1152]{1,0:T(8,128)(2,1)S(1)}, u32[]{:S(2)}, u32[]{:S(2)}) collective-permute-start(bf16[64,1152]{1,0:T(8,128)(2,1)S(1)} %pad_maximum_fusion.2), channel_id=1, source_target_pairs={{0,3},{1,4},{2,7},{3,0},{4,1},{5,6},{6,5},{7,2},{8,11},{9,12},{10,... | collective-permute-start | bytes 442376 | tf_op jit(solution)/shard_map/ppermute | solution.py:37
  13.0 1.5 %collective-permute-start.3 = (bf16[64,1152]{1,0:T(8,128)(2,1)S(1)}, bf16[64,1152]{1,0:T(8,128)(2,1)S(1)}, u32[]{:S(2)}, u32[]{:S(2)}) collective-permute-start(bf16[64,1152]{1,0:T(8,128)(2,1)S(1)} %pad_maximum_fusion.2), channel_id=1, source_target_pairs={{0,5},{1,2},{2,1},{3,6},{4,7},{5,0},{6,3},{7,4},{8,13},{9,10},{10,... | collective-permute-start | bytes 442376 | tf_op jit(solution)/shard_map/ppermute | solution.py:37
  14.5 0.0 collective-permute-done.4
  14.5 1.3 %collective-permute-start.5 = (bf16[32,1152]{1,0:T(8,128)(2,1)S(1)}, bf16[32,1152]{1,0:T(8,128)(2,1)S(1)}, u32[]{:S(2)}, u32[]{:S(2)}) collective-permute-start(bf16[32,1152]{1,0:T(8,128)(2,1)S(1)} %collective-permute-done.4), channel_id=1, source_target_pairs={{0,9},{1,8},{2,11},{3,10},{4,13},{5,12},{6,15},{7,14},{8,1},{9,0},... | collective-permute-start | bytes 221192 | tf_op jit(solution)/shard_map/ppermute | solution.py:26
  15.8 0.5 %collective-permute-done.2 = bf16[64,1152]{1,0:T(8,128)(2,1)S(1)} collective-permute-done((bf16[64,1152]{1,0:T(8,128)(2,1)S(1)}, bf16[64,1152]{1,0:T(8,128)(2,1)S(1)}, u32[]{:S(2)}, u32[]{:S(2)}) %collective-permute-start.2) | collective-permute-done | bytes 147488 | tf_op jit(solution)/shard_map/ppermute | solution.py:37
  16.3 0.8 %collective-permute-start.6 = (bf16[128,1152]{1,0:T(8,128)(2,1)S(1)}, bf16[128,1152]{1,0:T(8,128)(2,1)S(1)}, u32[]{:S(2)}, u32[]{:S(2)}) collective-permute-start(bf16[128,1152]{1,0:T(8,128)(2,1)S(1)} %pad_maximum_fusion), channel_id=1, source_target_pairs={{0,1},{1,0},{2,3},{3,2},{4,5},{5,4},{6,7},{7,6},{8,9},{9,8},{10,11... | collective-permute-start | bytes 884744 | tf_op jit(solution)/shard_map/ppermute | solution.py:26
  17.1 1.7 %collective-permute-done.5 = bf16[32,1152]{1,0:T(8,128)(2,1)S(1)} collective-permute-done((bf16[32,1152]{1,0:T(8,128)(2,1)S(1)}, bf16[32,1152]{1,0:T(8,128)(2,1)S(1)}, u32[]{:S(2)}, u32[]{:S(2)}) %collective-permute-start.5) | collective-permute-done | bytes 73760 | tf_op jit(solution)/shard_map/ppermute | solution.py:26
  18.8 0.0 collective-permute-done.3
  18.8 0.2 collective-permute-start.7
  19.1 0.5 %shard_map.42 = (f32[4,256]{1,0:T(4,128)S(1)}, f32[16,256]{1,0:T(8,128)S(1)}, f32[16,256]{1,0:T(8,128)S(1)}) custom-call(bf16[256,1152]{1,0:T(8,128)(2,1)S(1)} %get-tuple-element.22.refs_0_), custom_call_target="tpu_custom_call" | custom-call | flops 134217728 | bytes 1048576 | tf_op jit(solution)/shard_map/pallas_call | solution.py:281
  19.6 0.0 collective-permute-done.6.refs_1_
  19.6 0.6 %shard_map.43 = (f32[4,384]{1,0:T(4,128)S(1)}, f32[16,384]{1,0:T(8,128)S(1)}, f32[16,384]{1,0:T(8,128)S(1)}) custom-call(bf16[256,1152]{1,0:T(8,128)(2,1)S(1)} %get-tuple-element.22.refs_0_, bf16[128,1152]{1,0:T(8,128)(2,1)S(1)} %collective-permute-done.6.refs_1_, f32[4,256]{1,0:T(4,128)S(1)} %get-tuple-element.10.refs_2_, ...), custom_call_target="tpu_custom_call" | custom-call | flops 167772160 | bytes 1048576 | tf_op jit(solution)/shard_map/pallas_call | solution.py:290
  20.2 0.3 %collective-permute-done.7.refs_1_ = bf16[128,1152]{1,0:T(8,128)(2,1)S(1)} collective-permute-done((bf16[128,1152]{1,0:T(8,128)(2,1)S(1)}, bf16[128,1152]{1,0:T(8,128)(2,1)S(1)}, u32[]{:S(2)}, u32[]{:S(2)}) %collective-permute-start.7) | collective-permute-done | bytes 294944 | tf_op jit(solution)/shard_map/ppermute | solution.py:26
  20.4 1.6 %shard_map.44 = (f32[1,1]{1,0:T(1,128)}, bf16[16,1024]{1,0:T(8,128)(2,1)}) custom-call(bf16[384,1152]{1,0:T(8,128)(2,1)S(1)} %constant_dynamic-update-slice_fusion.refs_0_, bf16[128,1152]{1,0:T(8,128)(2,1)S(1)} %collective-permute-done.7.refs_1_, f32[4,384]{1,0:T(4,128)S(1)} %get-tuple-element.13.refs_2_, f32[16,384]{1,0:T(8,128)S(1)} %get-tuple-element.14.refs_3_, ...), custom_call_target="tpu_custom_call" | custom-call | flops 234881024 | bytes 1048576 | tf_op jit(solution)/shard_map/pallas_call | solution.py:299
  (12 shorter events, 0.2 us)
Async XLA Ops:
  1.4 5.4 %collective-permute-start = (bf16[16,1152]{1,0:T(8,128)(2,1)S(1)}, bf16[16,1152]{1,0:T(8,128)(2,1)S(1)}, u32[]{:S(2)}, u32[]{:S(2)}) collective-permute-start(bf16[16,1152]{1,0:T(8,128)(2,1)S(1)} %shard_map.41), channel_id=1, source_target_pairs={{0,17},{1,16},{2,19},{3,18},{4,21},{5,20},{6,23},{7,22},{8,25},{9,... | collective-permute-start | bytes 110600 | tf_op jit(solution)/shard_map/ppermute | solution.py:26
  6.9 4.3 %collective-permute-start.1 = (bf16[32,1152]{1,0:T(8,128)(2,1)S(1)}, bf16[32,1152]{1,0:T(8,128)(2,1)S(1)}, u32[]{:S(2)}, u32[]{:S(2)}) collective-permute-start(bf16[32,1152]{1,0:T(8,128)(2,1)S(1)} %pad_maximum_fusion.3), channel_id=1, source_target_pairs={{0,9},{1,8},{2,11},{3,10},{4,13},{5,12},{6,15},{7,14},{8,1},{9,0},... | collective-permute-start | bytes 221192 | tf_op jit(solution)/shard_map/ppermute | solution.py:26
  8.7 5.8 %collective-permute-start.4 = (bf16[32,1152]{1,0:T(8,128)(2,1)S(1)}, bf16[32,1152]{1,0:T(8,128)(2,1)S(1)}, u32[]{:S(2)}, u32[]{:S(2)}) collective-permute-start(bf16[32,1152]{1,0:T(8,128)(2,1)S(1)} %pad_maximum_fusion.3), channel_id=1, source_target_pairs={{0,6},{1,7},{2,4},{3,5},{4,2},{5,3},{6,0},{7,1},{8,14},{9,15},{10,... | collective-permute-start | bytes 221192 | tf_op jit(solution)/shard_map/ppermute | solution.py:26
  11.2 5.1 %collective-permute-start.2 = (bf16[64,1152]{1,0:T(8,128)(2,1)S(1)}, bf16[64,1152]{1,0:T(8,128)(2,1)S(1)}, u32[]{:S(2)}, u32[]{:S(2)}) collective-permute-start(bf16[64,1152]{1,0:T(8,128)(2,1)S(1)} %pad_maximum_fusion.2), channel_id=1, source_target_pairs={{0,3},{1,4},{2,7},{3,0},{4,1},{5,6},{6,5},{7,2},{8,11},{9,12},{10,... | collective-permute-start | bytes 442376 | tf_op jit(solution)/shard_map/ppermute | solution.py:37
  13.0 5.8 %collective-permute-start.3 = (bf16[64,1152]{1,0:T(8,128)(2,1)S(1)}, bf16[64,1152]{1,0:T(8,128)(2,1)S(1)}, u32[]{:S(2)}, u32[]{:S(2)}) collective-permute-start(bf16[64,1152]{1,0:T(8,128)(2,1)S(1)} %pad_maximum_fusion.2), channel_id=1, source_target_pairs={{0,5},{1,2},{2,1},{3,6},{4,7},{5,0},{6,3},{7,4},{8,13},{9,10},{10,... | collective-permute-start | bytes 442376 | tf_op jit(solution)/shard_map/ppermute | solution.py:37
  14.5 4.3 %collective-permute-start.5 = (bf16[32,1152]{1,0:T(8,128)(2,1)S(1)}, bf16[32,1152]{1,0:T(8,128)(2,1)S(1)}, u32[]{:S(2)}, u32[]{:S(2)}) collective-permute-start(bf16[32,1152]{1,0:T(8,128)(2,1)S(1)} %collective-permute-done.4), channel_id=1, source_target_pairs={{0,9},{1,8},{2,11},{3,10},{4,13},{5,12},{6,15},{7,14},{8,1},{9,0},... | collective-permute-start | bytes 221192 | tf_op jit(solution)/shard_map/ppermute | solution.py:26
  16.3 3.3 %collective-permute-start.6 = (bf16[128,1152]{1,0:T(8,128)(2,1)S(1)}, bf16[128,1152]{1,0:T(8,128)(2,1)S(1)}, u32[]{:S(2)}, u32[]{:S(2)}) collective-permute-start(bf16[128,1152]{1,0:T(8,128)(2,1)S(1)} %pad_maximum_fusion), channel_id=1, source_target_pairs={{0,1},{1,0},{2,3},{3,2},{4,5},{5,4},{6,7},{7,6},{8,9},{9,8},{10,11... | collective-permute-start | bytes 884744 | tf_op jit(solution)/shard_map/ppermute | solution.py:26
  18.8 1.6 %collective-permute-start.7 = (bf16[128,1152]{1,0:T(8,128)(2,1)S(1)}, bf16[128,1152]{1,0:T(8,128)(2,1)S(1)}, u32[]{:S(2)}, u32[]{:S(2)}) collective-permute-start(bf16[128,1152]{1,0:T(8,128)(2,1)S(1)} %pad_maximum_fusion.1), channel_id=1, source_target_pairs={{0,1},{1,0},{2,3},{3,2},{4,5},{5,4},{6,7},{7,6},{8,9},{9,8},{10,11... | collective-permute-start | bytes 884744 | tf_op jit(solution)/shard_map/ppermute | solution.py:26

commit v9 on v8

--- a/solution.py
+++ b/solution.py
@@ -237,7 +237,7 @@
     weight = (jnp.exp(masked - lse) - positive * inverse) / total
     mirrored = (jnp.exp(masked - lse_ref[...]) - positive * inv_ref[...]) / total
     both = jnp.concatenate([weight, mirrored], axis=0).astype(jnp.bfloat16)
-    parts = 2
+    parts = 4
     for k in range(parts):
         at = pl.ds(k * width // parts, width // parts)
         out = jnp.dot(both[:, :early], early_ref[:, at], preferred_element_type=jnp.float32)
@@ -311,7 +311,7 @@
             pltpu.VMEM((rows, total), jnp.float32),
             pltpu.VMEM((1, 1), jnp.float32),
             pltpu.VMEM((rows, width), jnp.bfloat16),
-            pltpu.SemaphoreType.DMA((3,)),
+            pltpu.SemaphoreType.DMA((5,)),
         ],
         compiler_params=params,
         cost_estimate=cost(total * total - early * early),

time: 22.2 us -> 22.2 us (level)
  no operation moved by 1% of the time
where the time goes in v9:
time: 22.2 us; the launch traced here: 22 us
  starting transfers between devices  13.4 us (60%)
  waiting for transfers between devices  4.32 us (19%)
  Pallas kernels  3.37 us (15%)
  between operations  0.7 us (3%)
    ppermute x6, starting transfers between devices, swap(): return lax.ppermute(held, AXES, [(i, i ^ mask) for i in range(devices)])  10.1 us
    ppermute x6, waiting for transfers between devices, swap(): return lax.ppermute(held, AXES, [(i, i ^ mask) for i in range(devices)])  3.87 us
    ppermute x2, starting transfers between devices, rotate(): return lax.ppermute(held, AXES, turned)  3.3 us
    pallas_call x1, Pallas kernels, on_device(): pl.pallas_call(lambda *refs: loss_and_grad(width, rows, *refs), out_shape...  1.57 us
    pallas_call x1, Pallas kernels, on_device(): pl.pallas_call(pack, out_shape=pltpu.VMEM((rows, width + LANES), jnp.bflo...  0.79 us
    pallas_call x1, Pallas kernels, on_device(): pl.pallas_call(lambda *refs: more_stats(width, rows, *refs), out_shape=st...  0.55 us
    pallas_call x1, Pallas kernels, on_device(): pl.pallas_call(lambda *refs: near_stats(width, rows, *refs), out_shape=st...  0.46 us
    ppermute x2, waiting for transfers between devices, rotate(): return lax.ppermute(held, AXES, turned)  0.46 us
  transfers between devices with their start and end apart: 8, of which 4 were waited for; matrix products, arithmetic and copies ran while one was open for 1% of the time, Pallas kernels for 5%

profile of v9, /device:TPU:0, one launch (start us, length us, event | category | flops | bytes accessed | tf_op | source)
XLA Modules:
  0.0 22.0 jit_solution(1894089333847243671)
XLA Ops:
  0.6 0.8 %shard_map.41 = bf16[16,1152]{1,0:T(8,128)(2,1)S(1)} custom-call(bf16[16,1024]{1,0:T(8,128)(2,1)} %rows_hbm.1, s32[1,16]{1,0:T(1,128)} %bitcast.2), custom_call_target="tpu_custom_call" | custom-call | tf_op jit(solution)/shard_map/pallas_call | solution.py:259
  1.4 3.6 %collective-permute-start = (bf16[16,1152]{1,0:T(8,128)(2,1)S(1)}, bf16[16,1152]{1,0:T(8,128)(2,1)S(1)}, u32[]{:S(2)}, u32[]{:S(2)}) collective-permute-start(bf16[16,1152]{1,0:T(8,128)(2,1)S(1)} %shard_map.41), channel_id=1, source_target_pairs={{0,17},{1,16},{2,19},{3,18},{4,21},{5,20},{6,23},{7,22},{8,25},{9,... | collective-permute-start | bytes 110600 | tf_op jit(solution)/shard_map/ppermute | solution.py:26
  5.0 1.9 %collective-permute-done = bf16[16,1152]{1,0:T(8,128)(2,1)S(1)} collective-permute-done((bf16[16,1152]{1,0:T(8,128)(2,1)S(1)}, bf16[16,1152]{1,0:T(8,128)(2,1)S(1)}, u32[]{:S(2)}, u32[]{:S(2)}) %collective-permute-start) | collective-permute-done | bytes 36896 | tf_op jit(solution)/shard_map/ppermute | solution.py:26
  6.9 1.8 %collective-permute-start.1 = (bf16[32,1152]{1,0:T(8,128)(2,1)S(1)}, bf16[32,1152]{1,0:T(8,128)(2,1)S(1)}, u32[]{:S(2)}, u32[]{:S(2)}) collective-permute-start(bf16[32,1152]{1,0:T(8,128)(2,1)S(1)} %pad_maximum_fusion.3), channel_id=1, source_target_pairs={{0,9},{1,8},{2,11},{3,10},{4,13},{5,12},{6,15},{7,14},{8,1},{9,0},... | collective-permute-start | bytes 221192 | tf_op jit(solution)/shard_map/ppermute | solution.py:26
  8.7 2.4 %collective-permute-start.4 = (bf16[32,1152]{1,0:T(8,128)(2,1)S(1)}, bf16[32,1152]{1,0:T(8,128)(2,1)S(1)}, u32[]{:S(2)}, u32[]{:S(2)}) collective-permute-start(bf16[32,1152]{1,0:T(8,128)(2,1)S(1)} %pad_maximum_fusion.3), channel_id=1, source_target_pairs={{0,6},{1,7},{2,4},{3,5},{4,2},{5,3},{6,0},{7,1},{8,14},{9,15},{10,... | collective-permute-start | bytes 221192 | tf_op jit(solution)/shard_map/ppermute | solution.py:26
  11.2 0.0 collective-permute-done.1
  11.2 1.8 %collective-permute-start.2 = (bf16[64,1152]{1,0:T(8,128)(2,1)S(1)}, bf16[64,1152]{1,0:T(8,128)(2,1)S(1)}, u32[]{:S(2)}, u32[]{:S(2)}) collective-permute-start(bf16[64,1152]{1,0:T(8,128)(2,1)S(1)} %pad_maximum_fusion.2), channel_id=1, source_target_pairs={{0,3},{1,4},{2,7},{3,0},{4,1},{5,6},{6,5},{7,2},{8,11},{9,12},{10,... | collective-permute-start | bytes 442376 | tf_op jit(solution)/shard_map/ppermute | solution.py:37
  13.0 1.5 %collective-permute-start.3 = (bf16[64,1152]{1,0:T(8,128)(2,1)S(1)}, bf16[64,1152]{1,0:T(8,128)(2,1)S(1)}, u32[]{:S(2)}, u32[]{:S(2)}) collective-permute-start(bf16[64,1152]{1,0:T(8,128)(2,1)S(1)} %pad_maximum_fusion.2), channel_id=1, source_target_pairs={{0,5},{1,2},{2,1},{3,6},{4,7},{5,0},{6,3},{7,4},{8,13},{9,10},{10,... | collective-permute-start | bytes 442376 | tf_op jit(solution)/shard_map/ppermute | solution.py:37
  14.5 0.0 collective-permute-done.4
  14.5 1.3 %collective-permute-start.5 = (bf16[32,1152]{1,0:T(8,128)(2,1)S(1)}, bf16[32,1152]{1,0:T(8,128)(2,1)S(1)}, u32[]{:S(2)}, u32[]{:S(2)}) collective-permute-start(bf16[32,1152]{1,0:T(8,128)(2,1)S(1)} %collective-permute-done.4), channel_id=1, source_target_pairs={{0,9},{1,8},{2,11},{3,10},{4,13},{5,12},{6,15},{7,14},{8,1},{9,0},... | collective-permute-start | bytes 221192 | tf_op jit(solution)/shard_map/ppermute | solution.py:26
  15.8 0.5 %collective-permute-done.2 = bf16[64,1152]{1,0:T(8,128)(2,1)S(1)} collective-permute-done((bf16[64,1152]{1,0:T(8,128)(2,1)S(1)}, bf16[64,1152]{1,0:T(8,128)(2,1)S(1)}, u32[]{:S(2)}, u32[]{:S(2)}) %collective-permute-start.2) | collective-permute-done | bytes 147488 | tf_op jit(solution)/shard_map/ppermute | solution.py:37
  16.3 0.8 %collective-permute-start.6 = (bf16[128,1152]{1,0:T(8,128)(2,1)S(1)}, bf16[128,1152]{1,0:T(8,128)(2,1)S(1)}, u32[]{:S(2)}, u32[]{:S(2)}) collective-permute-start(bf16[128,1152]{1,0:T(8,128)(2,1)S(1)} %pad_maximum_fusion), channel_id=1, source_target_pairs={{0,1},{1,0},{2,3},{3,2},{4,5},{5,4},{6,7},{7,6},{8,9},{9,8},{10,11... | collective-permute-start | bytes 884744 | tf_op jit(solution)/shard_map/ppermute | solution.py:26
  17.1 1.7 %collective-permute-done.5 = bf16[32,1152]{1,0:T(8,128)(2,1)S(1)} collective-permute-done((bf16[32,1152]{1,0:T(8,128)(2,1)S(1)}, bf16[32,1152]{1,0:T(8,128)(2,1)S(1)}, u32[]{:S(2)}, u32[]{:S(2)}) %collective-permute-start.5) | collective-permute-done | bytes 73760 | tf_op jit(solution)/shard_map/ppermute | solution.py:26
  18.8 0.0 collective-permute-done.3
  18.8 0.2 collective-permute-start.7
  19.1 0.5 %shard_map.42 = (f32[4,256]{1,0:T(4,128)S(1)}, f32[16,256]{1,0:T(8,128)S(1)}, f32[16,256]{1,0:T(8,128)S(1)}) custom-call(bf16[256,1152]{1,0:T(8,128)(2,1)S(1)} %get-tuple-element.22.refs_0_), custom_call_target="tpu_custom_call" | custom-call | flops 134217728 | bytes 1048576 | tf_op jit(solution)/shard_map/pallas_call | solution.py:281
  19.6 0.0 collective-permute-done.6.refs_1_
  19.6 0.6 %shard_map.43 = (f32[4,384]{1,0:T(4,128)S(1)}, f32[16,384]{1,0:T(8,128)S(1)}, f32[16,384]{1,0:T(8,128)S(1)}) custom-call(bf16[256,1152]{1,0:T(8,128)(2,1)S(1)} %get-tuple-element.22.refs_0_, bf16[128,1152]{1,0:T(8,128)(2,1)S(1)} %collective-permute-done.6.refs_1_, f32[4,256]{1,0:T(4,128)S(1)} %get-tuple-element.10.refs_2_, ...), custom_call_target="tpu_custom_call" | custom-call | flops 167772160 | bytes 1048576 | tf_op jit(solution)/shard_map/pallas_call | solution.py:290
  20.2 0.3 %collective-permute-done.7.refs_1_ = bf16[128,1152]{1,0:T(8,128)(2,1)S(1)} collective-permute-done((bf16[128,1152]{1,0:T(8,128)(2,1)S(1)}, bf16[128,1152]{1,0:T(8,128)(2,1)S(1)}, u32[]{:S(2)}, u32[]{:S(2)}) %collective-permute-start.7) | collective-permute-done | bytes 294944 | tf_op jit(solution)/shard_map/ppermute | solution.py:26
  20.4 1.6 %shard_map.44 = (f32[1,1]{1,0:T(1,128)}, bf16[16,1024]{1,0:T(8,128)(2,1)}) custom-call(bf16[384,1152]{1,0:T(8,128)(2,1)S(1)} %constant_dynamic-update-slice_fusion.refs_0_, bf16[128,1152]{1,0:T(8,128)(2,1)S(1)} %collective-permute-done.7.refs_1_, f32[4,384]{1,0:T(4,128)S(1)} %get-tuple-element.13.refs_2_, f32[16,384]{1,0:T(8,128)S(1)} %get-tuple-element.14.refs_3_, ...), custom_call_target="tpu_custom_call" | custom-call | flops 234881024 | bytes 1048576 | tf_op jit(solution)/shard_map/pallas_call | solution.py:299
  (12 shorter events, 0.2 us)
Async XLA Ops:
  1.4 5.4 %collective-permute-start = (bf16[16,1152]{1,0:T(8,128)(2,1)S(1)}, bf16[16,1152]{1,0:T(8,128)(2,1)S(1)}, u32[]{:S(2)}, u32[]{:S(2)}) collective-permute-start(bf16[16,1152]{1,0:T(8,128)(2,1)S(1)} %shard_map.41), channel_id=1, source_target_pairs={{0,17},{1,16},{2,19},{3,18},{4,21},{5,20},{6,23},{7,22},{8,25},{9,... | collective-permute-start | bytes 110600 | tf_op jit(solution)/shard_map/ppermute | solution.py:26
  6.9 4.3 %collective-permute-start.1 = (bf16[32,1152]{1,0:T(8,128)(2,1)S(1)}, bf16[32,1152]{1,0:T(8,128)(2,1)S(1)}, u32[]{:S(2)}, u32[]{:S(2)}) collective-permute-start(bf16[32,1152]{1,0:T(8,128)(2,1)S(1)} %pad_maximum_fusion.3), channel_id=1, source_target_pairs={{0,9},{1,8},{2,11},{3,10},{4,13},{5,12},{6,15},{7,14},{8,1},{9,0},... | collective-permute-start | bytes 221192 | tf_op jit(solution)/shard_map/ppermute | solution.py:26
  8.7 5.8 %collective-permute-start.4 = (bf16[32,1152]{1,0:T(8,128)(2,1)S(1)}, bf16[32,1152]{1,0:T(8,128)(2,1)S(1)}, u32[]{:S(2)}, u32[]{:S(2)}) collective-permute-start(bf16[32,1152]{1,0:T(8,128)(2,1)S(1)} %pad_maximum_fusion.3), channel_id=1, source_target_pairs={{0,6},{1,7},{2,4},{3,5},{4,2},{5,3},{6,0},{7,1},{8,14},{9,15},{10,... | collective-permute-start | bytes 221192 | tf_op jit(solution)/shard_map/ppermute | solution.py:26
  11.2 5.1 %collective-permute-start.2 = (bf16[64,1152]{1,0:T(8,128)(2,1)S(1)}, bf16[64,1152]{1,0:T(8,128)(2,1)S(1)}, u32[]{:S(2)}, u32[]{:S(2)}) collective-permute-start(bf16[64,1152]{1,0:T(8,128)(2,1)S(1)} %pad_maximum_fusion.2), channel_id=1, source_target_pairs={{0,3},{1,4},{2,7},{3,0},{4,1},{5,6},{6,5},{7,2},{8,11},{9,12},{10,... | collective-permute-start | bytes 442376 | tf_op jit(solution)/shard_map/ppermute | solution.py:37
  13.0 5.8 %collective-permute-start.3 = (bf16[64,1152]{1,0:T(8,128)(2,1)S(1)}, bf16[64,1152]{1,0:T(8,128)(2,1)S(1)}, u32[]{:S(2)}, u32[]{:S(2)}) collective-permute-start(bf16[64,1152]{1,0:T(8,128)(2,1)S(1)} %pad_maximum_fusion.2), channel_id=1, source_target_pairs={{0,5},{1,2},{2,1},{3,6},{4,7},{5,0},{6,3},{7,4},{8,13},{9,10},{10,... | collective-permute-start | bytes 442376 | tf_op jit(solution)/shard_map/ppermute | solution.py:37
  14.5 4.3 %collective-permute-start.5 = (bf16[32,1152]{1,0:T(8,128)(2,1)S(1)}, bf16[32,1152]{1,0:T(8,128)(2,1)S(1)}, u32[]{:S(2)}, u32[]{:S(2)}) collective-permute-start(bf16[32,1152]{1,0:T(8,128)(2,1)S(1)} %collective-permute-done.4), channel_id=1, source_target_pairs={{0,9},{1,8},{2,11},{3,10},{4,13},{5,12},{6,15},{7,14},{8,1},{9,0},... | collective-permute-start | bytes 221192 | tf_op jit(solution)/shard_map/ppermute | solution.py:26
  16.3 3.3 %collective-permute-start.6 = (bf16[128,1152]{1,0:T(8,128)(2,1)S(1)}, bf16[128,1152]{1,0:T(8,128)(2,1)S(1)}, u32[]{:S(2)}, u32[]{:S(2)}) collective-permute-start(bf16[128,1152]{1,0:T(8,128)(2,1)S(1)} %pad_maximum_fusion), channel_id=1, source_target_pairs={{0,1},{1,0},{2,3},{3,2},{4,5},{5,4},{6,7},{7,6},{8,9},{9,8},{10,11... | collective-permute-start | bytes 884744 | tf_op jit(solution)/shard_map/ppermute | solution.py:26
  18.8 1.6 %collective-permute-start.7 = (bf16[128,1152]{1,0:T(8,128)(2,1)S(1)}, bf16[128,1152]{1,0:T(8,128)(2,1)S(1)}, u32[]{:S(2)}, u32[]{:S(2)}) collective-permute-start(bf16[128,1152]{1,0:T(8,128)(2,1)S(1)} %pad_maximum_fusion.1), channel_id=1, source_target_pairs={{0,1},{1,0},{2,3},{3,2},{4,5},{5,4},{6,7},{7,6},{8,9},{9,8},{10,11... | collective-permute-start | bytes 884744 | tf_op jit(solution)/shard_map/ppermute | solution.py:26
